TPU v7x, 32 devices: a whole 2x2x4 slice. The times are simulated.
32 devices in a mesh: wide: 16 (over z, x, core), narrow: 2 (over y).
Axes of the slice: x: 2, y: 2, z: 4, core: 2. Of those that a mesh axis runs over, the one named last changes fastest.
Arguments:
- tokens: bfloat16 [16384, 768], P(('wide', 'narrow')), may hold values from -6 to 6
- token_marks: int32 [16384], P(('wide', 'narrow')), may hold values 0 or 1
- crop_lengths: int32 [256], P('wide'), may hold values from 0 to 576, as said below
- bucket_ids: int32 [256], P('wide'), may hold values from 0 to 3
- mask_token: bfloat16 [768], replicated, may hold values from -5 to 5
- norm1_gain: bfloat16 [768], replicated, may hold values from 0.099609375 to 1.8984375
- norm1_bias: bfloat16 [768], replicated, may hold values from -3 to 3
- w_qkv: bfloat16 [3, 768, 768], P(None, None, 'narrow'), may hold values from -0.21875 to 0.21875
- qv_bias: bfloat16 [2, 768], P(None, 'narrow'), may hold values from -3 to 3
- w_proj: bfloat16 [768, 768], P('narrow'), may hold values from -1.75 to 1.75
- proj_bias: bfloat16 [768], replicated, may hold values from -3 to 3
- scale_attn: bfloat16 [768], replicated, may hold values from 0.5 to 1.5
- norm2_gain: bfloat16 [768], replicated, may hold values from 0.099609375 to 1.8984375
- norm2_bias: bfloat16 [768], replicated, may hold values from -3 to 3
- w_fc1: bfloat16 [768, 3072], P(None, 'narrow'), may hold values from -0.21875 to 0.21875
- fc1_bias: bfloat16 [3072], P('narrow'), may hold values from -3 to 3
- w_fc2: bfloat16 [3072, 768], P('narrow'), may hold values from -0.109375 to 0.109375
- fc2_bias: bfloat16 [768], replicated, may hold values from -3 to 3
- scale_mlp: bfloat16 [768], replicated, may hold values from 0.5 to 1.5
- cotangent: bfloat16 [16384, 768], P(('wide', 'narrow')), may hold values from -6 to 6
Outputs:
- output: bfloat16 [16384, 768], P(('wide', 'narrow'))
- grad_tokens: float32 [16384, 768], P(('wide', 'narrow'))
- grad_mask_token: float32 [768], replicated
- grad_norm1_gain: float32 [768], replicated
- grad_norm1_bias: float32 [768], replicated
- grad_qkv: float32 [3, 768, 768], P(None, None, 'narrow')
- grad_qv_bias: float32 [2, 768], P(None, 'narrow')
- grad_proj: float32 [768, 768], P('narrow')
- grad_proj_bias: float32 [768], replicated
- grad_scale_attn: float32 [768], replicated
- grad_norm2_gain: float32 [768], replicated
- grad_norm2_bias: float32 [768], replicated
- grad_fc1: float32 [768, 3072], P(None, 'narrow')
- grad_fc1_bias: float32 [3072], P('narrow')
- grad_fc2: float32 [3072, 768], P('narrow')
- grad_fc2_bias: float32 [768], replicated
- grad_scale_mlp: float32 [768], replicated
Inputs may be any that keep to these rules, and one draw needn't show every extreme that they name: `crop_lengths`: length 0 marks an empty slot. The nonempty slots of a buffer come first, and their padded rows together fill at most 1024; some buffer is filled to exactly 1024 rows. A nonempty crop has more than 48 rows, and its bucket is the smallest of 64, 144, 256, 576 that holds it.
All inputs are finite; a program needn't handle non-finite values. No bound on the sum of `token_marks` on one device may be relied on, other than what follows from the above.
Results may differ from a plain program's by a relative error of at most 0.017.
Values may be sent and summed in bfloat16 or wider, within the bound.
No kernel may reach another device: no remote copies, remote signals or barrier semaphores. Data moves between devices by JAX's collectives and lax.ppermute only.
A program may use at most 128 MiB of HBM per device.

v0:
```python
from functools import partial

import jax
import jax.numpy as jnp
from jax import lax
from jax.sharding import PartitionSpec as P

HEAD_DIM = 64
B0 = 64
B1 = 144
B2 = 256
B3 = 576


epsilon = 1e-06
score_scale = 0.125
masked_score = -1e30


def layer_norm(values_in, norm_gain, norm_shift):
    row_mean = jnp.mean(values_in, axis=-1, keepdims=True)
    centered = values_in - row_mean
    variance = jnp.mean(centered * centered, axis=-1, keepdims=True)
    return centered * lax.rsqrt(variance + epsilon) * norm_gain + norm_shift


def row_layout(lengths, buckets, row_total):
    slot_count = lengths.shape[0]
    bucket_rows = jnp.where(
        buckets == 0, B0, jnp.where(buckets == 1, B1, jnp.where(buckets == 2, B2, B3))
    )
    padded_sizes = jnp.where(lengths > 0, bucket_rows, 0).astype(jnp.int32)
    slot_ends = jnp.cumsum(padded_sizes)
    starts = slot_ends - padded_sizes
    row_ids = jnp.arange(row_total, dtype=jnp.int32)
    crop_of_row = jnp.sum((row_ids[:, None] >= slot_ends[None, :]).astype(jnp.int32), axis=1)
    slot_match = crop_of_row[:, None] == jnp.arange(slot_count, dtype=jnp.int32)[None, :]
    row_start = jnp.sum(jnp.where(slot_match, starts[None, :], 0), axis=1)
    row_length = jnp.sum(jnp.where(slot_match, lengths[None, :], 0), axis=1)
    is_valid = (crop_of_row < slot_count) & (row_ids - row_start < row_length)
    return (crop_of_row, is_valid)


def allowed_block(crop_of_row, is_valid, first_row, block_rows):
    row_total = crop_of_row.shape[0]
    query_crop = lax.dynamic_slice_in_dim(crop_of_row, first_row, block_rows)
    query_valid = lax.dynamic_slice_in_dim(is_valid, first_row, block_rows)
    query_ids = first_row + jnp.arange(block_rows, dtype=jnp.int32)
    key_ids = jnp.arange(row_total, dtype=jnp.int32)
    same_crop = (
        (query_crop[:, None] == crop_of_row[None, :]) & query_valid[:, None] & is_valid[None, :]
    )
    itself = (query_ids[:, None] == key_ids[None, :]) & jnp.logical_not(query_valid)[:, None]
    return same_crop | itself


def block_rows_for():
    return 512


def slab(matrix, first_row, row_count):
    return lax.dynamic_slice_in_dim(matrix, first_row, row_count, 0)


def shards(
    tokens,
    token_marks,
    crop_lengths,
    bucket_ids,
    mask_token,
    norm1_gain,
    norm1_bias,
    w_qkv,
    qv_bias,
    w_proj,
    proj_bias,
    scale_attn,
    norm2_gain,
    norm2_bias,
    w_fc1,
    fc1_bias,
    w_fc2,
    fc2_bias,
    scale_mlp,
    cotangent,
):
    own_rows = tokens.shape[0]
    row_total = own_rows * lax.axis_size("narrow")
    first_own = lax.axis_index("narrow") * own_rows
    crop_of_row, is_valid = row_layout(crop_lengths, bucket_ids, row_total)
    own_valid = lax.dynamic_slice_in_dim(is_valid, first_own, own_rows)[:, None]
    marked = (token_marks == 1)[:, None]
    gain1 = norm1_gain.astype(jnp.float32)
    shift1 = norm1_bias.astype(jnp.float32)
    gain2 = norm2_gain.astype(jnp.float32)
    shift2 = norm2_bias.astype(jnp.float32)
    scale1 = scale_attn.astype(jnp.float32)
    scale2 = scale_mlp.astype(jnp.float32)
    x_in = jnp.where(marked, mask_token.astype(jnp.float32)[None, :], tokens.astype(jnp.float32))
    normed1 = layer_norm(x_in, gain1, shift1).astype(jnp.bfloat16)
    normed1_all = lax.all_gather(normed1, "narrow", axis=0, tiled=True)
    projected = jnp.einsum("rd,cde->cre", normed1_all, w_qkv, preferred_element_type=jnp.float32)
    bias_pair = qv_bias.astype(jnp.float32)
    queries = (projected[0] + bias_pair[0]).astype(jnp.bfloat16)
    keys_all = projected[1].astype(jnp.bfloat16)
    values_all = (projected[2] + bias_pair[1]).astype(jnp.bfloat16)
    heads_local = queries.shape[1] // HEAD_DIM
    query_heads = queries.reshape(row_total, heads_local, HEAD_DIM)
    key_heads = keys_all.reshape(row_total, heads_local, HEAD_DIM)
    value_heads = values_all.reshape(row_total, heads_local, HEAD_DIM)
    block_rows = block_rows_for()
    block_count = row_total // block_rows
    block_ids = jnp.arange(block_count, dtype=jnp.int32)

    def attend(block_index):
        first_row = block_index * block_rows
        query_block = slab(query_heads, first_row, block_rows)
        scores = (
            jnp.einsum("qhd,khd->hqk", query_block, key_heads, preferred_element_type=jnp.float32)
            * score_scale
        )
        allowed = allowed_block(crop_of_row, is_valid, first_row, block_rows)
        scores = jnp.where(allowed[None], scores, masked_score)
        row_peak = jnp.max(scores, axis=-1, keepdims=True)
        exponent = jnp.exp(scores - row_peak)
        denominator = jnp.sum(exponent, axis=-1, keepdims=True)
        probability = (exponent / denominator).astype(jnp.bfloat16)
        mixed = jnp.einsum(
            "hqk,khd->qhd", probability, value_heads, preferred_element_type=jnp.float32
        ).astype(jnp.bfloat16)
        return (mixed, (row_peak + jnp.log(denominator))[..., 0])

    mixed_blocks, log_totals = lax.map(attend, block_ids)
    heads_out = mixed_blocks.reshape(row_total, heads_local * HEAD_DIM)
    attn_out = lax.psum_scatter(
        jnp.dot(
            slab(heads_out, jnp.int32(0), own_rows * lax.axis_size("narrow")),
            w_proj,
            preferred_element_type=jnp.float32,
        ).astype(jnp.bfloat16),
        "narrow",
        scatter_dimension=0,
        tiled=True,
    ).astype(jnp.float32) + proj_bias.astype(jnp.float32)
    hidden = x_in + scale1 * attn_out
    normed2 = layer_norm(hidden, gain2, shift2).astype(jnp.bfloat16)
    normed2_all = lax.all_gather(normed2, "narrow", axis=0, tiled=True)
    pre_act = jnp.dot(normed2_all, w_fc1, preferred_element_type=jnp.float32) + fc1_bias.astype(
        jnp.float32
    )
    gelu_exact = partial(jax.nn.gelu, approximate=False)
    activated = gelu_exact(pre_act).astype(jnp.bfloat16)
    branch = lax.psum_scatter(
        jnp.dot(
            slab(activated, jnp.int32(0), own_rows * lax.axis_size("narrow")),
            w_fc2,
            preferred_element_type=jnp.float32,
        ).astype(jnp.bfloat16),
        "narrow",
        scatter_dimension=0,
        tiled=True,
    ).astype(jnp.float32) + fc2_bias.astype(jnp.float32)
    output = jnp.where(own_valid, hidden + scale2 * branch, 0.0).astype(jnp.bfloat16)
    grad_out = jnp.where(own_valid, cotangent.astype(jnp.float32), 0.0)
    grad_branch = (scale2 * grad_out).astype(jnp.bfloat16)
    grad_scale_mlp = jnp.sum(grad_out * branch, axis=0)
    grad_fc2_bias = jnp.sum(grad_branch.astype(jnp.float32), axis=0)
    grad_branch_all = lax.all_gather(grad_branch, "narrow", axis=0, tiled=True)
    grad_fc2 = jnp.einsum(
        "rf,rd->fd", activated, grad_branch_all, preferred_element_type=jnp.float32
    )
    grad_act = jnp.einsum("rd,fd->rf", grad_branch_all, w_fc2, preferred_element_type=jnp.float32)
    gelu_unused, gelu_back = jax.vjp(gelu_exact, pre_act)
    grad_pre = gelu_back(grad_act)[0].astype(jnp.bfloat16)
    grad_fc1_bias = jnp.sum(grad_pre.astype(jnp.float32), axis=0)
    grad_fc1 = jnp.einsum("rd,rf->df", normed2_all, grad_pre, preferred_element_type=jnp.float32)
    grad_normed2 = lax.psum_scatter(
        jnp.einsum(
            "rf,df->rd",
            slab(grad_pre, jnp.int32(0), own_rows * lax.axis_size("narrow")),
            w_fc1,
            preferred_element_type=jnp.float32,
        ).astype(jnp.bfloat16),
        "narrow",
        scatter_dimension=0,
        tiled=True,
    ).astype(jnp.float32)
    norm2_unused, norm2_back = jax.vjp(layer_norm, hidden, gain2, shift2)
    grad_hidden_part, grad_norm2_gain, grad_norm2_bias = norm2_back(grad_normed2)
    grad_hidden = grad_out + grad_hidden_part
    grad_attn = (scale1 * grad_hidden).astype(jnp.bfloat16)
    grad_scale_attn = jnp.sum(grad_hidden * attn_out, axis=0)
    grad_proj_bias = jnp.sum(grad_attn.astype(jnp.float32), axis=0)
    grad_attn_all = lax.all_gather(grad_attn, "narrow", axis=0, tiled=True)
    grad_proj = jnp.einsum(
        "re,rd->ed", heads_out, grad_attn_all, preferred_element_type=jnp.float32
    )
    grad_heads = jnp.einsum(
        "rd,ed->re", grad_attn_all, w_proj, preferred_element_type=jnp.float32
    ).astype(jnp.bfloat16)
    grad_heads = grad_heads.reshape(row_total, heads_local, HEAD_DIM)

    def attend_back(carried, block_index):
        key_sum, value_sum = carried
        first_row = block_index * block_rows
        query_block = slab(query_heads, first_row, block_rows)
        grad_block = slab(grad_heads, first_row, block_rows)
        log_block = log_totals[block_index]
        scores = (
            jnp.einsum("qhd,khd->hqk", query_block, key_heads, preferred_element_type=jnp.float32)
            * score_scale
        )
        allowed = allowed_block(crop_of_row, is_valid, first_row, block_rows)
        exact_probs = jnp.where(
            allowed[None],
            jnp.exp(jnp.where(allowed[None], scores, masked_score) - log_block[..., None]),
            0.0,
        )
        rounded = exact_probs.astype(jnp.bfloat16)
        value_sum = value_sum + jnp.einsum(
            "hqk,qhd->khd", rounded, grad_block, preferred_element_type=jnp.float32
        )
        grad_probs = jnp.einsum(
            "qhd,khd->hqk", grad_block, value_heads, preferred_element_type=jnp.float32
        )
        row_inner = jnp.sum(exact_probs * grad_probs, axis=-1, keepdims=True)
        grad_scores = (exact_probs * (grad_probs - row_inner)).astype(jnp.bfloat16)
        grad_query = (
            jnp.einsum("hqk,khd->qhd", grad_scores, key_heads, preferred_element_type=jnp.float32)
            * score_scale
        )
        key_sum = (
            key_sum
            + jnp.einsum(
                "hqk,qhd->khd", grad_scores, query_block, preferred_element_type=jnp.float32
            )
            * score_scale
        )
        return ((key_sum, value_sum), grad_query)

    zero_heads = jnp.zeros((row_total, heads_local, HEAD_DIM), jnp.float32)
    (key_sum, value_sum), query_blocks = lax.scan(attend_back, (zero_heads, zero_heads), block_ids)
    width_local = heads_local * HEAD_DIM
    grad_queries = query_blocks.reshape(row_total, width_local).astype(jnp.bfloat16)
    grad_keys = key_sum.reshape(row_total, width_local).astype(jnp.bfloat16)
    grad_values = value_sum.reshape(row_total, width_local).astype(jnp.bfloat16)
    grad_stack = jnp.stack([grad_queries, grad_keys, grad_values])
    grad_qkv = jnp.einsum(
        "rd,cre->cde", normed1_all, grad_stack, preferred_element_type=jnp.float32
    )
    grad_qv_bias = jnp.stack(
        [
            jnp.sum(grad_queries.astype(jnp.float32), axis=0),
            jnp.sum(grad_values.astype(jnp.float32), axis=0),
        ]
    )
    grad_qkv, grad_qv_bias, grad_proj, grad_fc1, grad_fc1_bias, grad_fc2 = lax.psum(
        (grad_qkv, grad_qv_bias, grad_proj, grad_fc1, grad_fc1_bias, grad_fc2), "wide"
    )
    grad_normed1 = lax.psum_scatter(
        jnp.einsum("cre,cde->rd", grad_stack, w_qkv, preferred_element_type=jnp.float32).astype(
            jnp.bfloat16
        ),
        "narrow",
        scatter_dimension=0,
        tiled=True,
    ).astype(jnp.float32)
    norm1_unused, norm1_back = jax.vjp(layer_norm, x_in, gain1, shift1)
    grad_x_part, grad_norm1_gain, grad_norm1_bias = norm1_back(grad_normed1)
    grad_x_in = grad_hidden + grad_x_part
    grad_tokens = jnp.where(marked, 0.0, grad_x_in)
    grad_mask_token = jnp.sum(jnp.where(marked, grad_x_in, 0.0), axis=0)
    (
        grad_mask_token,
        grad_norm1_gain,
        grad_norm1_bias,
        grad_proj_bias,
        grad_scale_attn,
        grad_norm2_gain,
        grad_norm2_bias,
        grad_fc2_bias,
        grad_scale_mlp,
    ) = lax.psum(
        (
            grad_mask_token,
            grad_norm1_gain,
            grad_norm1_bias,
            grad_proj_bias,
            grad_scale_attn,
            grad_norm2_gain,
            grad_norm2_bias,
            grad_fc2_bias,
            grad_scale_mlp,
        ),
        ("wide", "narrow"),
    )
    return (
        output,
        grad_tokens,
        grad_mask_token,
        grad_norm1_gain,
        grad_norm1_bias,
        grad_qkv,
        grad_qv_bias,
        grad_proj,
        grad_proj_bias,
        grad_scale_attn,
        grad_norm2_gain,
        grad_norm2_bias,
        grad_fc1,
        grad_fc1_bias,
        grad_fc2,
        grad_fc2_bias,
        grad_scale_mlp,
    )


def solution(mesh):
    return jax.shard_map(
        shards,
        mesh=mesh,
        in_specs=(
            P(("wide", "narrow"), None),
            P(("wide", "narrow")),
            P("wide"),
            P("wide"),
            P(),
            P(),
            P(),
            P(None, None, "narrow"),
            P(None, "narrow"),
            P("narrow", None),
            P(),
            P(),
            P(),
            P(),
            P(None, "narrow"),
            P("narrow"),
            P("narrow", None),
            P(),
            P(),
            P(("wide", "narrow"), None),
        ),
        out_specs=(
            P(("wide", "narrow"), None),
            P(("wide", "narrow"), None),
            P(),
            P(),
            P(),
            P(None, None, "narrow"),
            P(None, "narrow"),
            P("narrow", None),
            P(),
            P(),
            P(),
            P(),
            P(None, "narrow"),
            P("narrow"),
            P("narrow", None),
            P(),
            P(),
        ),
        check_vma=False,
    )
```

profile of v0, /device:TPU:0, one launch (start us, length us, event | category | flops | bytes accessed | tf_op | source)
XLA Modules:
  0.0 672.5 jit_solution(14743792329770781047)
XLA Ops:
  15.7 29.3 %all-gather.5.cloned.1.call-done = bf16[1024,768]{1,0:T(8,128)(2,1)} async-done(((bf16[512,768]{1,0:T(8,128)(2,1)}), bf16[1024,768]{1,0:T(8,128)(2,1)}) %all-gather.5.cloned.1.call-update) | async-done | bytes 1572880 | tf_op jit(solution)/shard_map/all_gather | solution.py:101
  45.0 4.0 convolution_bitcast_fusion
  50.9 29.5 %while.27 = (s32[]{:T(128)}, bf16[2,512,6,64]{1,3,2,0:T(8,128)(2,1)}, f32[2,6,512]{2,1,0:T(8,128)S(1)}, s32[2]{0:T(128)S(1)}, s32[1024]{0:T(1024)S(1)}, /*index=...) while((s32[]{:T(128)}, ...), condition=%wide.region_9.10_spmd, body=%wide.region_6.9_spmd.sunk | while | flops 846395392 | bytes 51779372 | solution.py:133
  60.4 4.4 fusion.122
  75.2 4.4 fusion.122
  86.2 25.7 %reduce-scatter.5.cloned.1.call-done = bf16[512,768]{1,0:T(8,128)(2,1)} async-done(((bf16[1024,768]{1,0:T(8,128)(2,1)}), bf16[512,768]{1,0:T(8,128)(2,1)}) %reduce-scatter.5.cloned.1.call-update) | async-done | bytes 786448 | tf_op jit(solution)/shard_map/reduce_scatter | solution.py:135
  119.4 24.2 %all-gather.7.cloned.1.call-done = bf16[1024,768]{1,0:T(8,128)(2,1)} async-done(((bf16[512,768]{1,0:T(8,128)(2,1)}), bf16[1024,768]{1,0:T(8,128)(2,1)}) %all-gather.7.cloned.1.call-update) | async-done | bytes 1572880 | tf_op jit(solution)/shard_map/all_gather | solution.py:147
  143.6 7.4 %fusion.65 = f32[1024,1536]{1,0:T(8,128)} fusion(bf16[1024,768]{1,0:T(8,128)(2,1)} %all-gather.7.cloned.1.call-done, bf16[768,1536]{1,0:T(8,128)(2,1)} %param.38), kind=kOutput, calls=%fused_computation.152 | convolution fusion | flops 2415919104 | bytes 10223616 | tf_op jit(solution)/shard_map/dot_general | solution.py:148
  151.0 21.9 %all-gather.9.cloned.1.call-done = bf16[1024,768]{1,0:T(8,128)(2,1)} async-done(((bf16[512,768]{1,0:T(8,128)(2,1)}), bf16[1024,768]{1,0:T(8,128)(2,1)}) %all-gather.9.cloned.1.call-update) | async-done | bytes 1572880 | tf_op jit(solution)/shard_map/all_gather | solution.py:168
  172.9 20.0 %convert_reduce_fusion = (f32[1536]{0:T(1024)}, bf16[1024,1536]{1,0:T(8,128)(2,1)S(1)}, f32[1024,1536]{1,0:T(8,128)}) fusion(f32[1024,1536]{1,0:T(8,128)} %fusion.65, f32[1536]{0:T(1024)S(1)} %convert_element_type.194, bf16[1024,768]{1,0:T(8,128)(2,1)} %all-gather.9.cloned.1.call-done, bf16[1536,768]{1,0:T(8,128)(2,1)S(1)} %copy-done), kind=kOutput, calls=%fused_computation.49 | convolution fusion | flops 2533882368 | bytes 19673088 | tf_op jit(solution)/shard_map/rd,fd->rf/dot_general | solution.py:172
  194.5 3.7 convolution_convert_fusion.1
  198.3 6.2 multiply_convert_fusion.1
  209.9 14.5 %reduce-scatter.9.cloned.1.call-done = bf16[512,768]{1,0:T(8,128)(2,1)} async-done(((bf16[1024,768]{1,0:T(8,128)(2,1)}), bf16[512,768]{1,0:T(8,128)(2,1)}) %reduce-scatter.9.cloned.1.call-update) | async-done | bytes 786448 | tf_op jit(solution)/shard_map/reduce_scatter | solution.py:177
  229.0 24.3 %reduce-scatter.7.cloned.1.call-done = bf16[512,768]{1,0:T(8,128)(2,1)} async-done(((bf16[1024,768]{1,0:T(8,128)(2,1)}), bf16[512,768]{1,0:T(8,128)(2,1)}) %reduce-scatter.7.cloned.1.call-update) | async-done | bytes 786448 | tf_op jit(solution)/shard_map/reduce_scatter | solution.py:153
  253.3 4.2 multiply_reduce_fusion.2
  260.5 27.3 %all-gather.11.cloned.1.call-done = bf16[1024,768]{1,0:T(8,128)(2,1)} async-done(((bf16[512,768]{1,0:T(8,128)(2,1)}), bf16[1024,768]{1,0:T(8,128)(2,1)}) %all-gather.11.cloned.1.call-update) | async-done | bytes 1572880 | tf_op jit(solution)/shard_map/all_gather | solution.py:194
  291.1 56.1 %while.28 = (s32[]{:T(128)}, f32[1024,6,64]{0,2,1:T(8,128)S(1)}, f32[1024,6,64]{0,2,1:T(8,128)}, bf16[2,512,6,64]{1,3,2,0:T(8,128)(2,1)}, s32[2]{0:T(128)S(1)}, ...) while((s32[]{:T(128)}, f32[1024,6,64]{0,2,1:T(8,128)S(1)}, ...), condition=%wide.region_19.20_spmd.clone, body=%wide.region_17.19_spmd.clone.sunk | while | flops 2075195392 | bytes 132757464 | solution.py:242
  297.1 3.7 bitcast_add_fusion.5
  300.8 7.6 %multiply_reduce_fusion.6 = (f32[6,512]{1,0:T(8,128)S(1)}, f32[6,512,1024]{2,1,0:T(8,128)}) fusion(f32[6,512]{1,0:T(8,128)S(1)} %dynamic-slice_bitcast_fusion.2, f32[6,512,1024]{2,1,0:T(8,128)S(1)} %fusion.132, pred[512,1024]{1,0:T(8,128)(4,1)S(1)} %fusion.134, bf16[1024,6,64]{0,2,1:T(8,128)(2,1)S(1)} %copy-done.27, ...), kind=kOutput, calls=%fused_computation.20.clone.1 | convolution fusion | flops 421524480 | bytes 26898436 | tf_op jit(solution)/shard_map/while/body/eval_jaxpr/qhd,khd->hqk/dot_general | solution.py:223
  308.4 7.3 %multiply_convert_fusion.7 = bf16[6,512,1024]{2,1,0:T(8,128)(2,1)S(1)} fusion(f32[6,512,1024]{2,1,0:T(8,128)} %get-tuple-element.462, f32[6,512]{1,0:T(8,128)S(1)} %get-tuple-element.463, f32[6,512]{1,0:T(8,128)S(1)} %dynamic-slice_bitcast_fusion.2, f32[6,512,1024]{2,1,0:T(8,128)S(1)} %fusion.132, pred[512,1024]{1,0:T(8,128)(4,1)S(1)} %fusion.134), kind=kLoop, calls=%fused_computation.19.clone.1 | loop fusion | flops 22020096 | bytes 32006144 | tf_op jit(solution)/shard_map/while/body/eval_jaxpr/convert_element_type | solution.py:227
  324.9 3.7 bitcast_add_fusion.5
  328.7 7.6 %multiply_reduce_fusion.6 = (f32[6,512]{1,0:T(8,128)S(1)}, f32[6,512,1024]{2,1,0:T(8,128)}) fusion(f32[6,512]{1,0:T(8,128)S(1)} %dynamic-slice_bitcast_fusion.2, f32[6,512,1024]{2,1,0:T(8,128)S(1)} %fusion.132, pred[512,1024]{1,0:T(8,128)(4,1)S(1)} %fusion.134, bf16[1024,6,64]{0,2,1:T(8,128)(2,1)S(1)} %copy-done.27, ...), kind=kOutput, calls=%fused_computation.20.clone.1 | convolution fusion | flops 421524480 | bytes 26898436 | tf_op jit(solution)/shard_map/while/body/eval_jaxpr/qhd,khd->hqk/dot_general | solution.py:223
  336.3 7.3 %multiply_convert_fusion.7 = bf16[6,512,1024]{2,1,0:T(8,128)(2,1)S(1)} fusion(f32[6,512,1024]{2,1,0:T(8,128)} %get-tuple-element.462, f32[6,512]{1,0:T(8,128)S(1)} %get-tuple-element.463, f32[6,512]{1,0:T(8,128)S(1)} %dynamic-slice_bitcast_fusion.2, f32[6,512,1024]{2,1,0:T(8,128)S(1)} %fusion.132, pred[512,1024]{1,0:T(8,128)(4,1)S(1)} %fusion.134), kind=kLoop, calls=%fused_computation.19.clone.1 | loop fusion | flops 22020096 | bytes 32006144 | tf_op jit(solution)/shard_map/while/body/eval_jaxpr/convert_element_type | solution.py:227
  352.4 5.8 bitcast_convert_fusion
  358.2 5.9 fusion.68
  364.2 4.4 fusion.67
  371.1 3.9 convolution_bitcast_fusion.1
  376.5 64.4 %all-reduce.1 = (f32[2,384]{1,0:T(2,128)}, f32[1536]{0:T(1024)}) all-reduce(f32[2,384]{1,0:T(2,128)S(1)} %pad_maximum_fusion.3, f32[1536]{0:T(1024)S(1)} %copy-done.53), channel_id=1, replica_groups=mesh['wide'=16,'narrow'=2] {'wide'}, use_global_device_ids=true, to_apply=%region_32.33 | all-reduce | flops 2304 | bytes 18432 | tf_op jit(solution)/shard_map/psum | solution.py:257
  447.0 39.9 %all-reduce = (f32[768]{0:T(1024)}, f32[768]{0:T(1024)}, f32[768]{0:T(1024)}, f32[768]{0:T(1024)}, f32[768]{0:T(1024)}, /*index=5*/f32[768]{0:T(1024)}, f32[768]{0:T(1024)}, f32[768]{0:T(1024)}, f32[768]{0:T(1024)}) all-reduce(f32[768]{0:T(1024)S(1)} %get-tuple-element.308, ...), channel_id=1, replica_groups=mesh['wide'=16,'narrow'=2] {'wide','narrow'}, use_global_device_ids=true, to_apply=%region_24.25 | all-reduce | flops 6912 | bytes 55296 | tf_op jit(solution)/shard_map/psum | solution.py:283
  489.7 160.6 %all-reduce.5.cloned.1.call-done = (f32[3,768,384]{1,2,0:T(8,128)}, f32[384,768]{1,0:T(8,128)}, f32[768,1536]{1,0:T(8,128)}, f32[1536,768]{1,0:T(8,128)}) async-done(((f32[3,768,384]{1,2,0:T(8,128)}, f32[384,768]{1,0:T(8,128)}, f32[768,1536]{1,0:T(8,128)}, f32[1536,768]{1,0:T(8,128)}), (f32[3,768,384]{1,2,0:T(8,128)}, f32[384,768]{1,0:T(8,128)}, f32[768,1536]{1,0:T(8,128)}, ...) | async-done | bytes 14155792 | tf_op jit(solution)/shard_map/psum | solution.py:257
  650.3 5.2 copy.61
  656.6 5.5 copy.94
  (289 shorter events, 96.4 us)
Async XLA Ops:
  7.2 165.7 %copy-start = (bf16[1536,768]{1,0:T(8,128)(2,1)S(1)}, bf16[1536,768]{1,0:T(8,128)(2,1)}, u32[]{:S(2)}) copy-start(bf16[1536,768]{1,0:T(8,128)(2,1)} %param.40) | copy-start | bytes 7077892
  7.2 6.2 copy-start.2
  7.2 37.8 %all-gather.5.cloned.1.call-start = ((), (), s32[]{:S(2)}) async-start(), calls=%async_computation.4 | async-start | bytes 2359296 | tf_op jit(solution)/shard_map/all_gather | solution.py:101
  8.1 245.1 %copy-start.39 = (pred[512]{0:T(512)(128)(4,1)}, pred[512]{0:T(512)(128)(4,1)S(1)}, u32[]{:S(2)}) copy-start(pred[512]{0:T(512)(128)(4,1)S(1)} %broadcast_compare_fusion) | copy-start | bytes 1540
  8.8 244.4 %copy-start.35 = (f32[768]{0:T(1024)}, f32[768]{0:T(1024)S(1)}, u32[]{:S(2)}) copy-start(f32[768]{0:T(1024)S(1)} %convert_element_type.177) | copy-start | bytes 9220
  12.0 37.1 %copy-start.43 = (f32[512]{0:T(512)}, f32[512]{0:T(512)S(1)}, u32[]{:S(2)}) copy-start(f32[512]{0:T(512)S(1)} %fusion.55) | copy-start | bytes 6148
  14.9 97.0 %reduce-scatter.5.cloned.1.call-start = ((), (), s32[]{:S(2)}) async-start(), calls=%async_computation.5 | async-start | bytes 2359296 | tf_op jit(solution)/shard_map/reduce_scatter | solution.py:135
  85.7 57.8 %all-gather.7.cloned.1.call-start = ((), (), s32[]{:S(2)}) async-start(), calls=%async_computation.6 | async-start | bytes 2359296 | tf_op jit(solution)/shard_map/all_gather | solution.py:147
  116.2 56.7 %all-gather.9.cloned.1.call-start = ((), (), s32[]{:S(2)}) async-start(), calls=%async_computation.8 | async-start | bytes 2359296 | tf_op jit(solution)/shard_map/all_gather | solution.py:168
  119.3 105.2 %reduce-scatter.9.cloned.1.call-start = ((), (), s32[]{:S(2)}) async-start(), calls=%async_computation.9 | async-start | bytes 2359296 | tf_op jit(solution)/shard_map/reduce_scatter | solution.py:177
  172.9 21.6 %copy-start.63 = (bf16[768,1536]{1,0:T(8,128)(2,1)S(1)}, bf16[768,1536]{1,0:T(8,128)(2,1)}, u32[]{:S(2)}) copy-start(bf16[768,1536]{1,0:T(8,128)(2,1)} %param.38) | copy-start | bytes 7077892
  198.2 55.0 %reduce-scatter.7.cloned.1.call-start = ((), (), s32[]{:S(2)}) async-start(), calls=%async_computation.7 | async-start | bytes 2359296 | tf_op jit(solution)/shard_map/reduce_scatter | solution.py:153
  209.8 14.6 %copy-start.4 = (bf16[512,768]{1,0:T(8,128)(2,1)S(1)}, bf16[512,768]{1,0:T(8,128)(2,1)}, u32[]{:S(2)}) copy-start(bf16[512,768]{1,0:T(8,128)(2,1)} %param.24) | copy-start | bytes 2359300
  209.8 14.6 %copy-start.8 = (bf16[512,768]{1,0:T(8,128)(2,1)S(1)}, bf16[512,768]{1,0:T(8,128)(2,1)}, u32[]{:S(2)}) copy-start(bf16[512,768]{1,0:T(8,128)(2,1)} %reduce-scatter.5.cloned.1.call-done) | copy-start | bytes 2359300
  209.9 77.9 %all-gather.11.cloned.1.call-start = ((), (), s32[]{:S(2)}) async-start(), calls=%async_computation.10 | async-start | bytes 2359296 | tf_op jit(solution)/shard_map/all_gather | solution.py:194
  260.4 180.6 %reduce-scatter.11.cloned.1.call-start = ((), (), s32[]{:S(2)}) async-start(), calls=%async_computation.11 | async-start | bytes 2359296 | tf_op jit(solution)/shard_map/reduce_scatter | solution.py:260
  260.4 30.6 %copy-start.6 = (bf16[1024,6,64]{0,2,1:T(8,128)(2,1)S(1)}, bf16[1024,6,64]{0,2,1:T(8,128)(2,1)}, u32[]{:S(2)}) copy-start(bf16[1024,6,64]{0,2,1:T(8,128)(2,1)} %get-tuple-element.588) | copy-start | bytes 2359300
  300.8 7.6 %copy-start.23 = (f32[1024,6,64]{0,2,1:T(8,128)}, f32[1024,6,64]{0,2,1:T(8,128)S(1)}, u32[]{:S(2)}) copy-start(f32[1024,6,64]{0,2,1:T(8,128)S(1)} %bitcast_add_fusion.5) | copy-start | bytes 4718596 | tf_op jit(solution)/shard_map/while
  308.4 7.3 %copy-start.15 = (bf16[2,512,6,64]{1,3,2,0:T(8,128)(2,1)S(1)}, bf16[2,512,6,64]{1,3,2,0:T(8,128)(2,1)}, u32[]{:S(2)}) copy-start(bf16[2,512,6,64]{1,3,2,0:T(8,128)(2,1)} %get-tuple-element.523) | copy-start | bytes 2359300 | tf_op jit(solution)/shard_map/while
  328.6 7.6 %copy-start.23 = (f32[1024,6,64]{0,2,1:T(8,128)}, f32[1024,6,64]{0,2,1:T(8,128)S(1)}, u32[]{:S(2)}) copy-start(f32[1024,6,64]{0,2,1:T(8,128)S(1)} %bitcast_add_fusion.5) | copy-start | bytes 4718596 | tf_op jit(solution)/shard_map/while
  336.3 7.3 %copy-start.15 = (bf16[2,512,6,64]{1,3,2,0:T(8,128)(2,1)S(1)}, bf16[2,512,6,64]{1,3,2,0:T(8,128)(2,1)}, u32[]{:S(2)}) copy-start(bf16[2,512,6,64]{1,3,2,0:T(8,128)(2,1)} %get-tuple-element.523) | copy-start | bytes 2359300 | tf_op jit(solution)/shard_map/while
  358.2 292.2 %all-reduce.5.cloned.1.call-start = ((), (), s32[]{:S(2)}) async-start(), calls=%async_computation.12 | async-start | bytes 28311552 | tf_op jit(solution)/shard_map/psum | solution.py:257
  358.2 5.9 copy-start.20
  375.0 65.9 %copy-start.5 = (bf16[512,768]{1,0:T(8,128)(2,1)S(1)}, bf16[512,768]{1,0:T(8,128)(2,1)}, u32[]{:S(2)}) copy-start(bf16[512,768]{1,0:T(8,128)(2,1)} %param.24) | copy-start | bytes 2359300
  375.0 65.9 %copy-start.36 = (f32[768]{0:T(1024)S(1)}, f32[768]{0:T(1024)}, u32[]{:S(2)}) copy-start(f32[768]{0:T(1024)} %copy-done.35) | copy-start | bytes 9220
  375.0 65.9 %copy-start.38 = (f32[768]{0:T(1024)S(1)}, f32[768]{0:T(1024)}, u32[]{:S(2)}) copy-start(f32[768]{0:T(1024)} %copy-done.37) | copy-start | bytes 9220
  375.0 65.9 %copy-start.40 = (pred[512]{0:T(512)(128)(4,1)S(1)}, pred[512]{0:T(512)(128)(4,1)}, u32[]{:S(2)}) copy-start(pred[512]{0:T(512)(128)(4,1)} %copy-done.39) | copy-start | bytes 1540
  375.0 65.9 %copy-start.42 = (f32[512]{0:T(512)S(1)}, f32[512]{0:T(512)}, u32[]{:S(2)}) copy-start(f32[512]{0:T(512)} %copy-done.41) | copy-start | bytes 6148
  376.1 66.8 %copy-start.46 = (f32[512]{0:T(512)S(1)}, f32[512]{0:T(512)}, u32[]{:S(2)}) copy-start(f32[512]{0:T(512)} %copy-done.45) | copy-start | bytes 6148
  376.1 66.8 %copy-start.44 = (f32[512]{0:T(512)S(1)}, f32[512]{0:T(512)}, u32[]{:S(2)}) copy-start(f32[512]{0:T(512)} %copy-done.43) | copy-start | bytes 6148
  376.3 68.7 %copy-start.10 = (f32[512,768]{1,0:T(8,128)S(1)}, f32[512,768]{1,0:T(8,128)}, u32[]{:S(2)}) copy-start(f32[512,768]{1,0:T(8,128)} %copy-done.9) | copy-start | bytes 4718596
  655.6 6.5 slice-start
  (57 other events, 155.3 us)
Sparse Core Ops, SparseCore 0:
  15.1 29.8 all-gather.4
  85.9 26.0 reduce-scatter.4
  116.3 27.2 all-gather.6
  145.6 27.2 all-gather.8
  198.4 26.0 reduce-scatter.8
  227.2 26.0 reduce-scatter.6
  260.5 27.2 all-gather.10
  358.3 26.0 reduce-scatter.10
  390.1 260.1 all-reduce.4
where the time goes:
time: 681 us; the launch traced here: 672 us
  waiting for transfers between devices  328 us (48%)
  matrix products  115 us (17%)
  blocking collectives  104 us (15%)
  other arithmetic  68.1 us (10%)
  local copies, waits for them, and re-layouts  34.9 us (5%)
  between operations  15 us (2%)
    psum x1, waiting for transfers between devices, shards(): lax.psum((grad_qkv, grad_qv_bias, grad_proj, grad_fc1, grad_fc1_bias, gra...  161 us
    psum x1, blocking collectives, shards(): lax.psum((grad_qkv, grad_qv_bias, grad_proj, grad_fc1, grad_fc1_bias, gra...  64.4 us
    psum x1, blocking collectives, shards(): lax.psum((grad_mask_token, grad_norm1_gain, grad_norm1_bias, grad_proj_bi...  39.9 us
    all_gather x1, waiting for transfers between devices, shards(): normed1_all = lax.all_gather(normed1, 'narrow', axis=0, tiled=True)  29.3 us
    all_gather x1, waiting for transfers between devices, shards(): grad_attn_all = lax.all_gather(grad_attn, 'narrow', axis=0, tiled=True)  27.3 us
    reduce_scatter x1, waiting for transfers between devices, shards(): lax.psum_scatter(jnp.dot(slab(heads_out, jnp.int32(0), own_rows * lax.axi...  25.7 us
    reduce_scatter x1, waiting for transfers between devices, shards(): lax.psum_scatter(jnp.dot(slab(activated, jnp.int32(0), own_rows * lax.axi...  24.3 us
    all_gather x1, waiting for transfers between devices, shards(): normed2_all = lax.all_gather(normed2, 'narrow', axis=0, tiled=True)  24.2 us
  transfers between devices with their start and end apart: 9, of which 8 were waited for; matrix products, arithmetic and copies ran while one was open for 7% of the time, Pallas kernels for 0%

commit v1 on v0

v1 whole, which is shorter than its diff:
```python
from functools import partial

import jax
import jax.numpy as jnp
from jax import lax
from jax.experimental import pallas as pl
from jax.experimental.pallas import tpu as pltpu
from jax.sharding import PartitionSpec as P

HEAD_DIM = 64
B0 = 64
B1 = 144
B2 = 256
B3 = 576

epsilon = 1e-06
masked_score = -1e30
F32 = jnp.float32
BF16 = jnp.bfloat16
WINDOW = 256
BIG_ROWS = 192
SWAP = ((0, 1), (1, 0))


def nn(a, b):
    return lax.dot_general(a, b, (((1,), (0,)), ((), ())), preferred_element_type=F32)


def nt(a, b):
    return lax.dot_general(a, b, (((1,), (1,)), ((), ())), preferred_element_type=F32)


def tn(a, b):
    return lax.dot_general(a, b, (((0,), (0,)), ((), ())), preferred_element_type=F32)


def normed_of(rows_in):
    width = rows_in.shape[-1]
    mean = jnp.sum(rows_in, axis=-1, keepdims=True) * (1.0 / width)
    centered = rows_in - mean
    variance = jnp.sum(centered * centered, axis=-1, keepdims=True) * (1.0 / width)
    inverse = lax.rsqrt(variance + epsilon)
    return centered * inverse, inverse


def norm_back(grad, gain, normal, inverse):
    width = grad.shape[-1]
    g = grad * gain
    mean_g = jnp.sum(g, axis=-1, keepdims=True) * (1.0 / width)
    mean_gn = jnp.sum(g * normal, axis=-1, keepdims=True) * (1.0 / width)
    return (g - mean_g - normal * mean_gn) * inverse


def call(kernel, out_shape, args, flops, moved, name, scratch=(), scalars=0):
    spec = pltpu.PrefetchScalarGridSpec(
        num_scalar_prefetch=scalars,
        grid=(),
        in_specs=[pl.BlockSpec(memory_space=pltpu.VMEM)] * (len(args) - scalars),
        out_specs=jax.tree.map(lambda s: pl.BlockSpec(memory_space=pltpu.VMEM), out_shape),
        scratch_shapes=list(scratch),
    )
    return pl.pallas_call(
        kernel,
        out_shape=out_shape,
        grid_spec=spec,
        compiler_params=pltpu.CompilerParams(vmem_limit_bytes=56 * 1024 * 1024),
        cost_estimate=pl.CostEstimate(flops=flops, bytes_accessed=moved, transcendentals=0),
        name=name,
    )(*args)


def shape(dims, kind=BF16):
    return jax.ShapeDtypeStruct(tuple(dims), kind)


def qkv_kernel(x_ref, vec_ref, bias_ref, w_ref, normed_ref, qkv_ref):
    pairs = qkv_ref.shape[1]
    for first in range(0, x_ref.shape[0], WINDOW):
        rows = pl.ds(first, WINDOW)
        normal, inverse = normed_of(x_ref[rows, :].astype(F32))
        normed = (normal * vec_ref[0:1, :] + vec_ref[1:2, :]).astype(BF16)
        normed_ref[rows, :] = normed
        for c in range(3):
            part = (nn(normed, w_ref[c]) + bias_ref[c : c + 1, :]).astype(BF16)
            if c == 0:
                part = part * 0.125
            for p in range(pairs):
                qkv_ref[c, p, rows, :] = part[:, p * 128 : (p + 1) * 128]


def slot_rows(meta, slot):
    bucket = meta[32 + slot]
    rows = jnp.where(bucket == 0, B0, jnp.where(bucket == 1, B1, jnp.where(bucket == 2, B2, B3)))
    return jnp.where(meta[slot] > 0, rows, 0)


def walk_groups(meta, slots, small, big):
    def more(state):
        slot, first = state
        return jnp.logical_and(slot < slots, meta[slot] > 0)

    def step(state):
        slot, first = state
        first = pl.multiple_of(first, 16)
        rows = slot_rows(meta, slot)

        def take_big():
            big(first, meta[slot])
            return slot + 1, first + B3

        def take_small():
            starts, ends, lasts = [jnp.int32(0)], [rows], [meta[slot]]
            going, end, count = jnp.bool_(True), rows, jnp.int32(1)
            for k in range(1, 4):
                size = slot_rows(meta, slot + k)
                going = going & (slot + k < slots) & (size > 0) & (end + size <= WINDOW)
                starts.append(jnp.where(going, end, WINDOW))
                lasts.append(jnp.where(going, end + meta[slot + k], WINDOW))
                end = jnp.where(going, end + size, end)
                ends.append(jnp.where(going, end, WINDOW))
                count = jnp.where(going, count + 1, count)
            small(first, starts, ends, lasts)
            return slot + count, first + end

        return lax.cond(rows == B3, take_big, take_small)

    lax.while_loop(more, step, (jnp.int32(0), jnp.int32(0)))


def slot_ids(ids, starts, stops, outside):
    result = jnp.full(ids.shape, outside, jnp.int32)
    for k in range(4):
        result = jnp.where((ids >= starts[k]) & (ids < stops[k]), k, result)
    return result


def attention_kernel(slots, meta, own_ref, other_ref, heads_ref, qkv_ref, mixed_ref):
    pairs = own_ref.shape[1]
    half = own_ref.shape[2]
    total = 2 * half
    first_own = pl.multiple_of(meta[64], half)
    first_other = pl.multiple_of(half - meta[64], half)
    for c in range(3):
        for p in range(pairs):
            qkv_ref[c, p, pl.ds(first_own, half), :] = own_ref[c, p]
            qkv_ref[c, p, pl.ds(first_other, half), :] = other_ref[c, p]
            qkv_ref[c, p, pl.ds(total, WINDOW), :] = jnp.zeros((WINDOW, 128), BF16)
    mixed_ref[...] = jnp.zeros(mixed_ref.shape, BF16)
    low = lax.broadcasted_iota(jnp.int32, (1, 128), 1) < HEAD_DIM
    lanes = (low, jnp.logical_not(low))

    def mix(p, first, count, keys, values, mask):
        q = qkv_ref[0, p, pl.ds(first, count), :]
        parts = []
        for h in range(2):
            scores = nt(jnp.where(lanes[h], q, 0), keys)
            scores = jnp.where(mask, scores, masked_score)
            peak = jnp.max(scores, axis=1, keepdims=True)
            exponent = jnp.exp(scores - peak)
            inverse = 1.0 / jnp.sum(exponent, axis=1, keepdims=True)
            parts.append(nn((exponent * inverse).astype(BF16), values))
        mixed_ref[p, pl.ds(first, count), :] = jnp.where(low, parts[0], parts[1]).astype(BF16)

    def small(first, starts, ends, lasts):
        row = slot_ids(lax.broadcasted_iota(jnp.int32, (WINDOW, 1), 0), starts, ends, 4)
        column = slot_ids(lax.broadcasted_iota(jnp.int32, (1, WINDOW), 1), starts, lasts, 5)
        mask = row == column

        def pair(p, carry):
            window = pl.ds(first, WINDOW)
            mix(p, first, WINDOW, qkv_ref[1, p, window, :], qkv_ref[2, p, window, :], mask)
            return carry

        lax.fori_loop(0, pairs, pair, 0)

    def big(first, length):
        mask = lax.broadcasted_iota(jnp.int32, (1, B3), 1) < length

        def pair(p, carry):
            window = pl.ds(first, B3)
            keys = qkv_ref[1, p, window, :]
            values = qkv_ref[2, p, window, :]
            for b in range(B3 // BIG_ROWS):
                mix(p, pl.multiple_of(first + b * BIG_ROWS, 16), BIG_ROWS, keys, values, mask)
            return carry

        lax.fori_loop(0, pairs, pair, 0)

    walk_groups(meta, slots, small, big)
    for p in range(pairs):
        heads_ref[0, :, p * 128 : (p + 1) * 128] = mixed_ref[p, pl.ds(first_own, half), :]
        heads_ref[1, :, p * 128 : (p + 1) * 128] = mixed_ref[p, pl.ds(first_other, half), :]


def attention_back_kernel(
    slots, meta, qkv_ref, own_ref, other_ref, w_ref, grad_ref, out_ref
):
    pairs = qkv_ref.shape[1]
    half = own_ref.shape[0]
    total = 2 * half
    first_own = pl.multiple_of(meta[64], half)
    first_other = pl.multiple_of(half - meta[64], half)
    for source, first in ((own_ref, first_own), (other_ref, first_other)):
        for b in range(0, half, WINDOW):
            part = nt(source[b : b + WINDOW, :], w_ref[...]).astype(BF16)
            for p in range(pairs):
                out_ref[p, pl.ds(pl.multiple_of(first + b, WINDOW), WINDOW), :] = part[
                    :, p * 128 : (p + 1) * 128
                ]
    for p in range(pairs):
        out_ref[p, pl.ds(total, WINDOW), :] = jnp.zeros((WINDOW, 128), BF16)
    grad_ref[...] = jnp.zeros(grad_ref.shape, BF16)
    low = lax.broadcasted_iota(jnp.int32, (1, 128), 1) < HEAD_DIM
    lanes = (low, jnp.logical_not(low))

    def back(p, first, count, keys, values, mask, rows_in):
        q = qkv_ref[0, p, pl.ds(first, count), :]
        grads = out_ref[p, pl.ds(first, count), :]
        if rows_in is not None:
            grads = jnp.where(rows_in, grads, 0)
        d_query = d_key = d_value = None
        for h in range(2):
            q_h = jnp.where(lanes[h], q, 0)
            g_h = jnp.where(lanes[h], grads, 0)
            k_h = jnp.where(lanes[h], keys, 0)
            scores = nt(keys, q_h)
            scores = jnp.where(mask, scores, masked_score)
            peak = jnp.max(scores, axis=0, keepdims=True)
            exponent = jnp.exp(scores - peak)
            probs = exponent * (1.0 / jnp.sum(exponent, axis=0, keepdims=True))
            grad_probs = nt(values, g_h)
            inner = jnp.sum(probs * grad_probs, axis=0, keepdims=True)
            grad_scores = (probs * (grad_probs - inner)).astype(BF16)
            parts = (tn(grad_scores, k_h), nn(grad_scores, q_h), nn(probs.astype(BF16), g_h))
            if h == 0:
                d_query, d_key, d_value = parts
            else:
                d_query, d_key, d_value = d_query + parts[0], d_key + parts[1], d_value + parts[2]
        grad_ref[0, p, pl.ds(first, count), :] = (d_query * 0.125).astype(BF16)
        return d_key, d_value

    def small(first, starts, ends, lasts):
        key = slot_ids(lax.broadcasted_iota(jnp.int32, (WINDOW, 1), 0), starts, lasts, 5)
        query = slot_ids(lax.broadcasted_iota(jnp.int32, (1, WINDOW), 1), starts, ends, 4)
        rows_in = slot_ids(lax.broadcasted_iota(jnp.int32, (WINDOW, 1), 0), starts, ends, 4) < 4
        mask = key == query
        window = pl.ds(first, WINDOW)

        def pair(p, carry):
            d_key, d_value = back(
                p, first, WINDOW, qkv_ref[1, p, window, :], qkv_ref[2, p, window, :], mask, rows_in
            )
            grad_ref[1, p, window, :] = d_key.astype(BF16)
            grad_ref[2, p, window, :] = d_value.astype(BF16)
            return carry

        lax.fori_loop(0, pairs, pair, 0)

    def big(first, length):
        mask = lax.broadcasted_iota(jnp.int32, (B3, 1), 0) < length
        window = pl.ds(first, B3)

        def pair(p, carry):
            keys = qkv_ref[1, p, window, :]
            values = qkv_ref[2, p, window, :]
            d_key = d_value = None
            for b in range(B3 // BIG_ROWS):
                begin = pl.multiple_of(first + b * BIG_ROWS, 16)
                parts = back(p, begin, BIG_ROWS, keys, values, mask, None)
                if b == 0:
                    d_key, d_value = parts
                else:
                    d_key, d_value = d_key + parts[0], d_value + parts[1]
            grad_ref[1, p, window, :] = d_key.astype(BF16)
            grad_ref[2, p, window, :] = d_value.astype(BF16)
            return carry

        lax.fori_loop(0, pairs, pair, 0)

    walk_groups(meta, slots, small, big)


def feed_kernel(
    keep_attn,
    mine_ref,
    theirs_ref,
    x_ref,
    gb_ref,
    vec_ref,
    bias_ref,
    wp_mine_ref,
    wp_theirs_ref,
    w1_ref,
    w2_ref,
    normed_ref,
    act_ref,
    gpre_ref,
    grad_ref,
    *attn_ref,
):
    units = w1_ref.shape[1]
    step = 512
    for first in range(0, x_ref.shape[0], WINDOW):
        rows = pl.ds(first, WINDOW)
        attn = nn(mine_ref[rows, :], wp_mine_ref[...]) + nn(theirs_ref[rows, :], wp_theirs_ref[...])
        attn = attn + vec_ref[6:7, :]
        if keep_attn:
            attn_ref[0][rows, :] = attn
        hidden = x_ref[rows, :].astype(F32) + vec_ref[4:5, :] * attn
        normal, inverse = normed_of(hidden)
        normed = (normal * vec_ref[2:3, :] + vec_ref[3:4, :]).astype(BF16)
        normed_ref[rows, :] = normed
        grad = gb_ref[rows, :]
        total = None
        for u in range(0, units, step):
            cols = slice(u, u + step)
            pre = nn(normed, w1_ref[:, cols]) + bias_ref[0:1, cols]
            half_phi = 0.5 * (1.0 + lax.erf(pre * 0.7071067811865476))
            act_ref[rows, cols] = (pre * half_phi).astype(BF16)
            slope = half_phi + pre * (jnp.exp(pre * pre * -0.5) * 0.3989422804014327)
            gpre = (nt(grad, w2_ref[cols, :]) * slope).astype(BF16)
            gpre_ref[rows, cols] = gpre
            part = nt(gpre, w1_ref[:, cols])
            total = part if total is None else total + part
        grad_ref[rows, :] = total.astype(BF16)


def feed_grad_kernel(
    n_own, n_other, a_own, a_other, p_own, p_other, g_own, g_other, fc1_ref, fc2_ref, bias_ref
):
    fc1_ref[...] = (tn(n_own[...], p_own[...]) + tn(n_other[...], p_other[...])).astype(BF16)
    fc2_ref[...] = (tn(a_own[...], g_own[...]) + tn(a_other[...], g_other[...])).astype(BF16)
    bias_ref[...] = jnp.sum(p_own[...].astype(F32), axis=0, keepdims=True) + jnp.sum(
        p_other[...].astype(F32), axis=0, keepdims=True
    )


def feed_grads(n_own, n_other, a_own, a_other, p_own, p_other, g_own, g_other):
    rows, units = a_own.shape
    width = n_own.shape[1]
    tile = 256
    whole = pl.BlockSpec((rows, width), lambda i: (0, 0))
    cut = pl.BlockSpec((rows, tile), lambda i: (0, i))
    return pl.pallas_call(
        feed_grad_kernel,
        grid=(units // tile,),
        in_specs=[whole, whole, cut, cut, cut, cut, whole, whole],
        out_specs=[
            pl.BlockSpec((width, tile), lambda i: (0, i)),
            pl.BlockSpec((tile, width), lambda i: (i, 0)),
            pl.BlockSpec((1, tile), lambda i: (0, i)),
        ],
        out_shape=[shape((width, units)), shape((units, width)), shape((1, units), F32)],
        compiler_params=pltpu.CompilerParams(vmem_limit_bytes=56 * 1024 * 1024),
        cost_estimate=pl.CostEstimate(
            flops=8 * rows * units * width, bytes_accessed=14000000, transcendentals=0
        ),
        name="feed_grads",
    )(n_own, n_other, a_own, a_other, p_own, p_other, g_own, g_other)


def branch_kernel(act_ref, w2_ref, out_ref):
    for first in range(0, act_ref.shape[0], WINDOW):
        rows = pl.ds(first, WINDOW)
        out_ref[rows, :] = nn(act_ref[rows, :], w2_ref[...]).astype(out_ref.dtype)


def middle_kernel(mine_ref, got_ref, attn_ref, x_ref, gout_ref, vec_ref, hidden_ref, ga_ref, sum_ref):
    sums = None
    for first in range(0, x_ref.shape[0], WINDOW):
        rows = pl.ds(first, WINDOW)
        attn = attn_ref[rows, :]
        normal, inverse = normed_of(x_ref[rows, :].astype(F32) + vec_ref[4:5, :] * attn)
        grad = mine_ref[rows, :].astype(F32) + got_ref[rows, :].astype(F32)
        grad_hidden = gout_ref[rows, :].astype(F32) + norm_back(
            grad, vec_ref[2:3, :], normal, inverse
        )
        hidden_ref[rows, :] = grad_hidden
        grad_attn = (vec_ref[4:5, :] * grad_hidden).astype(BF16)
        ga_ref[rows, :] = grad_attn
        parts = [
            jnp.sum(v, axis=0, keepdims=True)
            for v in (grad * normal, grad, grad_hidden * attn, grad_attn.astype(F32))
        ]
        sums = parts if sums is None else [a + b for a, b in zip(sums, parts)]
    for k in range(4):
        sum_ref[k : k + 1, :] = sums[k]


def share_kernel(meta, grad_ref, w_ref, own_ref, other_ref):
    pairs = grad_ref.shape[1]
    half = own_ref.shape[0]
    for first, target in ((half - meta[64], other_ref), (meta[64], own_ref)):
        for b in range(0, half, WINDOW):
            rows = pl.ds(pl.multiple_of(first + b, WINDOW), WINDOW)
            total = None
            for c in range(3):
                wide = jnp.concatenate([grad_ref[c, p, rows, :] for p in range(pairs)], axis=1)
                part = nt(wide, w_ref[c])
                total = part if total is None else total + part
            target[b : b + WINDOW, :] = total.astype(BF16)


def weight_kernel(
    meta, grad_ref, n_own, n_other, mine_ref, ga_own, ga_other, qkv_ref, proj_ref, bias_ref
):
    pairs = grad_ref.shape[1]
    half = n_own.shape[0]
    own = pl.ds(pl.multiple_of(meta[64], half), half)
    other = pl.ds(pl.multiple_of(half - meta[64], half), half)
    for c in range(3):
        wide_own = jnp.concatenate([grad_ref[c, p, own, :] for p in range(pairs)], axis=1)
        wide_other = jnp.concatenate([grad_ref[c, p, other, :] for p in range(pairs)], axis=1)
        qkv_ref[c] = (tn(n_own[...], wide_own) + tn(n_other[...], wide_other)).astype(BF16)
        bias_ref[c : c + 1, :] = jnp.sum(wide_own.astype(F32), axis=0, keepdims=True) + jnp.sum(
            wide_other.astype(F32), axis=0, keepdims=True
        )
    proj_ref[...] = (tn(mine_ref[0], ga_own[...]) + tn(mine_ref[1], ga_other[...])).astype(BF16)


def final_kernel(mine_ref, got_ref, x_ref, hidden_ref, mark_ref, vec_ref, tokens_ref, sum_ref):
    sums = None
    for first in range(0, x_ref.shape[0], WINDOW):
        rows = pl.ds(first, WINDOW)
        normal, inverse = normed_of(x_ref[rows, :].astype(F32))
        grad = mine_ref[rows, :].astype(F32) + got_ref[rows, :].astype(F32)
        grad_x = hidden_ref[rows, :] + norm_back(grad, vec_ref[0:1, :], normal, inverse)
        marked = mark_ref[rows, :] > 0.5
        tokens_ref[rows, :] = jnp.where(marked, 0.0, grad_x)
        parts = [
            jnp.sum(v, axis=0, keepdims=True)
            for v in (jnp.where(marked, grad_x, 0.0), grad * normal, grad)
        ]
        sums = parts if sums is None else [a + b for a, b in zip(sums, parts)]
    for k in range(3):
        sum_ref[k : k + 1, :] = sums[k]


def own_validity(lengths, buckets, first_own, own_rows):
    slots = lengths.shape[0]
    rows = jnp.where(buckets == 0, B0, jnp.where(buckets == 1, B1, jnp.where(buckets == 2, B2, B3)))
    padded = jnp.where(lengths > 0, rows, 0).astype(jnp.int32)
    before = jnp.tril(jnp.ones((slots, slots), jnp.int32), -1)
    starts = jnp.sum(before * padded[None, :], axis=1)
    ids = first_own + lax.broadcasted_iota(jnp.int32, (own_rows, slots), 0)
    inside = (ids >= starts[None, :]) & (ids < (starts + lengths)[None, :])
    return jnp.any(inside, axis=1, keepdims=True)


def shards(
    tokens,
    token_marks,
    crop_lengths,
    bucket_ids,
    mask_token,
    norm1_gain,
    norm1_bias,
    w_qkv,
    qv_bias,
    w_proj,
    proj_bias,
    scale_attn,
    norm2_gain,
    norm2_bias,
    w_fc1,
    fc1_bias,
    w_fc2,
    fc2_bias,
    scale_mlp,
    cotangent,
):
    half, width = tokens.shape
    slots = crop_lengths.shape[0]
    local = w_qkv.shape[2]
    pairs = local // 128
    units = w_fc1.shape[1]
    first_own = (lax.axis_index("narrow") * half).astype(jnp.int32)
    swap = lambda v: lax.ppermute(v, "narrow", SWAP)

    marked = (token_marks == 1)[:, None]
    x_own = jnp.where(marked, mask_token[None, :], tokens)
    x_other = swap(x_own)
    valid = own_validity(crop_lengths, bucket_ids, first_own, half)
    scale2 = scale_mlp.astype(F32)
    gout_own = jnp.where(valid, cotangent, 0).astype(BF16)
    gb_own = (scale2 * gout_own.astype(F32)).astype(BF16)
    gb_other = swap(gb_own)
    wp_other = swap(w_proj)
    pad = jnp.zeros((32 - slots,), jnp.int32)
    meta = jnp.concatenate(
        [crop_lengths, pad, bucket_ids, pad, jnp.full((8,), first_own, jnp.int32)]
    )
    vec = jnp.stack(
        [norm1_gain, norm1_bias, norm2_gain, norm2_bias, scale_attn, scale_mlp, proj_bias, fc2_bias]
    ).astype(F32)
    bias_q = jnp.stack([qv_bias[0], jnp.zeros_like(qv_bias[0]), qv_bias[1]]).astype(F32)
    bias_1 = fc1_bias.astype(F32)[None, :]
    mark_column = marked.astype(F32)

    def qkv(x):
        return call(
            qkv_kernel,
            [shape((half, width)), shape((3, pairs, half, 128))],
            (x, vec, bias_q, w_qkv),
            6 * half * width * local,
            5000000,
            "norm_qkv",
        )

    n_own, qkv_own = qkv(x_own)
    n_other, qkv_other = qkv(x_other)
    heads, qkv_all = call(
        partial(attention_kernel, slots),
        [shape((2, half, local)), shape((3, pairs, 2 * half + WINDOW, 128))],
        (meta, qkv_own, qkv_other),
        4 * 512 * 1024 * local,
        6000000,
        "attention",
        scratch=[pltpu.VMEM((pairs, 2 * half + WINDOW, 128), BF16)],
        scalars=1,
    )
    got = swap(heads)

    def feed(mine, theirs, x, gb, keep):
        outs = [shape((half, width)), shape((half, units)), shape((half, units)), shape((half, width))]
        if keep:
            outs.append(shape((half, width), F32))
        return call(
            partial(feed_kernel, keep),
            outs,
            (mine, theirs, x, gb, vec, bias_1, w_proj, wp_other, w_fc1, w_fc2),
            6 * half * width * units + 4 * half * local * width,
            12000000,
            "feed",
        )

    n2_other, act_other, gpre_other, gn2_other = feed(heads[1], got[0], x_other, gb_other, False)
    gn2_got = swap(gn2_other)
    n2_own, act_own, gpre_own, gn2_own, attn_own = feed(heads[0], got[1], x_own, gb_own, True)
    g_fc1, g_fc2, g_fc1b = feed_grads(
        n2_own, n2_other, act_own, act_other, gpre_own, gpre_other, gb_own, gb_other
    )
    g_fc1, g_fc2 = lax.psum((g_fc1, g_fc2), "wide")

    def branch_of(act, kind):
        return call(
            branch_kernel, shape((half, width), kind), (act, w_fc2), 2 * half * width * units, 6000000, "branch"
        )

    branch_got = swap(branch_of(act_other, BF16))
    grad_hidden, ga_own, sums2 = call(
        middle_kernel,
        [shape((half, width), F32), shape((half, width)), shape((4, width), F32)],
        (gn2_own, gn2_got, attn_own, x_own, gout_own, vec),
        20 * half * width,
        8000000,
        "middle",
    )
    ga_other = swap(ga_own)
    branch = (
        branch_of(act_own, F32).astype(BF16).astype(F32)
        + branch_got.astype(F32)
        + fc2_bias.astype(F32)
    )
    hidden = x_own.astype(F32) + scale_attn.astype(F32) * attn_own
    output = jnp.where(valid, hidden + scale2 * branch, 0.0).astype(BF16)
    g_smlp = jnp.sum(gout_own.astype(F32) * branch, axis=0)
    g_fc2b = jnp.sum(gb_own.astype(F32), axis=0)

    d_qkv = call(
        partial(attention_back_kernel, slots),
        shape((3, pairs, 2 * half + WINDOW, 128)),
        (meta, qkv_all, ga_own, ga_other, w_proj),
        10 * 512 * 1024 * local,
        8000000,
        "attention_back",
        scratch=[pltpu.VMEM((pairs, 2 * half + WINDOW, 128), BF16)],
        scalars=1,
    )
    gn1_own, gn1_other = call(
        share_kernel,
        [shape((half, width)), shape((half, width))],
        (meta, d_qkv, w_qkv),
        12 * half * width * local,
        6000000,
        "share",
        scalars=1,
    )
    gn1_got = swap(gn1_other)
    g_qkv, g_proj, d_bias = call(
        weight_kernel,
        [shape((3, width, local)), shape((local, width)), shape((3, local), F32)],
        (meta, d_qkv, n_own, n_other, heads, ga_own, ga_other),
        16 * half * width * local,
        9000000,
        "weights",
        scalars=1,
    )
    g_qkv, g_proj = lax.psum((g_qkv, g_proj), "wide")
    grad_tokens, sums1 = call(
        final_kernel,
        [shape((half, width), F32), shape((3, width), F32)],
        (gn1_own, gn1_got, x_own, grad_hidden, mark_column, vec),
        20 * half * width,
        8000000,
        "final",
    )
    rows = jnp.concatenate([sums1, sums2, g_fc2b[None], g_smlp[None]], axis=0)
    g_qvb = jnp.stack([d_bias[0], d_bias[2]])
    rows = lax.psum(rows, ("wide", "narrow"))
    g_qvb, g_fc1b = lax.psum((g_qvb, g_fc1b), "wide")
    return (
        output,
        grad_tokens,
        rows[0],
        rows[1],
        rows[2],
        g_qkv.astype(F32),
        g_qvb,
        g_proj.astype(F32),
        rows[6],
        rows[5],
        rows[3],
        rows[4],
        g_fc1.astype(F32),
        g_fc1b[0],
        g_fc2.astype(F32),
        rows[7],
        rows[8],
    )


def solution(mesh):
    rows = P(("wide", "narrow"), None)
    return jax.shard_map(
        shards,
        mesh=mesh,
        in_specs=(
            rows,
            P(("wide", "narrow")),
            P("wide"),
            P("wide"),
            P(),
            P(),
            P(),
            P(None, None, "narrow"),
            P(None, "narrow"),
            P("narrow", None),
            P(),
            P(),
            P(),
            P(),
            P(None, "narrow"),
            P("narrow"),
            P("narrow", None),
            P(),
            P(),
            rows,
        ),
        out_specs=(
            rows,
            rows,
            P(),
            P(),
            P(),
            P(None, None, "narrow"),
            P(None, "narrow"),
            P("narrow", None),
            P(),
            P(),
            P(),
            P(),
            P(None, "narrow"),
            P("narrow"),
            P("narrow", None),
            P(),
            P(),
        ),
        check_vma=False,
    )
```

time: 681 us -> 365 us (0.54)
  waiting for transfers between devices: 328 us -> 85.8 us
  matrix products: 115 us -> 0 us
  Pallas kernels: 0 us -> 99.1 us
  other arithmetic: 68.1 us -> 18.9 us
  local copies, waits for them, and re-layouts: 34.9 us -> 8.69 us
  blocking collectives: 104 us -> 121 us
  starting transfers between devices: 0.72 us -> 13.7 us
    psum x1, waiting for transfers between devices: 161 us -> 26 us  [shards(): g_qkv, g_proj = lax.psum((g_qkv, g_proj), 'wide')]
    dot_general x26 -> x0, matrix products: 115 us -> none  [the longest x1 20 us: shards(): jnp.einsum('rd,fd->rf', grad_branch_all, w_fc2, preferred_element_type=jn...]
    all_gather x4 -> x0, waiting for transfers between devices: 103 us -> none  [the longest x1 29.3 us: shards(): normed1_all = lax.all_gather(normed1, 'narrow', axis=0, tiled=True)]
    pallas_call x0 -> x13, Pallas kernels: none -> 99.1 us  [the longest x12 88.6 us: call(): pl.pallas_call(kernel, out_shape=out_shape, grid_spec=spec, compiler_para...]
    reduce_scatter x4 -> x0, waiting for transfers between devices: 64.6 us -> none  [the longest x1 25.7 us: shards(): lax.psum_scatter(jnp.dot(slab(heads_out, jnp.int32(0), own_rows * lax.axi...]
    ppermute x0 -> x8, waiting for transfers between devices: none -> 59.9 us  [shards(): swap = lambda v: lax.ppermute(v, 'narrow', SWAP)]
    reduce_sum x18 -> x3, other arithmetic: 32.7 us -> 4.68 us  [the longest x1 3.28 us: shards(): g_smlp = jnp.sum(gout_own.astype(F32) * branch, axis=0)]
    unnamed x129 -> x64, local copies, waits for them, and re-layouts: 22.7 us -> 3.84 us
  transfers between devices with their start and end apart: 9 -> 9, of which waited for: 8 -> 6; matrix products, arithmetic and copies ran while one was open for 7% -> 3% of each run, Pallas kernels for 0% -> 13%
where the time goes in v1:
time: 365 us; the launch traced here: 363 us
  blocking collectives  121 us (33%)
  Pallas kernels  99.1 us (27%)
  waiting for transfers between devices  85.8 us (24%)
  other arithmetic  18.9 us (5%)
  between operations  14.9 us (4%)
  starting transfers between devices  13.7 us (4%)
  local copies, waits for them, and re-layouts  8.69 us (2%)
    pallas_call x12, Pallas kernels, call(): pl.pallas_call(kernel, out_shape=out_shape, grid_spec=spec, compiler_para...  88.6 us
    psum x1, blocking collectives, shards(): g_qvb, g_fc1b = lax.psum((g_qvb, g_fc1b), 'wide')  83.4 us
    ppermute x8, waiting for transfers between devices, shards(): swap = lambda v: lax.ppermute(v, 'narrow', SWAP)  59.9 us
    psum x1, blocking collectives, shards(): rows = lax.psum(rows, ('wide', 'narrow'))  38 us
    psum x1, waiting for transfers between devices, shards(): g_qkv, g_proj = lax.psum((g_qkv, g_proj), 'wide')  26 us
    ppermute x8, starting transfers between devices, shards(): swap = lambda v: lax.ppermute(v, 'narrow', SWAP)  13.6 us
    pallas_call x1, Pallas kernels, feed_grads(): pl.pallas_call(feed_grad_kernel, grid=(units // tile,), in_specs=[whole,...  10.4 us
  transfers between devices with their start and end apart: 9, of which 6 were waited for; matrix products, arithmetic and copies ran while one was open for 3% of the time, Pallas kernels for 13%

profile of v1, /device:TPU:0, one launch (start us, length us, event | category | flops | bytes accessed | tf_op | source)
XLA Modules:
  0.0 362.5 jit_solution(4302707122835727233)
XLA Ops:
  8.1 1.3 broadcast_select_fusion.x_ref
  9.3 3.0 collective-permute-start
  14.8 4.5 %norm_qkv.2 = (bf16[512,768]{1,0:T(8,128)(2,1)}, bf16[3,3,512,128]{3,2,1,0:T(8,128)(2,1)}) custom-call(bf16[512,768]{1,0:T(8,128)(2,1)} %copy-done, f32[8,768]{1,0:T(8,128)} %convert_element_type.62.vec_ref, f32[3,384]{1,0:T(4,128)} %maximum_convert_fusion.bias_ref, bf16[3,768,384]{2,1,0:T(8,128)(2,1)} %w_ref.7), custom_call_target="tpu_custom_call" | custom-call | flops 905969664 | bytes 5000000 | tf_op jit(solution)/shard_map/norm_qkv/pallas_call | solution.py:62
  19.4 10.5 %collective-permute-done.x_ref = bf16[512,768]{1,0:T(8,128)(2,1)S(1)} collective-permute-done((bf16[512,768]{1,0:T(8,128)(2,1)S(1)}, bf16[512,768]{1,0:T(8,128)(2,1)S(1)}, u32[]{:S(2)}, u32[]{:S(2)}) %collective-permute-start) | collective-permute-done | bytes 786464 | tf_op jit(solution)/shard_map/ppermute | solution.py:478
  30.8 4.5 %norm_qkv.3 = (bf16[512,768]{1,0:T(8,128)(2,1)}, bf16[3,3,512,128]{3,2,1,0:T(8,128)(2,1)}) custom-call(bf16[512,768]{1,0:T(8,128)(2,1)} %copy-done.29, f32[8,768]{1,0:T(8,128)} %convert_element_type.62.vec_ref, f32[3,384]{1,0:T(4,128)} %maximum_convert_fusion.bias_ref, bf16[3,768,384]{2,1,0:T(8,128)(2,1)} %w_ref.7), custom_call_target="tpu_custom_call" | custom-call | flops 905969664 | bytes 5000000 | tf_op jit(solution)/shard_map/norm_qkv/pallas_call | solution.py:62
  35.3 10.8 %attention.1 = (bf16[2,512,384]{2,1,0:T(8,128)(2,1)}, bf16[3,3,1280,128]{3,2,1,0:T(8,128)(2,1)}) custom-call(s32[72]{0:T(128)} %concatenate.6.meta, bf16[3,3,512,128]{3,2,1,0:T(8,128)(2,1)} %get-tuple-element.45.own_ref, bf16[3,3,512,128]{3,2,1,0:T(8,128)(2,1)} %get-tuple-element.46.other_ref), custom_call_target="tpu_custom_call" | custom-call | flops 805306368 | bytes 6000000 | tf_op jit(solution)/shard_map/attention/pallas_call | solution.py:62
  46.1 1.8 collective-permute-start.1
  49.4 1.7 collective-permute-start.2
  52.7 10.2 %collective-permute-done.1 = bf16[2,512,384]{2,1,0:T(8,128)(2,1)S(1)} collective-permute-done((bf16[2,512,384]{2,1,0:T(8,128)(2,1)}, bf16[2,512,384]{2,1,0:T(8,128)(2,1)S(1)}, u32[]{:S(2)}, u32[]{:S(2)}) %collective-permute-start.1) | collective-permute-done | bytes 786464 | tf_op jit(solution)/shard_map/ppermute | solution.py:478
  63.9 28.5 %collective-permute-done.2.wp_theirs_ref = bf16[384,768]{1,0:T(8,128)(2,1)S(1)} collective-permute-done((bf16[384,768]{1,0:T(8,128)(2,1)S(1)}, bf16[384,768]{1,0:T(8,128)(2,1)S(1)}, u32[]{:S(2)}, u32[]{:S(2)}) %collective-permute-start.2) | collective-permute-done | bytes 589856 | tf_op jit(solution)/shard_map/ppermute | solution.py:478
  93.5 11.3 %feed.3 = (bf16[512,768]{1,0:T(8,128)(2,1)}, bf16[512,1536]{1,0:T(8,128)(2,1)}, bf16[512,1536]{1,0:T(8,128)(2,1)}, bf16[512,768]{1,0:T(8,128)(2,1)}) custom-call(bf16[512,384]{1,0:T(8,128)(2,1)} %get-tuple-element.97.mine_ref, bf16[512,384]{1,0:T(8,128)(2,1)} %get-tuple-element.95.theirs_ref, bf16[512,768]{1,0:T(8,128)(2,1)} %copy-done.29, ...), custom_call_target="tpu_custom_call" | custom-call | flops 4227858432 | bytes 12000000 | tf_op jit(solution)/shard_map/feed/pallas_call | solution.py:62
  104.7 2.0 collective-permute-start.5
  106.8 11.8 %feed.2 = (bf16[512,768]{1,0:T(8,128)(2,1)}, bf16[512,1536]{1,0:T(8,128)(2,1)}, bf16[512,1536]{1,0:T(8,128)(2,1)}, bf16[512,768]{1,0:T(8,128)(2,1)}, f32[512,768]{1,0:T(8,128)}) custom-call(bf16[512,384]{1,0:T(8,128)(2,1)} %get-tuple-element.98.mine_ref, bf16[512,384]{1,0:T(8,128)(2,1)} %get-tuple-element.96.theirs_ref, bf16[512,768]{1,0:T(8,128)(2,1)} %copy-done, ...), custom_call_target="tpu_custom_call" | custom-call | flops 4227858432 | bytes 12000000 | tf_op jit(solution)/shard_map/feed/pallas_call | solution.py:62
  118.6 4.1 %collective-permute-done.5.got_ref = bf16[512,768]{1,0:T(8,128)(2,1)S(1)} collective-permute-done((bf16[512,768]{1,0:T(8,128)(2,1)}, bf16[512,768]{1,0:T(8,128)(2,1)S(1)}, u32[]{:S(2)}, u32[]{:S(2)}) %collective-permute-start.5) | collective-permute-done | bytes 786464 | tf_op jit(solution)/shard_map/ppermute | solution.py:478
  123.5 5.7 %middle.1 = (f32[512,768]{1,0:T(8,128)}, bf16[512,768]{1,0:T(8,128)(2,1)}, f32[4,768]{1,0:T(4,128)}) custom-call(bf16[512,768]{1,0:T(8,128)(2,1)} %get-tuple-element.52.mine_ref, bf16[512,768]{1,0:T(8,128)(2,1)} %copy-done.6, f32[512,768]{1,0:T(8,128)} %get-tuple-element.48.attn_ref, bf16[512,768]{1,0:T(8,128)(2,1)} %copy-done, ...), custom_call_target="tpu_custom_call" | custom-call | flops 7864320 | bytes 8000000 | tf_op jit(solution)/shard_map/middle/pallas_call | solution.py:62
  129.3 2.3 collective-permute-start.6
  131.6 10.4 %feed_grads.1 = (bf16[768,1536]{1,0:T(8,128)(2,1)}, bf16[1536,768]{1,0:T(8,128)(2,1)}, f32[1,1536]{1,0:T(1,128)}) custom-call(bf16[512,768]{1,0:T(8,128)(2,1)} %get-tuple-element.66.n_own, bf16[512,768]{1,0:T(8,128)(2,1)} %get-tuple-element.67.n_other, bf16[512,1536]{1,0:T(8,128)(2,1)} %get-tuple-element.49.act_ref.a_own, ...), custom_call_target="tpu_custom_call" | custom-call | flops 4831838208 | bytes 14000000 | tf_op jit(solution)/shard_map/feed_grads/pallas_call | solution.py:344
  142.0 6.5 %collective-permute-done.6.other_ref.ga_other = bf16[512,768]{1,0:T(8,128)(2,1)S(1)} collective-permute-done((bf16[512,768]{1,0:T(8,128)(2,1)}, bf16[512,768]{1,0:T(8,128)(2,1)S(1)}, u32[]{:S(2)}, u32[]{:S(2)}) %collective-permute-start.6) | collective-permute-done | bytes 786464 | tf_op jit(solution)/shard_map/ppermute | solution.py:478
  149.4 11.6 %attention_back.1.grad_ref = bf16[3,3,1280,128]{3,2,1,0:T(8,128)(2,1)} custom-call(s32[72]{0:T(128)} %concatenate.6.meta, bf16[3,3,1280,128]{3,2,1,0:T(8,128)(2,1)} %get-tuple-element.51.qkv_ref, bf16[512,768]{1,0:T(8,128)(2,1)} %get-tuple-element.54.own_ref.ga_own, bf16[512,768]{1,0:T(8,128)(2,1)} %copy-done.10, bf16[384,768]{1,0:T(8,128)(2,1)} %w_ref.6), custom_call_target="tpu_custom_call" | custom-call | flops 2013265920 | bytes 8000000 | tf_op jit(solution)/shard_map/attention_back/pallas_call | solution.py:62
  161.0 7.9 %weights.1 = (bf16[3,768,384]{2,1,0:T(8,128)(2,1)}, bf16[384,768]{1,0:T(8,128)(2,1)}, f32[3,384]{1,0:T(4,128)}) custom-call(s32[72]{0:T(128)} %concatenate.6.meta, bf16[3,3,1280,128]{3,2,1,0:T(8,128)(2,1)} %attention_back.1.grad_ref, bf16[512,768]{1,0:T(8,128)(2,1)} %get-tuple-element.61.n_own, bf16[512,768]{1,0:T(8,128)(2,1)} %get-tuple-element.62.n_other, ...), custom_call_target="tpu_custom_call" | custom-call | flops 2415919104 | bytes 9000000 | tf_op jit(solution)/shard_map/weights/pallas_call | solution.py:62
  168.9 4.4 %branch.3 = bf16[512,768]{1,0:T(8,128)(2,1)} custom-call(bf16[512,1536]{1,0:T(8,128)(2,1)} %get-tuple-element.50.act_ref.a_other, bf16[1536,768]{1,0:T(8,128)(2,1)} %w2_ref.7), custom_call_target="tpu_custom_call" | custom-call | flops 1207959552 | bytes 6000000 | tf_op jit(solution)/shard_map/branch/pallas_call | solution.py:62
  173.3 2.3 collective-permute-start.4
  176.6 6.5 %share.1 = (bf16[512,768]{1,0:T(8,128)(2,1)}, bf16[512,768]{1,0:T(8,128)(2,1)}) custom-call(s32[72]{0:T(128)} %concatenate.6.meta, bf16[3,3,1280,128]{3,2,1,0:T(8,128)(2,1)} %attention_back.1.grad_ref, bf16[3,768,384]{2,1,0:T(8,128)(2,1)} %w_ref.7), custom_call_target="tpu_custom_call" | custom-call | flops 1811939328 | bytes 6000000 | tf_op jit(solution)/shard_map/share/pallas_call | solution.py:62
  183.2 4.8 %branch.2 = f32[512,768]{1,0:T(8,128)} custom-call(bf16[512,1536]{1,0:T(8,128)(2,1)} %get-tuple-element.49.act_ref.a_own, bf16[1536,768]{1,0:T(8,128)(2,1)} %w2_ref.7), custom_call_target="tpu_custom_call" | custom-call | flops 1207959552 | bytes 6000000 | tf_op jit(solution)/shard_map/branch/pallas_call | solution.py:62
  188.1 3.3 fusion.1
  191.4 83.4 %all-reduce = (f32[2,384]{1,0:T(2,128)}, f32[1536]{0:T(1024)}) all-reduce(f32[2,384]{1,0:T(2,128)S(1)} %pad_maximum_fusion.1, f32[1536]{0:T(1024)S(1)} %reduce.7), channel_id=1, replica_groups=mesh['wide'=16,'narrow'=2] {'wide'}, use_global_device_ids=true, to_apply=%region_6.7 | all-reduce | flops 2304 | bytes 18432 | tf_op jit(solution)/shard_map/psum | solution.py:611
  274.8 4.9 %final.1 = (f32[512,768]{1,0:T(8,128)}, f32[3,768]{1,0:T(4,128)}) custom-call(bf16[512,768]{1,0:T(8,128)(2,1)} %get-tuple-element.55.mine_ref, bf16[512,768]{1,0:T(8,128)(2,1)} %collective-permute-done.7.got_ref, bf16[512,768]{1,0:T(8,128)(2,1)} %copy-done, f32[512,768]{1,0:T(8,128)} %get-tuple-element.57.hidden_ref, f32[512,1]{1,0:T(8,128)} %copy.38.mark_ref, ...), custom_call_target="tpu_custom_call" | custom-call | flops 7864320 | bytes 8000000 | tf_op jit(solution)/shard_map/final/pallas_call | solution.py:62
  280.4 38.0 %psum.49 = f32[9,768]{1,0:T(8,128)S(1)} all-reduce(f32[9,768]{1,0:T(8,128)S(1)} %pad_maximum_fusion), channel_id=1, replica_groups=mesh['wide'=16,'narrow'=2] {'wide','narrow'}, use_global_device_ids=true, to_apply=%region_4.5 | all-reduce | flops 6912 | bytes 55296 | tf_op jit(solution)/shard_map/psum | solution.py:610
  319.1 26.0 %all-reduce.4.cloned.1.call-done = (bf16[3,768,384]{2,1,0:T(8,128)(2,1)}, bf16[384,768]{1,0:T(8,128)(2,1)}, bf16[768,1536]{1,0:T(8,128)(2,1)}, bf16[1536,768]{1,0:T(8,128)(2,1)}) async-done(((bf16[3,768,384]{2,1,0:T(8,128)(2,1)}, bf16[384,768]{1,0:T(8,128)(2,1)}, bf16[768,1536]{1,0:T(8,128)(2,1)}, bf16[1536,768]{1,0:T(8,128)(2,1)}), (bf16[3,768,384]{2,1,0:T(8,128)(2,1)}, bf16[384,768]{1,0:T(8,128)(2,1)}, ...) | async-done | bytes 7077904 | tf_op jit(solution)/shard_map/psum | solution.py:599
  345.1 3.6 %convert_element_type.75 = f32[3,768,384]{2,1,0:T(8,128)} convert(bf16[3,768,384]{2,1,0:T(8,128)(2,1)} %get-tuple-element.84) | non-fusion elementwise | flops 884736 | bytes 5308416 | tf_op jit(solution)/shard_map/convert_element_type | solution.py:618
  349.9 2.8 convert_element_type.77
  352.7 2.5 convert_element_type.78
  (110 shorter events, 14.5 us)
Async XLA Ops:
  7.2 5.2 %copy-start.27 = (s32[16]{0:T(128)S(1)}, s32[16]{0:T(128)}, u32[]{:S(2)}) copy-start(s32[16]{0:T(128)} %param.22) | copy-start | bytes 196
  7.2 5.2 %copy-start.28 = (s32[16]{0:T(128)S(1)}, s32[16]{0:T(128)}, u32[]{:S(2)}) copy-start(s32[16]{0:T(128)} %param.23) | copy-start | bytes 196
  7.2 5.4 %copy-start.15 = (bf16[768]{0:T(1024)(128)(2,1)S(1)}, bf16[768]{0:T(1024)(128)(2,1)}, u32[]{:S(2)}) copy-start(bf16[768]{0:T(1024)(128)(2,1)} %param.38) | copy-start | bytes 4612
  7.2 5.4 %copy-start.21 = (bf16[768]{0:T(1024)(128)(2,1)S(1)}, bf16[768]{0:T(1024)(128)(2,1)}, u32[]{:S(2)}) copy-start(bf16[768]{0:T(1024)(128)(2,1)} %param.25) | copy-start | bytes 4612
  7.2 5.4 %copy-start.22 = (bf16[768]{0:T(1024)(128)(2,1)S(1)}, bf16[768]{0:T(1024)(128)(2,1)}, u32[]{:S(2)}) copy-start(bf16[768]{0:T(1024)(128)(2,1)} %param.26) | copy-start | bytes 4612
  7.2 5.4 %copy-start.23 = (bf16[768]{0:T(1024)(128)(2,1)S(1)}, bf16[768]{0:T(1024)(128)(2,1)}, u32[]{:S(2)}) copy-start(bf16[768]{0:T(1024)(128)(2,1)} %param.32) | copy-start | bytes 4612
  7.3 5.4 %copy-start.24 = (bf16[768]{0:T(1024)(128)(2,1)S(1)}, bf16[768]{0:T(1024)(128)(2,1)}, u32[]{:S(2)}) copy-start(bf16[768]{0:T(1024)(128)(2,1)} %param.33) | copy-start | bytes 4612
  7.3 5.5 %copy-start.17 = (bf16[768]{0:T(1024)(128)(2,1)S(1)}, bf16[768]{0:T(1024)(128)(2,1)}, u32[]{:S(2)}) copy-start(bf16[768]{0:T(1024)(128)(2,1)} %param.31) | copy-start | bytes 4612
  7.3 5.5 %copy-start.25 = (bf16[768]{0:T(1024)(128)(2,1)S(1)}, bf16[768]{0:T(1024)(128)(2,1)}, u32[]{:S(2)}) copy-start(bf16[768]{0:T(1024)(128)(2,1)} %param.30) | copy-start | bytes 4612
  7.3 5.5 %copy-start.16 = (bf16[768]{0:T(1024)(128)(2,1)S(1)}, bf16[768]{0:T(1024)(128)(2,1)}, u32[]{:S(2)}) copy-start(bf16[768]{0:T(1024)(128)(2,1)} %param.37) | copy-start | bytes 4612
  7.3 6.8 %copy-start.18 = (bf16[2,384]{1,0:T(2,128)(2,1)S(1)}, bf16[2,384]{1,0:T(2,128)(2,1)}, u32[]{:S(2)}) copy-start(bf16[2,384]{1,0:T(2,128)(2,1)} %param.28) | copy-start | bytes 4612
  7.3 337.8 %all-reduce.4.cloned.1.call-start = ((), (), s32[]{:S(2)}) async-start(), calls=%async_computation | async-start | bytes 14155776 | tf_op jit(solution)/shard_map/psum | solution.py:599
  9.3 5.5 %copy-start = (bf16[512,768]{1,0:T(8,128)(2,1)}, bf16[512,768]{1,0:T(8,128)(2,1)S(1)}, u32[]{:S(2)}) copy-start(bf16[512,768]{1,0:T(8,128)(2,1)S(1)} %broadcast_select_fusion.x_ref) | copy-start | bytes 2359300
  9.3 20.6 %collective-permute-start = (bf16[512,768]{1,0:T(8,128)(2,1)S(1)}, bf16[512,768]{1,0:T(8,128)(2,1)S(1)}, u32[]{:S(2)}, u32[]{:S(2)}) collective-permute-start(bf16[512,768]{1,0:T(8,128)(2,1)S(1)} %broadcast_select_fusion.x_ref), channel_id=1, source_target_pairs={{0,1},{1,0},{2,3},{3,2},{4,5},{5,4},{6,7},{7,6},{8,9},{9,8},{10,11... | collective-permute-start | bytes 2359304 | tf_op jit(solution)/shard_map/ppermute | solution.py:478
  35.3 12.6 %copy-start.8 = (bf16[512,768]{1,0:T(8,128)(2,1)S(1)}, bf16[512,768]{1,0:T(8,128)(2,1)}, u32[]{:S(2)}) copy-start(bf16[512,768]{1,0:T(8,128)(2,1)} %param.39) | copy-start | bytes 2359300
  46.0 5.1 %copy-start.20 = (bf16[1536]{0:T(1024)(128)(2,1)S(1)}, bf16[1536]{0:T(1024)(128)(2,1)}, u32[]{:S(2)}) copy-start(bf16[1536]{0:T(1024)(128)(2,1)} %param.35) | copy-start | bytes 9220
  46.1 5.7 %copy-start.7 = (bf16[2,512,384]{2,1,0:T(8,128)(2,1)S(1)}, bf16[2,512,384]{2,1,0:T(8,128)(2,1)}, u32[]{:S(2)}) copy-start(bf16[2,512,384]{2,1,0:T(8,128)(2,1)} %get-tuple-element.47.mine_ref) | copy-start | bytes 2359300
  46.1 16.8 %collective-permute-start.1 = (bf16[2,512,384]{2,1,0:T(8,128)(2,1)}, bf16[2,512,384]{2,1,0:T(8,128)(2,1)S(1)}, u32[]{:S(2)}, u32[]{:S(2)}) collective-permute-start(bf16[2,512,384]{2,1,0:T(8,128)(2,1)} %get-tuple-element.47.mine_ref), channel_id=1, source_target_pairs={{0,1},{1,0},{2,3},{3,2},{4,5},{5,4},{6,7},{7,6},{8,9},{9,8},{10,11... | collective-permute-start | bytes 2359304 | tf_op jit(solution)/shard_map/ppermute | solution.py:478
  49.1 14.8 %copy-start.9 = (bf16[512,768]{1,0:T(8,128)(2,1)}, bf16[512,768]{1,0:T(8,128)(2,1)S(1)}, u32[]{:S(2)}) copy-start(bf16[512,768]{1,0:T(8,128)(2,1)S(1)} %get-tuple-element.89.gb_ref.g_own) | copy-start | bytes 2359300
  49.1 43.3 %collective-permute-start.3 = (bf16[512,768]{1,0:T(8,128)(2,1)S(1)}, bf16[512,768]{1,0:T(8,128)(2,1)S(1)}, u32[]{:S(2)}, u32[]{:S(2)}) collective-permute-start(bf16[512,768]{1,0:T(8,128)(2,1)S(1)} %get-tuple-element.89.gb_ref.g_own), channel_id=1, source_target_pairs={{0,1},{1,0},{2,3},{3,2},{4,5},{5,4},{6,7},{7,6},{8,9},{9,8},{10,11... | collective-permute-start | bytes 2359304 | tf_op jit(solution)/shard_map/ppermute | solution.py:478
  49.4 43.0 %collective-permute-start.2 = (bf16[384,768]{1,0:T(8,128)(2,1)S(1)}, bf16[384,768]{1,0:T(8,128)(2,1)S(1)}, u32[]{:S(2)}, u32[]{:S(2)}) collective-permute-start(bf16[384,768]{1,0:T(8,128)(2,1)S(1)} %copy-done.11), channel_id=1, source_target_pairs={{0,1},{1,0},{2,3},{3,2},{4,5},{5,4},{6,7},{7,6},{8,9},{9,8},{10,11... | collective-permute-start | bytes 1769480 | tf_op jit(solution)/shard_map/ppermute | solution.py:478
  104.7 17.9 %collective-permute-start.5 = (bf16[512,768]{1,0:T(8,128)(2,1)}, bf16[512,768]{1,0:T(8,128)(2,1)S(1)}, u32[]{:S(2)}, u32[]{:S(2)}) collective-permute-start(bf16[512,768]{1,0:T(8,128)(2,1)} %get-tuple-element.53), channel_id=1, source_target_pairs={{0,1},{1,0},{2,3},{3,2},{4,5},{5,4},{6,7},{7,6},{8,9},{9,8},{10,11... | collective-permute-start | bytes 2359304 | tf_op jit(solution)/shard_map/ppermute | solution.py:478
  129.3 19.2 %collective-permute-start.6 = (bf16[512,768]{1,0:T(8,128)(2,1)}, bf16[512,768]{1,0:T(8,128)(2,1)S(1)}, u32[]{:S(2)}, u32[]{:S(2)}) collective-permute-start(bf16[512,768]{1,0:T(8,128)(2,1)} %get-tuple-element.54.own_ref.ga_own), channel_id=1, source_target_pairs={{0,1},{1,0},{2,3},{3,2},{4,5},{5,4},{6,7},{7,6},{8,9},{9,8},{10,11... | collective-permute-start | bytes 2359304 | tf_op jit(solution)/shard_map/ppermute | solution.py:478
  173.3 14.7 %collective-permute-start.4 = (bf16[512,768]{1,0:T(8,128)(2,1)}, bf16[512,768]{1,0:T(8,128)(2,1)}, u32[]{:S(2)}, u32[]{:S(2)}) collective-permute-start(bf16[512,768]{1,0:T(8,128)(2,1)} %branch.3), channel_id=1, source_target_pairs={{0,1},{1,0},{2,3},{3,2},{4,5},{5,4},{6,7},{7,6},{8,9},{9,8},{10,11... | collective-permute-start | bytes 2359304 | tf_op jit(solution)/shard_map/ppermute | solution.py:478
  183.1 4.9 %copy-start.19 = (f32[1,1536]{1,0:T(1,128)S(1)}, f32[1,1536]{1,0:T(1,128)}, u32[]{:S(2)}) copy-start(f32[1,1536]{1,0:T(1,128)} %get-tuple-element.71) | copy-start | bytes 18436
  183.1 5.0 %copy-start.1 = (bf16[512,768]{1,0:T(8,128)(2,1)S(1)}, bf16[512,768]{1,0:T(8,128)(2,1)}, u32[]{:S(2)}) copy-start(bf16[512,768]{1,0:T(8,128)(2,1)} %get-tuple-element.90.gout_ref) | copy-start | bytes 2359300
  183.1 5.0 %copy-start.2 = (f32[512,768]{1,0:T(8,128)S(1)}, f32[512,768]{1,0:T(8,128)}, u32[]{:S(2)}) copy-start(f32[512,768]{1,0:T(8,128)} %get-tuple-element.48.attn_ref) | copy-start | bytes 4718596
  183.1 5.0 %copy-start.3 = (bf16[512,768]{1,0:T(8,128)(2,1)S(1)}, bf16[512,768]{1,0:T(8,128)(2,1)}, u32[]{:S(2)}) copy-start(bf16[512,768]{1,0:T(8,128)(2,1)} %param.20) | copy-start | bytes 2359300
  183.1 5.0 %copy-start.14 = (bf16[768]{0:T(1024)(128)(2,1)S(1)}, bf16[768]{0:T(1024)(128)(2,1)}, u32[]{:S(2)}) copy-start(bf16[768]{0:T(1024)(128)(2,1)} %param.24) | copy-start | bytes 4612
  183.1 91.7 %collective-permute-start.7 = (bf16[512,768]{1,0:T(8,128)(2,1)}, bf16[512,768]{1,0:T(8,128)(2,1)}, u32[]{:S(2)}, u32[]{:S(2)}) collective-permute-start(bf16[512,768]{1,0:T(8,128)(2,1)} %get-tuple-element.56), channel_id=1, source_target_pairs={{0,1},{1,0},{2,3},{3,2},{4,5},{5,4},{6,7},{7,6},{8,9},{9,8},{10,11... | collective-permute-start | bytes 2359304 | tf_op jit(solution)/shard_map/ppermute | solution.py:478
  274.8 4.9 %copy-start.13 = (f32[4,768]{1,0:T(4,128)S(1)}, f32[4,768]{1,0:T(4,128)}, u32[]{:S(2)}) copy-start(f32[4,768]{1,0:T(4,128)} %get-tuple-element.60) | copy-start | bytes 36868
  345.1 4.7 %copy-start.5 = (bf16[768,1536]{1,0:T(8,128)(2,1)S(1)}, bf16[768,1536]{1,0:T(8,128)(2,1)}, u32[]{:S(2)}) copy-start(bf16[768,1536]{1,0:T(8,128)(2,1)} %get-tuple-element.86) | copy-start | bytes 7077892
  (9 other events, 17.7 us)
Sparse Core Ops, SparseCore 0:
  169.1 175.9 all-reduce.3

commit v2 on v1

v2 whole, which is shorter than its diff:
```python
from functools import partial

import jax
import jax.numpy as jnp
from jax import lax
from jax.experimental import pallas as pl
from jax.experimental.pallas import tpu as pltpu
from jax.sharding import PartitionSpec as P

HEAD_DIM = 64
B0 = 64
B1 = 144
B2 = 256
B3 = 576

epsilon = 1e-06
masked_score = -1e30
F32 = jnp.float32
BF16 = jnp.bfloat16
WINDOW = 256
BIG_ROWS = 128
SWAP = ((0, 1), (1, 0))


def nn(a, b):
    return lax.dot_general(a, b, (((1,), (0,)), ((), ())), preferred_element_type=F32)


def nt(a, b):
    return lax.dot_general(a, b, (((1,), (1,)), ((), ())), preferred_element_type=F32)


def tn(a, b):
    return lax.dot_general(a, b, (((0,), (0,)), ((), ())), preferred_element_type=F32)


def normed_of(rows_in):
    width = rows_in.shape[-1]
    mean = jnp.sum(rows_in, axis=-1, keepdims=True) * (1.0 / width)
    centered = rows_in - mean
    variance = jnp.sum(centered * centered, axis=-1, keepdims=True) * (1.0 / width)
    inverse = lax.rsqrt(variance + epsilon)
    return centered * inverse, inverse


def norm_back(grad, gain, normal, inverse):
    width = grad.shape[-1]
    g = grad * gain
    mean_g = jnp.sum(g, axis=-1, keepdims=True) * (1.0 / width)
    mean_gn = jnp.sum(g * normal, axis=-1, keepdims=True) * (1.0 / width)
    return (g - mean_g - normal * mean_gn) * inverse


def estimate(micros):
    return pl.CostEstimate(flops=int(micros * 1e9), bytes_accessed=1000, transcendentals=0)


def call(kernel, out_shape, args, micros, name, scratch=(), scalars=0):
    spec = pltpu.PrefetchScalarGridSpec(
        num_scalar_prefetch=scalars,
        grid=(),
        in_specs=[pl.BlockSpec(memory_space=pltpu.VMEM)] * (len(args) - scalars),
        out_specs=jax.tree.map(lambda s: pl.BlockSpec(memory_space=pltpu.VMEM), out_shape),
        scratch_shapes=list(scratch),
    )
    return pl.pallas_call(
        kernel,
        out_shape=out_shape,
        grid_spec=spec,
        compiler_params=pltpu.CompilerParams(vmem_limit_bytes=22 * 1024 * 1024),
        cost_estimate=estimate(micros),
        name=name,
    )(*args)


def shape(dims, kind=BF16):
    return jax.ShapeDtypeStruct(tuple(dims), kind)


def over_rows(total, body, carry=0):
    def step(i, carry):
        result = body(pl.ds(pl.multiple_of(i * WINDOW, WINDOW), WINDOW), carry)
        return carry if result is None else result

    return lax.fori_loop(0, total // WINDOW, step, carry)


def qkv_kernel(x_ref, vec_ref, bias_ref, w_ref, normed_ref, qkv_ref):
    pairs = qkv_ref.shape[1]

    def block(rows, carry):
        normal, inverse = normed_of(x_ref[rows, :].astype(F32))
        normed = (normal * vec_ref[0:1, :] + vec_ref[1:2, :]).astype(BF16)
        normed_ref[rows, :] = normed
        for c in range(3):
            part = (nn(normed, w_ref[c]) + bias_ref[c : c + 1, :]).astype(BF16)
            if c == 0:
                part = part * 0.125
            for p in range(pairs):
                qkv_ref[c, p, rows, :] = part[:, p * 128 : (p + 1) * 128]

    over_rows(x_ref.shape[0], block)


def slot_rows(meta, slot):
    bucket = meta[32 + slot]
    rows = jnp.where(bucket == 0, B0, jnp.where(bucket == 1, B1, jnp.where(bucket == 2, B2, B3)))
    return jnp.where(meta[slot] > 0, rows, 0)


def walk_groups(meta, slots, small, big):
    def more(state):
        slot, first = state
        return jnp.logical_and(slot < slots, meta[slot] > 0)

    def step(state):
        slot, first = state
        first = pl.multiple_of(first, 16)
        rows = slot_rows(meta, slot)

        def take_big():
            big(first, meta[slot])
            return slot + 1, first + B3

        def take_small():
            starts, ends, lasts = [jnp.int32(0)], [rows], [meta[slot]]
            going, end, count = jnp.bool_(True), rows, jnp.int32(1)
            for k in range(1, 4):
                size = slot_rows(meta, slot + k)
                going = going & (slot + k < slots) & (size > 0) & (end + size <= WINDOW)
                starts.append(jnp.where(going, end, WINDOW))
                lasts.append(jnp.where(going, end + meta[slot + k], WINDOW))
                end = jnp.where(going, end + size, end)
                ends.append(jnp.where(going, end, WINDOW))
                count = jnp.where(going, count + 1, count)
            small(first, starts, ends, lasts)
            return slot + count, first + end

        return lax.cond(rows == B3, take_big, take_small)

    lax.while_loop(more, step, (jnp.int32(0), jnp.int32(0)))


def slot_ids(ids, starts, stops, outside):
    result = jnp.full(ids.shape, outside, jnp.int32)
    for k in range(4):
        result = jnp.where((ids >= starts[k]) & (ids < stops[k]), k, result)
    return result


def attention_kernel(slots, meta, own_ref, other_ref, heads_ref, qkv_ref, mixed_ref):
    pairs = own_ref.shape[1]
    half = own_ref.shape[2]
    total = 2 * half
    first_own = pl.multiple_of(meta[64], half)
    first_other = pl.multiple_of(half - meta[64], half)
    for c in range(3):
        for p in range(pairs):
            qkv_ref[c, p, pl.ds(first_own, half), :] = own_ref[c, p]
            qkv_ref[c, p, pl.ds(first_other, half), :] = other_ref[c, p]
            qkv_ref[c, p, pl.ds(total, WINDOW), :] = jnp.zeros((WINDOW, 128), BF16)
    mixed_ref[...] = jnp.zeros(mixed_ref.shape, BF16)
    low = lax.broadcasted_iota(jnp.int32, (1, 128), 1) < HEAD_DIM
    lanes = (low, jnp.logical_not(low))

    def mix(chosen, first, count, window, mask):
        scores = []
        for p in chosen:
            q = qkv_ref[0, p, pl.ds(first, count), :]
            keys = qkv_ref[1, p, window, :]
            for h in range(2):
                scores.append(nt(jnp.where(lanes[h], q, 0), keys))
        probs = []
        for score in scores:
            score = jnp.where(mask, score, masked_score)
            exponent = jnp.exp(score - jnp.max(score, axis=1, keepdims=True))
            inverse = 1.0 / jnp.sum(exponent, axis=1, keepdims=True)
            probs.append((exponent * inverse).astype(BF16))
        for k, p in enumerate(chosen):
            values = qkv_ref[2, p, window, :]
            mixed = jnp.where(low, nn(probs[2 * k], values), nn(probs[2 * k + 1], values))
            mixed_ref[p, pl.ds(first, count), :] = mixed.astype(BF16)

    def small(first, starts, ends, lasts):
        row = slot_ids(lax.broadcasted_iota(jnp.int32, (WINDOW, 1), 0), starts, ends, 4)
        column = slot_ids(lax.broadcasted_iota(jnp.int32, (1, WINDOW), 1), starts, lasts, 5)
        mix(range(pairs), first, WINDOW, pl.ds(first, WINDOW), row == column)

    def big(first, length):
        mask = lax.broadcasted_iota(jnp.int32, (1, B3), 1) < length

        def block(b, carry):
            begin = pl.multiple_of(first + b * BIG_ROWS, 16)
            mix(range(pairs), begin, BIG_ROWS, pl.ds(first, B3), mask)
            return carry

        lax.fori_loop(0, pl.cdiv(B3, BIG_ROWS), block, 0)

    walk_groups(meta, slots, small, big)
    for p in range(pairs):
        heads_ref[0, :, p * 128 : (p + 1) * 128] = mixed_ref[p, pl.ds(first_own, half), :]
        heads_ref[1, :, p * 128 : (p + 1) * 128] = mixed_ref[p, pl.ds(first_other, half), :]


def attention_back_kernel(
    slots, meta, qkv_ref, own_ref, other_ref, w_ref, grad_ref, out_ref, sum_ref
):
    pairs = qkv_ref.shape[1]
    half = own_ref.shape[0]
    total = 2 * half
    first_own = pl.multiple_of(meta[64], half)
    first_other = pl.multiple_of(half - meta[64], half)
    for source, first in ((own_ref, first_own), (other_ref, first_other)):

        def project(i, carry):
            begin = pl.multiple_of(i * WINDOW, WINDOW)
            part = nt(source[pl.ds(begin, WINDOW), :], w_ref[...]).astype(BF16)
            for p in range(pairs):
                out_ref[p, pl.ds(pl.multiple_of(first + begin, WINDOW), WINDOW), :] = part[
                    :, p * 128 : (p + 1) * 128
                ]
            return carry

        lax.fori_loop(0, half // WINDOW, project, 0)
    for p in range(pairs):
        out_ref[p, pl.ds(total, WINDOW), :] = jnp.zeros((WINDOW, 128), BF16)
    grad_ref[...] = jnp.zeros(grad_ref.shape, BF16)
    low = lax.broadcasted_iota(jnp.int32, (1, 128), 1) < HEAD_DIM
    lanes = (low, jnp.logical_not(low))

    def back(chosen, first, count, window, mask, rows_in):
        work = []
        for p in chosen:
            q = qkv_ref[0, p, pl.ds(first, count), :]
            keys = qkv_ref[1, p, window, :]
            values = qkv_ref[2, p, window, :]
            grads = out_ref[p, pl.ds(first, count), :]
            if rows_in is not None:
                grads = jnp.where(rows_in, grads, 0)
            for h in range(2):
                q_h = jnp.where(lanes[h], q, 0)
                g_h = jnp.where(lanes[h], grads, 0)
                work.append((nt(keys, q_h), nt(values, g_h), q_h, g_h))
        pieces = []
        for scores, grad_probs, q_h, g_h in work:
            scores = jnp.where(mask, scores, masked_score)
            exponent = jnp.exp(scores - jnp.max(scores, axis=0, keepdims=True))
            probs = exponent * (1.0 / jnp.sum(exponent, axis=0, keepdims=True))
            inner = jnp.sum(probs * grad_probs, axis=0, keepdims=True)
            grad_scores = (probs * (grad_probs - inner)).astype(BF16)
            pieces.append((probs.astype(BF16), grad_scores, q_h, g_h))
        results = []
        for k, p in enumerate(chosen):
            keys = qkv_ref[1, p, window, :]
            d_query = d_key = d_value = 0.0
            for h in range(2):
                probs, grad_scores, q_h, g_h = pieces[2 * k + h]
                d_query = d_query + tn(grad_scores, jnp.where(lanes[h], keys, 0))
                d_key = d_key + nn(grad_scores, q_h)
                d_value = d_value + nn(probs, g_h)
            grad_ref[0, p, pl.ds(first, count), :] = (d_query * 0.125).astype(BF16)
            results.append((d_key, d_value))
        return results

    def small(first, starts, ends, lasts):
        key = slot_ids(lax.broadcasted_iota(jnp.int32, (WINDOW, 1), 0), starts, lasts, 5)
        query = slot_ids(lax.broadcasted_iota(jnp.int32, (1, WINDOW), 1), starts, ends, 4)
        rows_in = slot_ids(lax.broadcasted_iota(jnp.int32, (WINDOW, 1), 0), starts, ends, 4) < 4
        window = pl.ds(first, WINDOW)
        parts = back(range(pairs), first, WINDOW, window, key == query, rows_in)
        for p, (d_key, d_value) in enumerate(parts):
            grad_ref[1, p, window, :] = d_key.astype(BF16)
            grad_ref[2, p, window, :] = d_value.astype(BF16)

    def big(first, length):
        mask = lax.broadcasted_iota(jnp.int32, (B3, 1), 0) < length
        window = pl.ds(first, B3)
        sum_ref[...] = jnp.zeros(sum_ref.shape, F32)

        def block(b, carry):
            begin = pl.multiple_of(first + b * BIG_ROWS, 16)
            rows_in = lax.broadcasted_iota(jnp.int32, (BIG_ROWS, 1), 0) < B3 - b * BIG_ROWS
            for p, parts in enumerate(back(range(pairs), begin, BIG_ROWS, window, mask, rows_in)):
                for c in range(2):
                    sum_ref[c, p] += parts[c]
            return carry

        lax.fori_loop(0, pl.cdiv(B3, BIG_ROWS), block, 0)
        for p in range(pairs):
            for c in range(2):
                grad_ref[1 + c, p, window, :] = sum_ref[c, p].astype(BF16)

    walk_groups(meta, slots, small, big)


def feed_kernel(
    keep_attn,
    meta,
    mine_ref,
    theirs_ref,
    x_ref,
    gb_ref,
    vec_ref,
    bias_ref,
    wp_ref,
    wp_first_ref,
    wp_second_ref,
    w1_ref,
    w2_ref,
    normed_ref,
    act_ref,
    gpre_ref,
    grad_ref,
    *attn_ref,
):
    units = w1_ref.shape[1]
    step = 512
    which = 0 if keep_attn else 1
    even = meta[65] == 0
    wp_theirs = jnp.concatenate(
        [
            jnp.where(even, wp_first_ref[...], wp_second_ref[...]),
            jnp.where(even, wp_second_ref[...], wp_first_ref[...]),
        ],
        axis=1,
    )

    def block(rows, carry):
        attn = nn(mine_ref[which, rows, :], wp_ref[...])
        attn = attn + nn(theirs_ref[1 - which, rows, :], wp_theirs)
        attn = attn + vec_ref[6:7, :]
        if keep_attn:
            attn_ref[0][rows, :] = attn
        hidden = x_ref[rows, :].astype(F32) + vec_ref[4:5, :] * attn
        normal, inverse = normed_of(hidden)
        normed = (normal * vec_ref[2:3, :] + vec_ref[3:4, :]).astype(BF16)
        normed_ref[rows, :] = normed
        grad = gb_ref[rows, :]
        total = None
        for u in range(0, units, step):
            cols = slice(u, u + step)
            pre = nn(normed, w1_ref[:, cols]) + bias_ref[0:1, cols]
            half_phi = 0.5 * (1.0 + lax.erf(pre * 0.7071067811865476))
            act_ref[rows, cols] = (pre * half_phi).astype(BF16)
            slope = half_phi + pre * (jnp.exp(pre * pre * -0.5) * 0.3989422804014327)
            gpre = (nt(grad, w2_ref[cols, :]) * slope).astype(BF16)
            gpre_ref[rows, cols] = gpre
            part = nt(gpre, w1_ref[:, cols])
            total = part if total is None else total + part
        grad_ref[rows, :] = total.astype(BF16)

    over_rows(x_ref.shape[0], block)


def feed_grad_kernel(
    n_own, n_other, a_own, a_other, p_own, p_other, g_own, g_other, fc1_ref, fc2_ref, bias_ref
):
    units = a_own.shape[1]
    tile = 512

    def block(i, carry):
        cols = pl.ds(pl.multiple_of(i * tile, tile), tile)
        fc1_ref[:, cols] = (
            tn(n_own[...], p_own[:, cols]) + tn(n_other[...], p_other[:, cols])
        ).astype(BF16)
        fc2_ref[cols, :] = (
            tn(a_own[:, cols], g_own[...]) + tn(a_other[:, cols], g_other[...])
        ).astype(BF16)
        bias_ref[:, cols] = jnp.sum(p_own[:, cols].astype(F32), axis=0, keepdims=True) + jnp.sum(
            p_other[:, cols].astype(F32), axis=0, keepdims=True
        )
        return carry

    lax.fori_loop(0, units // tile, block, 0)


def feed_grads(n_own, n_other, a_own, a_other, p_own, p_other, g_own, g_other):
    units = a_own.shape[1]
    width = n_own.shape[1]
    return call(
        feed_grad_kernel,
        [shape((width, units)), shape((units, width)), shape((1, units), F32)],
        (n_own, n_other, a_own, a_other, p_own, p_other, g_own, g_other),
        8,
        "feed_grads",
    )


def branch_kernel(act_ref, w2_ref, out_ref):
    def block(rows, carry):
        out_ref[rows, :] = nn(act_ref[rows, :], w2_ref[...]).astype(out_ref.dtype)

    over_rows(act_ref.shape[0], block)


def middle_kernel(mine_ref, got_ref, attn_ref, x_ref, gout_ref, vec_ref, hidden_ref, ga_ref, sum_ref):
    def block(rows, sums):
        attn = attn_ref[rows, :]
        normal, inverse = normed_of(x_ref[rows, :].astype(F32) + vec_ref[4:5, :] * attn)
        grad = mine_ref[rows, :].astype(F32) + got_ref[rows, :].astype(F32)
        grad_hidden = gout_ref[rows, :].astype(F32) + norm_back(
            grad, vec_ref[2:3, :], normal, inverse
        )
        hidden_ref[rows, :] = grad_hidden
        grad_attn = (vec_ref[4:5, :] * grad_hidden).astype(BF16)
        ga_ref[rows, :] = grad_attn
        parts = [
            jnp.sum(v, axis=0, keepdims=True)
            for v in (grad * normal, grad, grad_hidden * attn, grad_attn.astype(F32))
        ]
        return [a + b for a, b in zip(sums, parts)]

    zero = jnp.zeros((1, x_ref.shape[1]), F32)
    sums = over_rows(x_ref.shape[0], block, [zero] * 4)
    for k in range(4):
        sum_ref[k : k + 1, :] = sums[k]


def share_kernel(meta, grad_ref, w_ref, own_ref, other_ref):
    pairs = grad_ref.shape[1]
    half = own_ref.shape[0]
    for first, target in ((half - meta[64], other_ref), (meta[64], own_ref)):

        def block(to_rows, carry):
            rows = pl.ds(pl.multiple_of(first + to_rows.start, WINDOW), WINDOW)
            total = None
            for c in range(3):
                wide = jnp.concatenate([grad_ref[c, p, rows, :] for p in range(pairs)], axis=1)
                part = nt(wide, w_ref[c])
                total = part if total is None else total + part
            target[to_rows, :] = total.astype(BF16)

        over_rows(half, block)


def weight_kernel(
    meta, grad_ref, n_own, n_other, mine_ref, ga_own, ga_other, out_ref, bias_ref
):
    pairs = grad_ref.shape[1]
    width = n_own.shape[1]
    local = pairs * 128
    half = n_own.shape[0]
    own = pl.ds(pl.multiple_of(meta[64], half), half)
    other = pl.ds(pl.multiple_of(half - meta[64], half), half)
    for c in range(3):
        wide_own = jnp.concatenate([grad_ref[c, p, own, :] for p in range(pairs)], axis=1)
        wide_other = jnp.concatenate([grad_ref[c, p, other, :] for p in range(pairs)], axis=1)
        out_ref[pl.ds(c * width, width), :] = (
            tn(n_own[...], wide_own) + tn(n_other[...], wide_other)
        ).astype(BF16)
        bias_ref[c : c + 1, :] = jnp.sum(wide_own.astype(F32), axis=0, keepdims=True) + jnp.sum(
            wide_other.astype(F32), axis=0, keepdims=True
        )
    proj = (tn(mine_ref[0], ga_own[...]) + tn(mine_ref[1], ga_other[...])).astype(BF16)
    for b in range(width // local):
        out_ref[pl.ds(3 * width + b * local, local), :] = proj[:, b * local : (b + 1) * local]


def final_kernel(mine_ref, got_ref, x_ref, hidden_ref, mark_ref, vec_ref, tokens_ref, sum_ref):
    def block(rows, sums):
        normal, inverse = normed_of(x_ref[rows, :].astype(F32))
        grad = mine_ref[rows, :].astype(F32) + got_ref[rows, :].astype(F32)
        grad_x = hidden_ref[rows, :] + norm_back(grad, vec_ref[0:1, :], normal, inverse)
        marked = mark_ref[rows, :] > 0.5
        tokens_ref[rows, :] = jnp.where(marked, 0.0, grad_x)
        parts = [
            jnp.sum(v, axis=0, keepdims=True)
            for v in (jnp.where(marked, grad_x, 0.0), grad * normal, grad)
        ]
        return [a + b for a, b in zip(sums, parts)]

    zero = jnp.zeros((1, x_ref.shape[1]), F32)
    sums = over_rows(x_ref.shape[0], block, [zero] * 3)
    for k in range(3):
        sum_ref[k : k + 1, :] = sums[k]


def unpack_kernel(meta, mine_ref, got_ref, qkv_ref, proj_ref):
    width = qkv_ref.shape[1]
    local = qkv_ref.shape[2]

    def write(low_ref, high_ref):
        qkv_ref[0] = low_ref[:width, :].astype(F32)
        qkv_ref[1] = low_ref[width:, :].astype(F32)
        qkv_ref[2] = high_ref[:width, :].astype(F32)
        for b in range(width // local):
            proj_ref[:, b * local : (b + 1) * local] = high_ref[
                width + b * local : width + (b + 1) * local, :
            ].astype(F32)

    @pl.when(meta[65] == 0)
    def even():
        write(mine_ref, got_ref)

    @pl.when(meta[65] != 0)
    def odd():
        write(got_ref, mine_ref)


def own_validity(lengths, buckets, first_own, own_rows):
    slots = lengths.shape[0]
    rows = jnp.where(buckets == 0, B0, jnp.where(buckets == 1, B1, jnp.where(buckets == 2, B2, B3)))
    padded = jnp.where(lengths > 0, rows, 0).astype(jnp.int32)
    before = jnp.tril(jnp.ones((slots, slots), jnp.int32), -1)
    starts = jnp.sum(before * padded[None, :], axis=1)
    ids = first_own + lax.broadcasted_iota(jnp.int32, (own_rows, slots), 0)
    inside = (ids >= starts[None, :]) & (ids < (starts + lengths)[None, :])
    return jnp.any(inside, axis=1, keepdims=True)


def steps_of_wide():
    size = lax.axis_size("wide")
    bits = list(range(size.bit_length() - 1))
    even, odd = bits[1:], bits[1:]
    if len(bits) > 2:
        odd = [bits[2], bits[1]] + bits[3:]
    return [(0, 0)] + list(zip(even, odd))


def hop(value, step):
    size = lax.axis_size("wide")
    pairs = tuple((i, i ^ (1 << step[i % 2])) for i in range(size))
    return lax.ppermute(value, "wide", pairs)


def upper(step):
    index = lax.axis_index("wide")
    shift = jnp.where(index % 2 == 0, step[0], step[1])
    return (index >> shift) % 2


def halve(part, step):
    rows = part.shape[0] // 2
    high = upper(step)
    keep = lax.dynamic_slice_in_dim(part, high * rows, rows)
    give = lax.dynamic_slice_in_dim(part, (1 - high) * rows, rows)
    return (keep.astype(F32) + hop(give, step).astype(F32)).astype(BF16)


def double(part, step):
    got = hop(part, step)
    return jnp.where(
        upper(step) == 0, jnp.concatenate([part, got]), jnp.concatenate([got, part])
    )


def column_half(w_proj):
    columns = w_proj.shape[1] // 2
    core = lax.axis_index("wide") % 2
    return lax.ppermute(
        lax.dynamic_slice_in_dim(w_proj, core * columns, columns, 1), "narrow", SWAP
    )


def shards(
    tokens,
    token_marks,
    crop_lengths,
    bucket_ids,
    mask_token,
    norm1_gain,
    norm1_bias,
    w_qkv,
    qv_bias,
    w_proj,
    proj_bias,
    scale_attn,
    norm2_gain,
    norm2_bias,
    w_fc1,
    fc1_bias,
    w_fc2,
    fc2_bias,
    scale_mlp,
    cotangent,
):
    half, width = tokens.shape
    slots = crop_lengths.shape[0]
    local = w_qkv.shape[2]
    pairs = local // 128
    units = w_fc1.shape[1]
    first_own = (lax.axis_index("narrow") * half).astype(jnp.int32)
    swap = lambda v: lax.ppermute(v, "narrow", SWAP)

    marked = (token_marks == 1)[:, None]
    x_own = jnp.where(marked, mask_token[None, :], tokens)
    x_other = swap(x_own)
    valid = own_validity(crop_lengths, bucket_ids, first_own, half)
    scale2 = scale_mlp.astype(F32)
    gout_own = jnp.where(valid, cotangent, 0).astype(BF16)
    gb_own = (scale2 * gout_own.astype(F32)).astype(BF16)
    pad = jnp.zeros((32 - slots,), jnp.int32)
    meta = jnp.concatenate(
        [
            crop_lengths,
            pad,
            bucket_ids,
            pad,
            jnp.stack([first_own, (lax.axis_index("wide") % 2).astype(jnp.int32)]),
        ]
    )
    vec = jnp.stack(
        [norm1_gain, norm1_bias, norm2_gain, norm2_bias, scale_attn, scale_mlp, proj_bias, fc2_bias]
    ).astype(F32)
    bias_q = jnp.stack([qv_bias[0], jnp.zeros_like(qv_bias[0]), qv_bias[1]]).astype(F32)
    bias_1 = fc1_bias.astype(F32)[None, :]
    mark_column = marked.astype(F32)

    def qkv(x):
        return call(
            qkv_kernel,
            [shape((half, width)), shape((3, pairs, half, 128))],
            (x, vec, bias_q, w_qkv),
            2,
            "norm_qkv",
        )

    n_own, qkv_own = qkv(x_own)
    n_own, gb_start, wp_start = lax.optimization_barrier((n_own, gb_own, w_proj))
    gb_other = swap(gb_start)
    wp_mine = column_half(wp_start)
    n_other, qkv_other = qkv(x_other)
    heads, qkv_all = call(
        partial(attention_kernel, slots),
        [shape((2, half, local)), shape((3, pairs, 2 * half + WINDOW, 128))],
        (meta, qkv_own, qkv_other),
        8,
        "attention",
        scratch=[pltpu.VMEM((pairs, 2 * half + WINDOW, 128), BF16)],
        scalars=1,
    )
    heads, gb_other, wp_mine = lax.optimization_barrier((heads, gb_other, wp_mine))
    got = swap(heads)
    wp_next = hop(wp_mine, (0, 0))

    def feed(x, gb, keep):
        outs = [shape((half, width)), shape((half, units)), shape((half, units)), shape((half, width))]
        if keep:
            outs.append(shape((half, width), F32))
        return call(
            partial(feed_kernel, keep),
            outs,
            (meta, heads, got, x, gb, vec, bias_1, w_proj, wp_mine, wp_next, w_fc1, w_fc2),
            7,
            "feed",
            scalars=1,
        )

    n2_other, act_other, gpre_other, gn2_other = feed(x_other, gb_other, False)
    gn2_got = swap(gn2_other)
    n2_own, act_own, gpre_own, gn2_own, attn_own = feed(x_own, gb_own, True)
    g_fc1, g_fc2, g_fc1b = feed_grads(
        n2_own, n2_other, act_own, act_other, gpre_own, gpre_other, gb_own, gb_other
    )

    gn2_got, g_fc1, g_fc2 = lax.optimization_barrier((gn2_got, g_fc1, g_fc2))
    sum_fc1, sum_fc2 = lax.psum((g_fc1, g_fc2), "wide")

    operands = (
        gn2_own, gn2_got, attn_own, x_own, gout_own, gb_own, act_own, act_other, qkv_all, n_own, n_other, heads, g_fc1b
    )

    def rest(operands):
        gn2_own, gn2_got, attn_own, x_own, gout_own, gb_own, act_own, act_other, qkv_all, n_own, n_other, heads, g_fc1b = operands
        grad_hidden, ga_own, sums2 = call(
            middle_kernel,
            [shape((half, width), F32), shape((half, width)), shape((4, width), F32)],
            (gn2_own, gn2_got, attn_own, x_own, gout_own, vec),
            3,
            "middle",
        )
        ga_other = swap(ga_own)
        def branch_of(act, kind):
            return call(
                branch_kernel, shape((half, width), kind), (act, w_fc2), 2, "branch"
            )

        branch_got = swap(branch_of(act_other, BF16))
        branch_own = branch_of(act_own, F32)
        ga_other, branch_own = lax.optimization_barrier((ga_other, branch_own))
        d_qkv = call(
            partial(attention_back_kernel, slots),
            shape((3, pairs, 2 * half + WINDOW, 128)),
            (meta, qkv_all, ga_own, ga_other, w_proj),
            9,
            "attention_back",
            scratch=[
                pltpu.VMEM((pairs, 2 * half + WINDOW, 128), BF16),
                pltpu.VMEM((2, pairs, B3, 128), F32),
            ],
            scalars=1,
        )
        d_qkv, branch_got = lax.optimization_barrier((d_qkv, branch_got))
        gn1_own, gn1_other = call(
            share_kernel,
            [shape((half, width)), shape((half, width))],
            (meta, d_qkv, w_qkv),
            3,
            "share",
            scalars=1,
        )
        gn1_got = swap(gn1_other)
        d_qkv, gn1_own = lax.optimization_barrier((d_qkv, gn1_own))
        g_attn, d_bias = call(
            weight_kernel,
            [shape((4 * width, local)), shape((3, local), F32)],
            (meta, d_qkv, n_own, n_other, heads, ga_own, ga_other),
            5,
            "weights",
            scalars=1,
        )
        steps = steps_of_wide()
        part = halve(halve(g_attn, steps[0]), steps[1])
        part, gn1_got = lax.optimization_barrier((part, gn1_got))
        branch = branch_own + branch_got.astype(F32) + fc2_bias.astype(F32)
        hidden = x_own.astype(F32) + scale_attn.astype(F32) * attn_own
        output = jnp.where(valid, hidden + scale2 * branch, 0.0).astype(BF16)
        g_smlp = jnp.sum(gout_own.astype(F32) * branch, axis=0)
        g_fc2b = jnp.sum(gb_own.astype(F32), axis=0)
        grad_tokens, sums1 = call(
            final_kernel,
            [shape((half, width), F32), shape((3, width), F32)],
            (gn1_own, gn1_got, x_own, grad_hidden, mark_column, vec),
            3,
            "final",
        )
        wide_only = jnp.concatenate([d_bias[0], d_bias[2], g_fc1b[0]]).reshape(-1, width)
        small = jnp.concatenate([sums1, sums2, g_fc2b[None], g_smlp[None], wide_only], axis=0)
        for step in steps[2:]:
            part = halve(part, step)
        for step in reversed(steps[1:]):
            part, small = lax.optimization_barrier((part, small))
            part, small = double(part, step), small + hop(small, step)
        small = small + hop(small, steps[0])
        count = 9
        rows = small[:count] + swap(small[:count])
        flat = small[count:].reshape(-1)
        g_qvb = flat[: 2 * local].reshape(2, local)
        g_fc1b = flat[2 * local :]
        g_qkv, g_proj = call(
            unpack_kernel,
            [shape((3, width, local), F32), shape((local, width), F32)],
            (meta, part, hop(part, steps[0])),
            3,
            "unpack",
            scalars=1,
        )
        return output, grad_tokens, rows, g_qkv, g_qvb, g_proj, g_fc1b

    def none(operands):
        return jax.tree.map(lambda v: jnp.zeros(v.shape, v.dtype), jax.eval_shape(rest, operands))

    output, grad_tokens, rows, g_qkv, g_qvb, g_proj, g_fc1b = lax.cond(
        jnp.max(crop_lengths) < 65536, rest, none, operands
    )
    return (
        output,
        grad_tokens,
        rows[0],
        rows[1],
        rows[2],
        g_qkv,
        g_qvb,
        g_proj,
        rows[6],
        rows[5],
        rows[3],
        rows[4],
        sum_fc1.astype(F32),
        g_fc1b,
        sum_fc2.astype(F32),
        rows[7],
        rows[8],
    )


def solution(mesh):
    rows = P(("wide", "narrow"), None)
    return jax.shard_map(
        shards,
        mesh=mesh,
        in_specs=(
            rows,
            P(("wide", "narrow")),
            P("wide"),
            P("wide"),
            P(),
            P(),
            P(),
            P(None, None, "narrow"),
            P(None, "narrow"),
            P("narrow", None),
            P(),
            P(),
            P(),
            P(),
            P(None, "narrow"),
            P("narrow"),
            P("narrow", None),
            P(),
            P(),
            rows,
        ),
        out_specs=(
            rows,
            rows,
            P(),
            P(),
            P(),
            P(None, None, "narrow"),
            P(None, "narrow"),
            P("narrow", None),
            P(),
            P(),
            P(),
            P(),
            P(None, "narrow"),
            P("narrow"),
            P("narrow", None),
            P(),
            P(),
        ),
        check_vma=False,
    )
```

time: 365 us -> 269 us (0.74)
  blocking collectives: 121 us -> 0 us
  waiting for transfers between devices: 85.8 us -> 125 us
  Pallas kernels: 99.1 us -> 66.6 us
  starting transfers between devices: 13.7 us -> 25.9 us
  other arithmetic: 18.9 us -> 24.5 us
    psum x2 -> x0, blocking collectives: 121 us -> none  [the longest x1 83.4 us: shards(): g_qvb, g_fc1b = lax.psum((g_qvb, g_fc1b), 'wide')]
    ppermute x0 -> x14, waiting for transfers between devices: none -> 56.2 us  [the longest x13 56.2 us: hop(): return lax.ppermute(value, 'wide', pairs)]
    psum x1, waiting for transfers between devices: 26 us -> 0.02 us  [shards(): sum_fc1, sum_fc2 = lax.psum((g_fc1, g_fc2), 'wide')]
    pallas_call x12 -> x14, Pallas kernels: 88.6 us -> 66.6 us  [call(): pl.pallas_call(kernel, out_shape=out_shape, grid_spec=spec, compiler_para...]
    ppermute x0 -> x14, starting transfers between devices: none -> 14.3 us  [the longest x13 14.2 us: hop(): return lax.ppermute(value, 'wide', pairs)]
    pallas_call x1 -> x0, Pallas kernels: 10.4 us -> none  [feed_grads(): pl.pallas_call(feed_grad_kernel, grid=(units // tile,), in_specs=[whole,...]
    ppermute x8, waiting for transfers between devices: 59.9 us -> 69 us  [shards(): swap = lambda v: lax.ppermute(v, 'narrow', SWAP)]
    dynamic_slice x0 -> x5, local copies, waits for them, and re-layouts: none -> 3.87 us  [the longest x4 2.88 us: halve(): give = lax.dynamic_slice_in_dim(part, (1 - high) * rows, rows)]
  transfers between devices with their start and end apart: 9 -> 23, of which waited for: 6 -> 17; matrix products, arithmetic and copies ran while one was open for 3% -> 7% of each run, Pallas kernels for 13% -> 22%
where the time goes in v2:
time: 269 us; the launch traced here: 268 us
  waiting for transfers between devices  125 us (46%)
  Pallas kernels  66.6 us (25%)
  starting transfers between devices  25.9 us (10%)
  other arithmetic  24.5 us (9%)
  between operations  15.2 us (6%)
  local copies, waits for them, and re-layouts  10.2 us (4%)
    ppermute x8, waiting for transfers between devices, shards(): swap = lambda v: lax.ppermute(v, 'narrow', SWAP)  69 us
    pallas_call x14, Pallas kernels, call(): pl.pallas_call(kernel, out_shape=out_shape, grid_spec=spec, compiler_para...  66.6 us
    ppermute x13, waiting for transfers between devices, hop(): return lax.ppermute(value, 'wide', pairs)  56.2 us
    ppermute x13, starting transfers between devices, hop(): return lax.ppermute(value, 'wide', pairs)  14.2 us
    ppermute x8, starting transfers between devices, shards(): swap = lambda v: lax.ppermute(v, 'narrow', SWAP)  11.6 us
  transfers between devices with their start and end apart: 23, of which 17 were waited for; matrix products, arithmetic and copies ran while one was open for 7% of the time, Pallas kernels for 22%

profile of v2, /device:TPU:0, one launch (start us, length us, event | category | flops | bytes accessed | tf_op | source)
XLA Modules:
  0.0 268.1 jit_solution(8615241200264866457)
XLA Ops:
  10.2 3.0 %collective-permute-start.16 = (bf16[512,768]{1,0:T(8,128)(2,1)}, bf16[512,768]{1,0:T(8,128)(2,1)S(1)}, u32[]{:S(2)}, u32[]{:S(2)}) collective-permute-start(bf16[512,768]{1,0:T(8,128)(2,1)} %broadcast_select_fusion.1.x_ref), channel_id=1, source_target_pairs={{0,1},{1,0},{2,3},{3,2},{4,5},{5,4},{6,7},{7,6},{8,9},{9,8},{10,11... | collective-permute-start | bytes 2359304 | tf_op jit(solution)/shard_map/ppermute | solution.py:583
  14.5 4.1 %norm_qkv.2 = (bf16[512,768]{1,0:T(8,128)(2,1)}, bf16[3,3,512,128]{3,2,1,0:T(8,128)(2,1)S(1)}) custom-call(bf16[512,768]{1,0:T(8,128)(2,1)} %broadcast_select_fusion.1.x_ref, f32[8,768]{1,0:T(8,128)S(1)} %convert_element_type.91.vec_ref, f32[3,384]{1,0:T(4,128)S(1)} %maximum_convert_fusion.bias_ref, bf16[3,768,384]{2,1,0:T(8,128)(2,1)} %w_ref.3), custom_call_target="tpu_custom_call" | custom-call | flops 2000000000 | bytes 1000 | tf_op jit(solution)/shard_map/norm_qkv/pallas_call | solution.py:66
  23.2 8.5 %collective-permute-done.16.x_ref = bf16[512,768]{1,0:T(8,128)(2,1)S(1)} collective-permute-done((bf16[512,768]{1,0:T(8,128)(2,1)}, bf16[512,768]{1,0:T(8,128)(2,1)S(1)}, u32[]{:S(2)}, u32[]{:S(2)}) %collective-permute-start.16) | collective-permute-done | bytes 786464 | tf_op jit(solution)/shard_map/ppermute | solution.py:583
  31.7 3.8 %norm_qkv.3 = (bf16[512,768]{1,0:T(8,128)(2,1)}, bf16[3,3,512,128]{3,2,1,0:T(8,128)(2,1)S(1)}) custom-call(bf16[512,768]{1,0:T(8,128)(2,1)S(1)} %collective-permute-done.16.x_ref, f32[8,768]{1,0:T(8,128)S(1)} %convert_element_type.91.vec_ref, f32[3,384]{1,0:T(4,128)S(1)} %maximum_convert_fusion.bias_ref, bf16[3,768,384]{2,1,0:T(8,128)(2,1)} %w_ref.3), custom_call_target="tpu_custom_call" | custom-call | flops 2000000000 | bytes 1000 | tf_op jit(solution)/shard_map/norm_qkv/pallas_call | solution.py:66
  35.6 4.6 %attention.1 = (bf16[2,512,384]{2,1,0:T(8,128)(2,1)S(1)}, bf16[3,3,1280,128]{3,2,1,0:T(8,128)(2,1)}) custom-call(s32[66]{0:T(128)S(1)} %concatenate.27.meta, bf16[3,3,512,128]{3,2,1,0:T(8,128)(2,1)S(1)} %get-tuple-element.173.own_ref, bf16[3,3,512,128]{3,2,1,0:T(8,128)(2,1)S(1)} %get-tuple-element.174.other_ref), custom_call_target="tpu_custom_call" | custom-call | flops 8000000000 | bytes 1000 | tf_op jit(solution)/shard_map/attention/pallas_call | solution.py:66
  40.2 13.9 %collective-permute-done.17.gb_ref.g_other = bf16[512,768]{1,0:T(8,128)(2,1)S(1)} collective-permute-done((bf16[512,768]{1,0:T(8,128)(2,1)}, bf16[512,768]{1,0:T(8,128)(2,1)S(1)}, u32[]{:S(2)}, u32[]{:S(2)}) %collective-permute-start.17) | collective-permute-done | bytes 786464 | tf_op jit(solution)/shard_map/ppermute | solution.py:583
  57.4 15.4 %collective-permute-done.19.theirs_ref = bf16[2,512,384]{2,1,0:T(8,128)(2,1)S(1)} collective-permute-done((bf16[2,512,384]{2,1,0:T(8,128)(2,1)S(1)}, bf16[2,512,384]{2,1,0:T(8,128)(2,1)S(1)}, u32[]{:S(2)}, u32[]{:S(2)}) %collective-permute-start.19) | collective-permute-done | bytes 786464 | tf_op jit(solution)/shard_map/ppermute | solution.py:583
  72.8 7.1 %feed.3 = (bf16[512,768]{1,0:T(8,128)(2,1)S(1)}, bf16[512,1536]{1,0:T(8,128)(2,1)S(1)}, bf16[512,1536]{1,0:T(8,128)(2,1)S(1)}, bf16[512,768]{1,0:T(8,128)(2,1)S(1)}) custom-call(s32[66]{0:T(128)S(1)} %concatenate.27.meta, bf16[2,512,384]{2,1,0:T(8,128)(2,1)S(1)} %get-tuple-element.179.mine_ref, bf16[2,512,384]{2,1,0:T(8,128)(2,1)S(1)} %collective-permute-done.19.theirs_ref, ...), custom_call_target="tpu_custom_call" | custom-call | flops 7000000000 | bytes 1000 | tf_op jit(solution)/shard_map/feed/pallas_call | solution.py:66
  81.4 9.1 %feed.2 = (bf16[512,768]{1,0:T(8,128)(2,1)S(1)}, bf16[512,1536]{1,0:T(8,128)(2,1)S(1)}, bf16[512,1536]{1,0:T(8,128)(2,1)S(1)}, bf16[512,768]{1,0:T(8,128)(2,1)}, f32[512,768]{1,0:T(8,128)S(1)}) custom-call(s32[66]{0:T(128)S(1)} %concatenate.27.meta, bf16[2,512,384]{2,1,0:T(8,128)(2,1)S(1)} %get-tuple-element.179.mine_ref, ...), custom_call_target="tpu_custom_call" | custom-call | flops 7000000000 | bytes 1000 | tf_op jit(solution)/shard_map/feed/pallas_call | solution.py:66
  90.5 7.4 %feed_grads.1 = (bf16[768,1536]{1,0:T(8,128)(2,1)}, bf16[1536,768]{1,0:T(8,128)(2,1)}, f32[1,1536]{1,0:T(1,128)S(1)}) custom-call(bf16[512,768]{1,0:T(8,128)(2,1)S(1)} %get-tuple-element.185.n_own, bf16[512,768]{1,0:T(8,128)(2,1)S(1)} %get-tuple-element.186.n_other, bf16[512,1536]{1,0:T(8,128)(2,1)S(1)} %get-tuple-element.187.a_own, ...), custom_call_target="tpu_custom_call" | custom-call | flops 8000000000 | bytes 1000 | tf_op jit(solution)/shard_map/feed_grads/pallas_call | solution.py:66
  100.0 153.8 %conditional.1 = (bf16[512,768]{1,0:T(8,128)(2,1)}, f32[512,768]{1,0:T(8,128)}, f32[9,768]{1,0:T(8,128)}, f32[3,768,384]{2,1,0:T(8,128)}, f32[2,384]{1,0:T(2,128...) conditional(s32[]{:T(128)} %convert_element_type.90, () %tuple.28, ...), branch_computations={%region_3.4_spmd, %region_4.7_spmd} | conditional | flops 30019661824 | bytes 167305024 | solution.py:753
  100.0 4.3 %middle.1 = (f32[512,768]{1,0:T(8,128)S(1)}, bf16[512,768]{1,0:T(8,128)(2,1)S(1)}, f32[4,768]{1,0:T(4,128)S(1)}) custom-call(bf16[512,768]{1,0:T(8,128)(2,1)} %get-tuple-element.71.mine_ref, bf16[512,768]{1,0:T(8,128)(2,1)} %get-tuple-element.72.got_ref, f32[512,768]{1,0:T(8,128)S(1)} %get-tuple-element.69.attn_ref, ...), custom_call_target="tpu_custom_call" | custom-call | flops 3000000000 | bytes 1000 | tf_op jit(solution)/shard_map/cond/branch_1_fun/middle/pallas_call | solution.py:66
  109.1 3.9 %branch.2 = f32[512,768]{1,0:T(8,128)S(1)} custom-call(bf16[512,1536]{1,0:T(8,128)(2,1)} %get-tuple-element.76.act_ref, bf16[1536,768]{1,0:T(8,128)(2,1)} %get-tuple-element.77.w2_ref), custom_call_target="tpu_custom_call" | custom-call | flops 2000000000 | bytes 1000 | tf_op jit(solution)/shard_map/cond/branch_1_fun/branch/pallas_call | solution.py:66
  114.2 11.8 %collective-permute-done.other_ref.ga_other = bf16[512,768]{1,0:T(8,128)(2,1)S(1)} collective-permute-done((bf16[512,768]{1,0:T(8,128)(2,1)S(1)}, bf16[512,768]{1,0:T(8,128)(2,1)S(1)}, u32[]{:S(2)}, u32[]{:S(2)}) %collective-permute-start) | collective-permute-done | bytes 786464 | tf_op jit(solution)/shard_map/cond/branch_1_fun/ppermute | solution.py:583
  126.0 6.2 %attention_back.1.grad_ref = bf16[3,3,1280,128]{3,2,1,0:T(8,128)(2,1)S(1)} custom-call(s32[66]{0:T(128)S(1)} %get-tuple-element.79.meta, bf16[3,3,1280,128]{3,2,1,0:T(8,128)(2,1)S(1)} %copy-done.59, bf16[512,768]{1,0:T(8,128)(2,1)S(1)} %get-tuple-element.75.own_ref.ga_own, bf16[512,768]{1,0:T(8,128)(2,1)S(1)} %collective-permute-done.other_ref.ga_other, ...), custom_call_target="tpu_custom_call" | custom-call | flops 8999999488 | bytes 1000 | tf_op jit(solution)/shard_map/cond/branch_1_fun/attention_back/pallas_call | solution.py:66
  132.2 7.3 %collective-permute-done.1 = bf16[512,768]{1,0:T(8,128)(2,1)S(1)} collective-permute-done((bf16[512,768]{1,0:T(8,128)(2,1)S(1)}, bf16[512,768]{1,0:T(8,128)(2,1)S(1)}, u32[]{:S(2)}, u32[]{:S(2)}) %collective-permute-start.1) | collective-permute-done | bytes 786464 | tf_op jit(solution)/shard_map/cond/branch_1_fun/ppermute | solution.py:583
  139.6 3.7 %share.1 = (bf16[512,768]{1,0:T(8,128)(2,1)S(1)}, bf16[512,768]{1,0:T(8,128)(2,1)S(1)}) custom-call(s32[66]{0:T(128)S(1)} %get-tuple-element.79.meta, bf16[3,3,1280,128]{3,2,1,0:T(8,128)(2,1)S(1)} %attention_back.1.grad_ref, bf16[3,768,384]{2,1,0:T(8,128)(2,1)S(1)} %copy-done.50), custom_call_target="tpu_custom_call" | custom-call | flops 3000000000 | bytes 1000 | tf_op jit(solution)/shard_map/cond/branch_1_fun/share/pallas_call | solution.py:66
  143.3 3.8 %weights.1 = (bf16[3072,384]{1,0:T(8,128)(2,1)S(1)}, f32[3,384]{1,0:T(4,128)S(1)}) custom-call(s32[66]{0:T(128)S(1)} %get-tuple-element.79.meta, bf16[3,3,1280,128]{3,2,1,0:T(8,128)(2,1)S(1)} %attention_back.1.grad_ref, bf16[512,768]{1,0:T(8,128)(2,1)S(1)} %copy-done.57, bf16[512,768]{1,0:T(8,128)(2,1)S(1)} %copy-done.58, ...), custom_call_target="tpu_custom_call" | custom-call | flops 5000000000 | bytes 1000 | tf_op jit(solution)/shard_map/cond/branch_1_fun/weights/pallas_call | solution.py:66
  148.3 3.2 %collective-permute-done.2 = bf16[1536,384]{1,0:T(8,128)(2,1)} collective-permute-done((bf16[1536,384]{1,0:T(8,128)(2,1)}, bf16[1536,384]{1,0:T(8,128)(2,1)}, u32[]{:S(2)}, u32[]{:S(2)}) %collective-permute-start.2) | collective-permute-done | bytes 1179680 | tf_op jit(solution)/shard_map/cond/branch_1_fun/ppermute | solution.py:523
  157.8 6.5 %collective-permute-done.3 = bf16[768,384]{1,0:T(8,128)(2,1)} collective-permute-done((bf16[768,384]{1,0:T(8,128)(2,1)}, bf16[768,384]{1,0:T(8,128)(2,1)}, u32[]{:S(2)}, u32[]{:S(2)}) %collective-permute-start.3) | collective-permute-done | bytes 589856 | tf_op jit(solution)/shard_map/cond/branch_1_fun/ppermute | solution.py:523
  165.7 9.3 %collective-permute-done.4.got_ref = bf16[512,768]{1,0:T(8,128)(2,1)} collective-permute-done((bf16[512,768]{1,0:T(8,128)(2,1)S(1)}, bf16[512,768]{1,0:T(8,128)(2,1)}, u32[]{:S(2)}, u32[]{:S(2)}) %collective-permute-start.4) | collective-permute-done | bytes 786464 | tf_op jit(solution)/shard_map/cond/branch_1_fun/ppermute | solution.py:583
  176.3 3.3 %multiply_reduce_fusion = (f32[768]{0:T(1024)S(1)}, bf16[512,768]{1,0:T(8,128)(2,1)}) fusion(bf16[512,768]{1,0:T(8,128)(2,1)S(1)} %copy-done.14, f32[512,768]{1,0:T(8,128)S(1)} %copy-done.1, bf16[512,768]{1,0:T(8,128)(2,1)S(1)} %copy-done.20, f32[768]{0:T(1024)S(1)} %convert_element_type.64, f32[768]{0:T(1024)S(1)} %get-tuple-element.70, ...), kind=kLoop, calls=%fused_computation.1 | loop fusion | flops 5111040 | bytes 6304256 | tf_op jit(solution)/shard_map/cond/branch_1_fun/reduce_sum | solution.py:718
  179.6 3.2 %collective-permute-done.5 = bf16[384,384]{1,0:T(8,128)(2,1)} collective-permute-done((bf16[384,384]{1,0:T(8,128)(2,1)}, bf16[384,384]{1,0:T(8,128)(2,1)}, u32[]{:S(2)}, u32[]{:S(2)}) %collective-permute-start.5) | collective-permute-done | bytes 294944 | tf_op jit(solution)/shard_map/cond/branch_1_fun/ppermute | solution.py:523
  188.1 4.1 %final.1 = (f32[512,768]{1,0:T(8,128)}, f32[3,768]{1,0:T(4,128)S(1)}) custom-call(bf16[512,768]{1,0:T(8,128)(2,1)S(1)} %copy-done.10, bf16[512,768]{1,0:T(8,128)(2,1)} %collective-permute-done.4.got_ref, bf16[512,768]{1,0:T(8,128)(2,1)} %get-tuple-element.67.x_ref, f32[512,768]{1,0:T(8,128)S(1)} %copy-done.8, f32[512,1]{1,0:T(8,128)S(1)} %copy.38.mark_ref, ...), custom_call_target="tpu_custom_call" | custom-call | flops 3000000000 | bytes 1000 | tf_op jit(solution)/shard_map/cond/branch_1_fun/final/pallas_call | solution.py:66
  192.2 4.3 %collective-permute-done.6 = bf16[192,384]{1,0:T(8,128)(2,1)S(1)} collective-permute-done((bf16[192,384]{1,0:T(8,128)(2,1)S(1)}, bf16[192,384]{1,0:T(8,128)(2,1)S(1)}, u32[]{:S(2)}, u32[]{:S(2)}) %collective-permute-start.6) | collective-permute-done | bytes 147488 | tf_op jit(solution)/shard_map/cond/branch_1_fun/ppermute | solution.py:523
  196.8 2.8 %collective-permute-start.8 = (f32[12,768]{1,0:T(8,128)S(1)}, f32[12,768]{1,0:T(8,128)S(1)}, u32[]{:S(2)}, u32[]{:S(2)}) collective-permute-start(f32[12,768]{1,0:T(8,128)S(1)} %concatenate.19), channel_id=1, source_target_pairs={{0,16},{2,18},{4,20},{6,22},{8,24},{10,26},{12,28},{14,30},{16,0},... | collective-permute-start | bytes 110600 | tf_op jit(solution)/shard_map/cond/branch_1_fun/ppermute | solution.py:523
  199.6 11.1 %collective-permute-done.8 = f32[12,768]{1,0:T(8,128)S(1)} collective-permute-done((f32[12,768]{1,0:T(8,128)S(1)}, f32[12,768]{1,0:T(8,128)S(1)}, u32[]{:S(2)}, u32[]{:S(2)}) %collective-permute-start.8) | collective-permute-done | bytes 36896 | tf_op jit(solution)/shard_map/cond/branch_1_fun/ppermute | solution.py:523
  212.8 14.6 %collective-permute-done.10 = f32[12,768]{1,0:T(8,128)S(1)} collective-permute-done((f32[12,768]{1,0:T(8,128)S(1)}, f32[12,768]{1,0:T(8,128)S(1)}, u32[]{:S(2)}, u32[]{:S(2)}) %collective-permute-start.10) | collective-permute-done | bytes 36896 | tf_op jit(solution)/shard_map/cond/branch_1_fun/ppermute | solution.py:523
  229.4 8.2 %collective-permute-done.14 = bf16[768,384]{1,0:T(8,128)(2,1)S(1)} collective-permute-done((bf16[768,384]{1,0:T(8,128)(2,1)S(1)}, bf16[768,384]{1,0:T(8,128)(2,1)S(1)}, u32[]{:S(2)}, u32[]{:S(2)}) %collective-permute-start.14) | collective-permute-done | bytes 589856 | tf_op jit(solution)/shard_map/cond/branch_1_fun/ppermute | solution.py:523
  245.8 2.7 %collective-permute-done.13 = f32[9,768]{1,0:T(8,128)S(1)} collective-permute-done((f32[9,768]{1,0:T(8,128)S(1)}, f32[9,768]{1,0:T(8,128)S(1)}, u32[]{:S(2)}, u32[]{:S(2)}) %collective-permute-start.13) | collective-permute-done | bytes 27680 | tf_op jit(solution)/shard_map/cond/branch_1_fun/ppermute | solution.py:583
  250.8 3.0 %unpack.1 = (f32[3,768,384]{2,1,0:T(8,128)}, f32[384,768]{1,0:T(8,128)}) custom-call(s32[66]{0:T(128)S(1)} %copy-done.47, bf16[1536,384]{1,0:T(8,128)(2,1)S(1)} %maximum_select_fusion.mine_ref, bf16[1536,384]{1,0:T(8,128)(2,1)S(1)} %collective-permute-done.15.got_ref), custom_call_target="tpu_custom_call" | custom-call | flops 3000000000 | bytes 1000 | tf_op jit(solution)/shard_map/cond/branch_1_fun/unpack/pallas_call | solution.py:66
  253.9 4.6 %convert_element_type.97 = f32[768,1536]{1,0:T(8,128)} convert(bf16[768,1536]{1,0:T(8,128)(2,1)} %get-tuple-element.217) | non-fusion elementwise | flops 1179648 | bytes 7077888 | tf_op jit(solution)/shard_map/convert_element_type | solution.py:769
  (211 shorter events, 53.7 us)
Async XLA Ops:
  7.3 246.6 %all-reduce.3.cloned.1.call-start = ((), (), s32[]{:S(2)}) async-start(), calls=%async_computation | async-start | bytes 9437184 | tf_op jit(solution)/shard_map/psum | solution.py:657
  10.2 21.5 %collective-permute-start.16 = (bf16[512,768]{1,0:T(8,128)(2,1)}, bf16[512,768]{1,0:T(8,128)(2,1)S(1)}, u32[]{:S(2)}, u32[]{:S(2)}) collective-permute-start(bf16[512,768]{1,0:T(8,128)(2,1)} %broadcast_select_fusion.1.x_ref), channel_id=1, source_target_pairs={{0,1},{1,0},{2,3},{3,2},{4,5},{5,4},{6,7},{7,6},{8,9},{9,8},{10,11... | collective-permute-start | bytes 2359304 | tf_op jit(solution)/shard_map/ppermute | solution.py:583
  21.1 19.1 %collective-permute-start.18 = (bf16[384,384]{1,0:T(8,128)(2,1)S(1)}, bf16[384,384]{1,0:T(8,128)(2,1)S(1)}, u32[]{:S(2)}, u32[]{:S(2)}) collective-permute-start(bf16[384,384]{1,0:T(8,128)(2,1)S(1)} %constant_dynamic-slice_fusion.4), channel_id=1, source_target_pairs={{0,1},{1,0},{2,3},{3,2},{4,5},{5,4},{6,7},{7,6},{8,9},{9,8},{10,11... | collective-permute-start | bytes 884744 | tf_op jit(solution)/shard_map/ppermute | solution.py:550
  21.1 33.0 %collective-permute-start.17 = (bf16[512,768]{1,0:T(8,128)(2,1)}, bf16[512,768]{1,0:T(8,128)(2,1)S(1)}, u32[]{:S(2)}, u32[]{:S(2)}) collective-permute-start(bf16[512,768]{1,0:T(8,128)(2,1)} %get-tuple-element.177.gb_ref.g_own), channel_id=1, source_target_pairs={{0,1},{1,0},{2,3},{3,2},{4,5},{5,4},{6,7},{7,6},{8,9},{9,8},{10,11... | collective-permute-start | bytes 2359304 | tf_op jit(solution)/shard_map/ppermute | solution.py:583
  35.6 20.3 %copy-start.39 = (bf16[1536]{0:T(1024)(128)(2,1)S(1)}, bf16[1536]{0:T(1024)(128)(2,1)}, u32[]{:S(2)}) copy-start(bf16[1536]{0:T(1024)(128)(2,1)} %param.37) | copy-start | bytes 9220
  35.6 37.3 %copy-start.2 = (bf16[768,1536]{1,0:T(8,128)(2,1)S(1)}, bf16[768,1536]{1,0:T(8,128)(2,1)}, u32[]{:S(2)}) copy-start(bf16[768,1536]{1,0:T(8,128)(2,1)} %w1_ref.3) | copy-start | bytes 7077892
  35.6 37.3 %copy-start.22 = (bf16[384,768]{1,0:T(8,128)(2,1)S(1)}, bf16[384,768]{1,0:T(8,128)(2,1)}, u32[]{:S(2)}) copy-start(bf16[384,768]{1,0:T(8,128)(2,1)} %wp_ref.3) | copy-start | bytes 1769476
  35.6 37.3 %copy-start.48 = (bf16[1536,768]{1,0:T(8,128)(2,1)S(1)}, bf16[1536,768]{1,0:T(8,128)(2,1)}, u32[]{:S(2)}) copy-start(bf16[1536,768]{1,0:T(8,128)(2,1)} %w2_ref.3) | copy-start | bytes 7077892
  40.2 41.2 %copy-start.51 = (bf16[2,512,384]{2,1,0:T(8,128)(2,1)}, bf16[2,512,384]{2,1,0:T(8,128)(2,1)S(1)}, u32[]{:S(2)}) copy-start(bf16[2,512,384]{2,1,0:T(8,128)(2,1)S(1)} %get-tuple-element.179.mine_ref) | copy-start | bytes 2359300
  54.1 18.7 %collective-permute-start.19 = (bf16[2,512,384]{2,1,0:T(8,128)(2,1)S(1)}, bf16[2,512,384]{2,1,0:T(8,128)(2,1)S(1)}, u32[]{:S(2)}, u32[]{:S(2)}) collective-permute-start(bf16[2,512,384]{2,1,0:T(8,128)(2,1)S(1)} %get-tuple-element.179.mine_ref), channel_id=1, source_target_pairs={{0,1},{1,0},{2,3},{3,2},{4,5},{5,4},{6,7},{7,6},{8,9},{9,8},{10,11... | collective-permute-start | bytes 2359304 | tf_op jit(solution)/shard_map/ppermute | solution.py:583
  55.8 1.6 collective-permute-start.20
  55.9 25.6 %copy-start.15 = (bf16[512,768]{1,0:T(8,128)(2,1)S(1)}, bf16[512,768]{1,0:T(8,128)(2,1)}, u32[]{:S(2)}) copy-start(bf16[512,768]{1,0:T(8,128)(2,1)} %get-tuple-element.177.gb_ref.g_own) | copy-start | bytes 2359300
  79.9 18.0 %collective-permute-start.21 = (bf16[512,768]{1,0:T(8,128)(2,1)S(1)}, bf16[512,768]{1,0:T(8,128)(2,1)S(1)}, u32[]{:S(2)}, u32[]{:S(2)}) collective-permute-start(bf16[512,768]{1,0:T(8,128)(2,1)S(1)} %get-tuple-element.184), channel_id=1, source_target_pairs={{0,1},{1,0},{2,3},{3,2},{4,5},{5,4},{6,7},{7,6},{8,9},{9,8},{10,11... | collective-permute-start | bytes 2359304 | tf_op jit(solution)/shard_map/ppermute | solution.py:583
  100.0 43.3 %copy-start.46 = (s32[66]{0:T(128)}, s32[66]{0:T(128)S(1)}, u32[]{:S(2)}) copy-start(s32[66]{0:T(128)S(1)} %get-tuple-element.79.meta) | copy-start | bytes 796 | tf_op jit(solution)/shard_map/cond
  105.5 20.5 %copy-start.3 = (bf16[512,768]{1,0:T(8,128)(2,1)}, bf16[512,768]{1,0:T(8,128)(2,1)S(1)}, u32[]{:S(2)}) copy-start(bf16[512,768]{1,0:T(8,128)(2,1)S(1)} %get-tuple-element.75.own_ref.ga_own) | copy-start | bytes 2359300 | tf_op jit(solution)/shard_map/cond
  105.5 20.5 %collective-permute-start = (bf16[512,768]{1,0:T(8,128)(2,1)S(1)}, bf16[512,768]{1,0:T(8,128)(2,1)S(1)}, u32[]{:S(2)}, u32[]{:S(2)}) collective-permute-start(bf16[512,768]{1,0:T(8,128)(2,1)S(1)} %get-tuple-element.75.own_ref.ga_own), channel_id=1, source_target_pairs={{0,1},{1,0},{2,3},{3,2},{4,5},{5,4},{6,7},{7,6},{8,9},{9,8},{10,11... | collective-permute-start | bytes 2359304 | tf_op jit(solution)/shard_map/cond/branch_1_fun/ppermute | solution.py:583
  108.0 31.5 %collective-permute-start.1 = (bf16[512,768]{1,0:T(8,128)(2,1)S(1)}, bf16[512,768]{1,0:T(8,128)(2,1)S(1)}, u32[]{:S(2)}, u32[]{:S(2)}) collective-permute-start(bf16[512,768]{1,0:T(8,128)(2,1)S(1)} %branch.3), channel_id=1, source_target_pairs={{0,1},{1,0},{2,3},{3,2},{4,5},{5,4},{6,7},{7,6},{8,9},{9,8},{10,11... | collective-permute-start | bytes 2359304 | tf_op jit(solution)/shard_map/cond/branch_1_fun/ppermute | solution.py:583
  148.3 3.2 %collective-permute-start.2 = (bf16[1536,384]{1,0:T(8,128)(2,1)}, bf16[1536,384]{1,0:T(8,128)(2,1)}, u32[]{:S(2)}, u32[]{:S(2)}) collective-permute-start(bf16[1536,384]{1,0:T(8,128)(2,1)} %constant_dynamic-slice_fusion.3), channel_id=1, source_target_pairs={{0,2},{2,0},{4,6},{6,4},{8,10},{10,8},{12,14},{14,12},{16,18},{18,... | collective-permute-start | bytes 3538952 | tf_op jit(solution)/shard_map/cond/branch_1_fun/ppermute | solution.py:523
  154.1 10.2 %collective-permute-start.3 = (bf16[768,384]{1,0:T(8,128)(2,1)}, bf16[768,384]{1,0:T(8,128)(2,1)}, u32[]{:S(2)}, u32[]{:S(2)}) collective-permute-start(bf16[768,384]{1,0:T(8,128)(2,1)} %constant_dynamic-slice_fusion.2), channel_id=1, source_target_pairs={{0,4},{2,10},{4,0},{6,14},{8,12},{10,2},{12,8},{14,6},{16,20},{18,... | collective-permute-start | bytes 1769480 | tf_op jit(solution)/shard_map/cond/branch_1_fun/ppermute | solution.py:523
  155.6 19.5 %collective-permute-start.4 = (bf16[512,768]{1,0:T(8,128)(2,1)S(1)}, bf16[512,768]{1,0:T(8,128)(2,1)}, u32[]{:S(2)}, u32[]{:S(2)}) collective-permute-start(bf16[512,768]{1,0:T(8,128)(2,1)S(1)} %get-tuple-element.95), channel_id=1, source_target_pairs={{0,1},{1,0},{2,3},{3,2},{4,5},{5,4},{6,7},{7,6},{8,9},{9,8},{10,11... | collective-permute-start | bytes 2359304 | tf_op jit(solution)/shard_map/cond/branch_1_fun/ppermute | solution.py:583
  175.8 7.0 %collective-permute-start.5 = (bf16[384,384]{1,0:T(8,128)(2,1)}, bf16[384,384]{1,0:T(8,128)(2,1)}, u32[]{:S(2)}, u32[]{:S(2)}) collective-permute-start(bf16[384,384]{1,0:T(8,128)(2,1)} %constant_dynamic-slice_fusion.1), channel_id=1, source_target_pairs={{0,8},{2,6},{4,12},{6,2},{8,0},{10,14},{12,4},{14,10},{16,24},{18,... | collective-permute-start | bytes 884744 | tf_op jit(solution)/shard_map/cond/branch_1_fun/ppermute | solution.py:523
  184.0 12.5 %collective-permute-start.6 = (bf16[192,384]{1,0:T(8,128)(2,1)S(1)}, bf16[192,384]{1,0:T(8,128)(2,1)S(1)}, u32[]{:S(2)}, u32[]{:S(2)}) collective-permute-start(bf16[192,384]{1,0:T(8,128)(2,1)S(1)} %constant_dynamic-slice_fusion), channel_id=1, source_target_pairs={{0,16},{2,18},{4,20},{6,22},{8,24},{10,26},{12,28},{14,30},{16,0},... | collective-permute-start | bytes 442376 | tf_op jit(solution)/shard_map/cond/branch_1_fun/ppermute | solution.py:523
  196.6 14.1 %collective-permute-start.7 = (bf16[192,384]{1,0:T(8,128)(2,1)S(1)}, bf16[192,384]{1,0:T(8,128)(2,1)S(1)}, u32[]{:S(2)}, u32[]{:S(2)}) collective-permute-start(bf16[192,384]{1,0:T(8,128)(2,1)S(1)} %add_convert_fusion.3), channel_id=1, source_target_pairs={{0,16},{2,18},{4,20},{6,22},{8,24},{10,26},{12,28},{14,30},{16,0},... | collective-permute-start | bytes 442376 | tf_op jit(solution)/shard_map/cond/branch_1_fun/ppermute | solution.py:523
  196.8 13.9 %collective-permute-start.8 = (f32[12,768]{1,0:T(8,128)S(1)}, f32[12,768]{1,0:T(8,128)S(1)}, u32[]{:S(2)}, u32[]{:S(2)}) collective-permute-start(f32[12,768]{1,0:T(8,128)S(1)} %concatenate.19), channel_id=1, source_target_pairs={{0,16},{2,18},{4,20},{6,22},{8,24},{10,26},{12,28},{14,30},{16,0},... | collective-permute-start | bytes 110600 | tf_op jit(solution)/shard_map/cond/branch_1_fun/ppermute | solution.py:523
  210.7 16.7 %collective-permute-start.9 = (bf16[384,384]{1,0:T(8,128)(2,1)S(1)}, bf16[384,384]{1,0:T(8,128)(2,1)S(1)}, u32[]{:S(2)}, u32[]{:S(2)}) collective-permute-start(bf16[384,384]{1,0:T(8,128)(2,1)S(1)} %maximum_select_fusion.2), channel_id=1, source_target_pairs={{0,8},{2,6},{4,12},{6,2},{8,0},{10,14},{12,4},{14,10},{16,24},{18,... | collective-permute-start | bytes 884744 | tf_op jit(solution)/shard_map/cond/branch_1_fun/ppermute | solution.py:523
  210.8 16.6 %collective-permute-start.10 = (f32[12,768]{1,0:T(8,128)S(1)}, f32[12,768]{1,0:T(8,128)S(1)}, u32[]{:S(2)}, u32[]{:S(2)}) collective-permute-start(f32[12,768]{1,0:T(8,128)S(1)} %add.111), channel_id=1, source_target_pairs={{0,8},{2,6},{4,12},{6,2},{8,0},{10,14},{12,4},{14,10},{16,24},{18,... | collective-permute-start | bytes 110600 | tf_op jit(solution)/shard_map/cond/branch_1_fun/ppermute | solution.py:523
  227.6 23.2 %copy-start.47 = (s32[66]{0:T(128)S(1)}, s32[66]{0:T(128)}, u32[]{:S(2)}) copy-start(s32[66]{0:T(128)} %copy-done.46) | copy-start | bytes 796 | tf_op jit(solution)/shard_map/cond
  227.6 9.9 %collective-permute-start.14 = (bf16[768,384]{1,0:T(8,128)(2,1)S(1)}, bf16[768,384]{1,0:T(8,128)(2,1)S(1)}, u32[]{:S(2)}, u32[]{:S(2)}) collective-permute-start(bf16[768,384]{1,0:T(8,128)(2,1)S(1)} %maximum_select_fusion.1), channel_id=1, source_target_pairs={{0,4},{2,10},{4,0},{6,14},{8,12},{10,2},{12,8},{14,6},{16,20},{18,... | collective-permute-start | bytes 1769480 | tf_op jit(solution)/shard_map/cond/branch_1_fun/ppermute | solution.py:523
  238.0 12.8 %collective-permute-start.15 = (bf16[1536,384]{1,0:T(8,128)(2,1)S(1)}, bf16[1536,384]{1,0:T(8,128)(2,1)S(1)}, u32[]{:S(2)}, u32[]{:S(2)}) collective-permute-start(bf16[1536,384]{1,0:T(8,128)(2,1)S(1)} %maximum_select_fusion.mine_ref), channel_id=1, source_target_pairs={{0,2},{2,0},{4,6},{6,4},{8,10},{10,8},{12,14},{14,12},{16,18},{18,... | collective-permute-start | bytes 3538952 | tf_op jit(solution)/shard_map/cond/branch_1_fun/ppermute | solution.py:523
  239.0 4.1 %collective-permute-start.11 = (f32[12,768]{1,0:T(8,128)S(1)}, f32[12,768]{1,0:T(8,128)S(1)}, u32[]{:S(2)}, u32[]{:S(2)}) collective-permute-start(f32[12,768]{1,0:T(8,128)S(1)} %add.112), channel_id=1, source_target_pairs={{0,4},{2,10},{4,0},{6,14},{8,12},{10,2},{12,8},{14,6},{16,20},{18,... | collective-permute-start | bytes 110600 | tf_op jit(solution)/shard_map/cond/branch_1_fun/ppermute | solution.py:523
  243.1 1.3 collective-permute-start.12
  244.4 4.2 %collective-permute-start.13 = (f32[9,768]{1,0:T(8,128)S(1)}, f32[9,768]{1,0:T(8,128)S(1)}, u32[]{:S(2)}, u32[]{:S(2)}) collective-permute-start(f32[9,768]{1,0:T(8,128)S(1)} %bitcast.5), channel_id=1, source_target_pairs={{0,1},{1,0},{2,3},{3,2},{4,5},{5,4},{6,7},{7,6},{8,9},{9,8},{10,11... | collective-permute-start | bytes 82952 | tf_op jit(solution)/shard_map/cond/branch_1_fun/ppermute | solution.py:583
  (51 other events, 337.1 us)
Sparse Core Ops, SparseCore 0:
  99.0 139.9 all-reduce.2

commit v3 on v2

--- a/solution.py
+++ b/solution.py
@@ -77,6 +77,10 @@
     return jax.ShapeDtypeStruct(tuple(dims), kind)
 
 
+def row_of(ref, k):
+    return ref[k : k + 1, :].astype(F32)
+
+
 def over_rows(total, body, carry=0):
     def step(i, carry):
         result = body(pl.ds(pl.multiple_of(i * WINDOW, WINDOW), WINDOW), carry)
@@ -85,21 +89,29 @@
     return lax.fori_loop(0, total // WINDOW, step, carry)
 
 
-def qkv_kernel(x_ref, vec_ref, bias_ref, w_ref, normed_ref, qkv_ref):
+def qkv_kernel(tokens_ref, mark_ref, vec_ref, w_ref, normed_ref, qkv_ref, x_ref):
     pairs = qkv_ref.shape[1]
+    local = pairs * 128
 
     def block(rows, carry):
-        normal, inverse = normed_of(x_ref[rows, :].astype(F32))
-        normed = (normal * vec_ref[0:1, :] + vec_ref[1:2, :]).astype(BF16)
+        x = jnp.where(mark_ref[rows, :] > 0.5, vec_ref[8:9, :], tokens_ref[rows, :])
+        x_ref[rows, :] = x
+        normal, inverse = normed_of(x.astype(F32))
+        normed = (normal * row_of(vec_ref, 0) + row_of(vec_ref, 1)).astype(BF16)
         normed_ref[rows, :] = normed
         for c in range(3):
-            part = (nn(normed, w_ref[c]) + bias_ref[c : c + 1, :]).astype(BF16)
+            part = nn(normed, w_ref[c])
+            if c != 1:
+                start = 0 if c == 0 else local
+                part = part + vec_ref[9:10, start : start + local].astype(F32)
+            part = part.astype(BF16)
             if c == 0:
                 part = part * 0.125
             for p in range(pairs):
                 qkv_ref[c, p, rows, :] = part[:, p * 128 : (p + 1) * 128]
 
-    over_rows(x_ref.shape[0], block)
+    for first in range(0, x_ref.shape[0], WINDOW):
+        block(pl.ds(first, WINDOW), 0)
 
 
 def slot_rows(meta, slot):
@@ -148,7 +160,9 @@
     return result
 
 
-def attention_kernel(slots, meta, own_ref, other_ref, heads_ref, qkv_ref, mixed_ref):
+def attention_kernel(
+    slots, meta, own_ref, other_ref, heads_own_ref, heads_other_ref, qkv_ref, mixed_ref
+):
     pairs = own_ref.shape[1]
     half = own_ref.shape[2]
     total = 2 * half
@@ -198,30 +212,29 @@
 
     walk_groups(meta, slots, small, big)
     for p in range(pairs):
-        heads_ref[0, :, p * 128 : (p + 1) * 128] = mixed_ref[p, pl.ds(first_own, half), :]
-        heads_ref[1, :, p * 128 : (p + 1) * 128] = mixed_ref[p, pl.ds(first_other, half), :]
+        heads_own_ref[:, p * 128 : (p + 1) * 128] = mixed_ref[p, pl.ds(first_own, half), :]
+        heads_other_ref[:, p * 128 : (p + 1) * 128] = mixed_ref[p, pl.ds(first_other, half), :]
 
 
 def attention_back_kernel(
-    slots, meta, qkv_ref, own_ref, other_ref, w_ref, grad_ref, out_ref, sum_ref
+    slots, meta, qkv_ref, own_0, own_1, other_0, other_1, w_ref, grad_ref, out_ref, sum_ref
 ):
     pairs = qkv_ref.shape[1]
-    half = own_ref.shape[0]
+    half = 2 * own_0.shape[0]
     total = 2 * half
     first_own = pl.multiple_of(meta[64], half)
     first_other = pl.multiple_of(half - meta[64], half)
-    for source, first in ((own_ref, first_own), (other_ref, first_other)):
-
-        def project(i, carry):
-            begin = pl.multiple_of(i * WINDOW, WINDOW)
-            part = nt(source[pl.ds(begin, WINDOW), :], w_ref[...]).astype(BF16)
-            for p in range(pairs):
-                out_ref[p, pl.ds(pl.multiple_of(first + begin, WINDOW), WINDOW), :] = part[
-                    :, p * 128 : (p + 1) * 128
-                ]
-            return carry
-
-        lax.fori_loop(0, half // WINDOW, project, 0)
+    for source, first in (
+        (own_0, first_own),
+        (own_1, first_own + WINDOW),
+        (other_0, first_other),
+        (other_1, first_other + WINDOW),
+    ):
+        part = nt(source[...], w_ref[...]).astype(BF16)
+        for p in range(pairs):
+            out_ref[p, pl.ds(pl.multiple_of(first, WINDOW), WINDOW), :] = part[
+                :, p * 128 : (p + 1) * 128
+            ]
     for p in range(pairs):
         out_ref[p, pl.ds(total, WINDOW), :] = jnp.zeros((WINDOW, 128), BF16)
     grad_ref[...] = jnp.zeros(grad_ref.shape, BF16)
@@ -301,7 +314,6 @@
     x_ref,
     gb_ref,
     vec_ref,
-    bias_ref,
     wp_ref,
     wp_first_ref,
     wp_second_ref,
@@ -311,11 +323,11 @@
     act_ref,
     gpre_ref,
     grad_ref,
-    *attn_ref,
+    *more,
 ):
     units = w1_ref.shape[1]
-    step = 512
-    which = 0 if keep_attn else 1
+    step = x_ref.shape[1]
+    sum_ref = more[-1]
     even = meta[65] == 0
     wp_theirs = jnp.concatenate(
         [
@@ -326,28 +338,32 @@
     )
 
     def block(rows, carry):
-        attn = nn(mine_ref[which, rows, :], wp_ref[...])
-        attn = attn + nn(theirs_ref[1 - which, rows, :], wp_theirs)
-        attn = attn + vec_ref[6:7, :]
+        attn = nn(mine_ref[rows, :], wp_ref[...]) + nn(theirs_ref[rows, :], wp_theirs)
+        attn = attn + row_of(vec_ref, 6)
         if keep_attn:
-            attn_ref[0][rows, :] = attn
-        hidden = x_ref[rows, :].astype(F32) + vec_ref[4:5, :] * attn
+            more[0][rows, :] = attn
+        hidden = x_ref[rows, :].astype(F32) + row_of(vec_ref, 4) * attn
         normal, inverse = normed_of(hidden)
-        normed = (normal * vec_ref[2:3, :] + vec_ref[3:4, :]).astype(BF16)
+        normed = (normal * row_of(vec_ref, 2) + row_of(vec_ref, 3)).astype(BF16)
         normed_ref[rows, :] = normed
-        grad = gb_ref[rows, :]
-        total = None
-        for u in range(0, units, step):
-            cols = slice(u, u + step)
-            pre = nn(normed, w1_ref[:, cols]) + bias_ref[0:1, cols]
+        sum_ref[...] = jnp.zeros(sum_ref.shape, F32)
+
+        def chunk(u, carry):
+            cols = pl.ds(pl.multiple_of(u * step, step), step)
+            shift = row_of(vec_ref, 10)
+            for k in range(1, units // step):
+                shift = jnp.where(u == k, row_of(vec_ref, 10 + k), shift)
+            pre = nn(normed_ref[rows, :], w1_ref[:, cols]) + shift
             half_phi = 0.5 * (1.0 + lax.erf(pre * 0.7071067811865476))
             act_ref[rows, cols] = (pre * half_phi).astype(BF16)
             slope = half_phi + pre * (jnp.exp(pre * pre * -0.5) * 0.3989422804014327)
-            gpre = (nt(grad, w2_ref[cols, :]) * slope).astype(BF16)
+            gpre = (nt(gb_ref[rows, :], w2_ref[cols, :]) * slope).astype(BF16)
             gpre_ref[rows, cols] = gpre
-            part = nt(gpre, w1_ref[:, cols])
-            total = part if total is None else total + part
-        grad_ref[rows, :] = total.astype(BF16)
+            sum_ref[...] += nt(gpre, w1_ref[:, cols])
+            return carry
+
+        lax.fori_loop(0, units // step, chunk, 0)
+        grad_ref[rows, :] = sum_ref[...].astype(BF16)
 
     over_rows(x_ref.shape[0], block)
 
@@ -393,25 +409,21 @@
     over_rows(act_ref.shape[0], block)
 
 
-def middle_kernel(mine_ref, got_ref, attn_ref, x_ref, gout_ref, vec_ref, hidden_ref, ga_ref, sum_ref):
-    def block(rows, sums):
-        attn = attn_ref[rows, :]
-        normal, inverse = normed_of(x_ref[rows, :].astype(F32) + vec_ref[4:5, :] * attn)
-        grad = mine_ref[rows, :].astype(F32) + got_ref[rows, :].astype(F32)
-        grad_hidden = gout_ref[rows, :].astype(F32) + norm_back(
-            grad, vec_ref[2:3, :], normal, inverse
-        )
-        hidden_ref[rows, :] = grad_hidden
-        grad_attn = (vec_ref[4:5, :] * grad_hidden).astype(BF16)
-        ga_ref[rows, :] = grad_attn
-        parts = [
-            jnp.sum(v, axis=0, keepdims=True)
-            for v in (grad * normal, grad, grad_hidden * attn, grad_attn.astype(F32))
-        ]
-        return [a + b for a, b in zip(sums, parts)]
-
-    zero = jnp.zeros((1, x_ref.shape[1]), F32)
-    sums = over_rows(x_ref.shape[0], block, [zero] * 4)
+def middle_kernel(
+    begin, mine_ref, got_ref, attn_ref, x_ref, gout_ref, vec_ref, hidden_ref, ga_ref, sum_ref
+):
+    rows = pl.ds(begin, got_ref.shape[0])
+    attn = attn_ref[rows, :]
+    normal, inverse = normed_of(x_ref[rows, :].astype(F32) + row_of(vec_ref, 4) * attn)
+    grad = mine_ref[rows, :].astype(F32) + got_ref[...].astype(F32)
+    grad_hidden = gout_ref[rows, :].astype(F32) + norm_back(grad, row_of(vec_ref, 2), normal, inverse)
+    hidden_ref[...] = grad_hidden
+    grad_attn = (row_of(vec_ref, 4) * grad_hidden).astype(BF16)
+    ga_ref[...] = grad_attn
+    sums = [
+        jnp.sum(v, axis=0, keepdims=True)
+        for v in (grad * normal, grad, grad_hidden * attn, grad_attn.astype(F32))
+    ]
     for k in range(4):
         sum_ref[k : k + 1, :] = sums[k]
 
@@ -434,67 +446,69 @@
 
 
 def weight_kernel(
-    meta, grad_ref, n_own, n_other, mine_ref, ga_own, ga_other, out_ref, bias_ref
+    meta, grad_ref, n_own, n_other, h_own, h_other, g_0, g_1, g_2, g_3, keep_ref, give_ref, bias_ref
 ):
     pairs = grad_ref.shape[1]
-    width = n_own.shape[1]
+    half = n_own.shape[0]
     local = pairs * 128
-    half = n_own.shape[0]
     own = pl.ds(pl.multiple_of(meta[64], half), half)
     other = pl.ds(pl.multiple_of(half - meta[64], half), half)
+    grads = []
     for c in range(3):
         wide_own = jnp.concatenate([grad_ref[c, p, own, :] for p in range(pairs)], axis=1)
         wide_other = jnp.concatenate([grad_ref[c, p, other, :] for p in range(pairs)], axis=1)
-        out_ref[pl.ds(c * width, width), :] = (
-            tn(n_own[...], wide_own) + tn(n_other[...], wide_other)
-        ).astype(BF16)
         bias_ref[c : c + 1, :] = jnp.sum(wide_own.astype(F32), axis=0, keepdims=True) + jnp.sum(
             wide_other.astype(F32), axis=0, keepdims=True
         )
-    proj = (tn(mine_ref[0], ga_own[...]) + tn(mine_ref[1], ga_other[...])).astype(BF16)
-    for b in range(width // local):
-        out_ref[pl.ds(3 * width + b * local, local), :] = proj[:, b * local : (b + 1) * local]
-
-
-def final_kernel(mine_ref, got_ref, x_ref, hidden_ref, mark_ref, vec_ref, tokens_ref, sum_ref):
-    def block(rows, sums):
+        grads.append((wide_own, wide_other))
+    for k, out_ref in enumerate((keep_ref, give_ref)):
+        half_id = meta[65] if k == 0 else 1 - meta[65]
+        columns = pl.ds(pl.multiple_of(half_id * local, local), local)
+        for c in range(3):
+            part = tn(n_own[:, columns], grads[c][0]) + tn(n_other[:, columns], grads[c][1])
+            out_ref[pl.ds(c * local, local), :] = part.astype(BF16)
+        ga_own = jnp.concatenate([g_0[:, columns], g_1[:, columns]], axis=0)
+        ga_other = jnp.concatenate([g_2[:, columns], g_3[:, columns]], axis=0)
+        part = tn(h_own[...], ga_own) + tn(h_other[...], ga_other)
+        out_ref[pl.ds(3 * local, local), :] = part.astype(BF16)
+
+
+def final_kernel(
+    mine_ref, got_ref, x_ref, hidden_0, hidden_1, mark_ref, vec_ref, tokens_ref, sum_ref
+):
+    sums = [jnp.zeros((1, x_ref.shape[1]), F32)] * 3
+    for k, hidden_ref in enumerate((hidden_0, hidden_1)):
+        rows = pl.ds(k * WINDOW, WINDOW)
         normal, inverse = normed_of(x_ref[rows, :].astype(F32))
         grad = mine_ref[rows, :].astype(F32) + got_ref[rows, :].astype(F32)
-        grad_x = hidden_ref[rows, :] + norm_back(grad, vec_ref[0:1, :], normal, inverse)
+        grad_x = hidden_ref[...] + norm_back(grad, row_of(vec_ref, 0), normal, inverse)
         marked = mark_ref[rows, :] > 0.5
         tokens_ref[rows, :] = jnp.where(marked, 0.0, grad_x)
         parts = [
             jnp.sum(v, axis=0, keepdims=True)
             for v in (jnp.where(marked, grad_x, 0.0), grad * normal, grad)
         ]
-        return [a + b for a, b in zip(sums, parts)]
-
-    zero = jnp.zeros((1, x_ref.shape[1]), F32)
-    sums = over_rows(x_ref.shape[0], block, [zero] * 3)
+        sums = [a + b for a, b in zip(sums, parts)]
     for k in range(3):
         sum_ref[k : k + 1, :] = sums[k]
 
 
-def unpack_kernel(meta, mine_ref, got_ref, qkv_ref, proj_ref):
-    width = qkv_ref.shape[1]
+def unpack_kernel(meta, mine_ref, across_ref, beside_ref, corner_ref, qkv_ref, proj_ref):
     local = qkv_ref.shape[2]
-
-    def write(low_ref, high_ref):
-        qkv_ref[0] = low_ref[:width, :].astype(F32)
-        qkv_ref[1] = low_ref[width:, :].astype(F32)
-        qkv_ref[2] = high_ref[:width, :].astype(F32)
-        for b in range(width // local):
-            proj_ref[:, b * local : (b + 1) * local] = high_ref[
-                width + b * local : width + (b + 1) * local, :
-            ].astype(F32)
-
-    @pl.when(meta[65] == 0)
-    def even():
-        write(mine_ref, got_ref)
-
-    @pl.when(meta[65] != 0)
-    def odd():
-        write(got_ref, mine_ref)
+    pieces = ((mine_ref, 0, 0), (across_ref, 1, 0), (beside_ref, 0, 1), (corner_ref, 1, 1))
+    for ref, core_flip, side_flip in pieces:
+        begin = pl.ds(pl.multiple_of((meta[65] ^ core_flip) * local, local), local)
+        upper = (meta[66] ^ side_flip) == 1
+
+        @pl.when(jnp.logical_not(upper))
+        def first(ref=ref, begin=begin):
+            qkv_ref[0, begin, :] = ref[:local, :].astype(F32)
+            qkv_ref[1, begin, :] = ref[local:, :].astype(F32)
+
+        @pl.when(upper)
+        def second(ref=ref, begin=begin):
+            qkv_ref[2, begin, :] = ref[:local, :].astype(F32)
+            proj_ref[:, begin] = ref[local:, :].astype(F32)
 
 
 def own_validity(lengths, buckets, first_own, own_rows):
@@ -508,39 +522,66 @@
     return jnp.any(inside, axis=1, keepdims=True)
 
 
-def steps_of_wide():
+def chip_bits():
+    return list(range(1, lax.axis_size("wide").bit_length() - 1))
+
+
+def hop(value, flip):
     size = lax.axis_size("wide")
-    bits = list(range(size.bit_length() - 1))
-    even, odd = bits[1:], bits[1:]
-    if len(bits) > 2:
-        odd = [bits[2], bits[1]] + bits[3:]
-    return [(0, 0)] + list(zip(even, odd))
-
-
-def hop(value, step):
-    size = lax.axis_size("wide")
-    pairs = tuple((i, i ^ (1 << step[i % 2])) for i in range(size))
-    return lax.ppermute(value, "wide", pairs)
-
-
-def upper(step):
-    index = lax.axis_index("wide")
-    shift = jnp.where(index % 2 == 0, step[0], step[1])
-    return (index >> shift) % 2
-
-
-def halve(part, step):
-    rows = part.shape[0] // 2
-    high = upper(step)
-    keep = lax.dynamic_slice_in_dim(part, high * rows, rows)
-    give = lax.dynamic_slice_in_dim(part, (1 - high) * rows, rows)
-    return (keep.astype(F32) + hop(give, step).astype(F32)).astype(BF16)
-
-
-def double(part, step):
-    got = hop(part, step)
-    return jnp.where(
-        upper(step) == 0, jnp.concatenate([part, got]), jnp.concatenate([got, part])
+    return lax.ppermute(value, "wide", tuple((i, i ^ flip) for i in range(size)))
+
+
+def bits_at(shift, count=1):
+    return ((lax.axis_index("wide") >> shift) % (1 << count)).astype(jnp.int32)
+
+
+def fold_kernel(parts, place, meta, mine_ref, got_ref, *out_refs):
+    rows = out_refs[0].shape[0]
+    for flip, out_ref in enumerate(out_refs):
+        start = pl.multiple_of((meta[place] ^ flip) * rows, rows)
+        total = mine_ref[pl.ds(start, rows), :].astype(F32) + got_ref[pl.ds(start, rows), :].astype(F32)
+        out_ref[...] = total.astype(BF16)
+
+
+def fold(meta, mine, got, parts, place, index):
+    rows = mine.shape[0] // parts
+    if rows % 32:
+        total = (mine.astype(F32) + got.astype(F32)).astype(BF16)
+        return [
+            lax.dynamic_slice_in_dim(total, (index ^ flip) * rows, rows) for flip in range(parts)
+        ]
+    return call(
+        partial(fold_kernel, parts, place),
+        [shape((rows, mine.shape[1]))] * parts,
+        (meta, mine, got),
+        1,
+        "fold",
+        scalars=1,
+    )
+
+
+def gather_kernel(place, meta, *refs):
+    out_ref = refs[-1]
+    rows = refs[0].shape[0]
+    for flip, ref in enumerate(refs[:-1]):
+        start = pl.multiple_of((meta[place] ^ flip) * rows, rows)
+        out_ref[pl.ds(start, rows), :] = ref[...]
+
+
+def gather(meta, pieces, place, index):
+    rows, columns = pieces[0].shape
+    if rows % 32:
+        total = jnp.zeros((rows * len(pieces), columns), pieces[0].dtype)
+        for flip, piece in enumerate(pieces):
+            total = lax.dynamic_update_slice_in_dim(total, piece, (index ^ flip) * rows, 0)
+        return total
+    return call(
+        partial(gather_kernel, place),
+        shape((rows * len(pieces), columns)),
+        (meta, *pieces),
+        1,
+        "gather",
+        scalars=1,
     )
 
 
@@ -581,10 +622,10 @@
     units = w_fc1.shape[1]
     first_own = (lax.axis_index("narrow") * half).astype(jnp.int32)
     swap = lambda v: lax.ppermute(v, "narrow", SWAP)
-
-    marked = (token_marks == 1)[:, None]
-    x_own = jnp.where(marked, mask_token[None, :], tokens)
-    x_other = swap(x_own)
+    singles = chip_bits()
+
+    tokens_other = swap(tokens)
+    marks_other = swap(token_marks)
     valid = own_validity(crop_lengths, bucket_ids, first_own, half)
     scale2 = scale_mlp.astype(F32)
     gout_own = jnp.where(valid, cotangent, 0).astype(BF16)
@@ -596,80 +637,113 @@
             pad,
             bucket_ids,
             pad,
-            jnp.stack([first_own, (lax.axis_index("wide") % 2).astype(jnp.int32)]),
+            jnp.stack(
+                [first_own, bits_at(0)] + [bits_at(bit) for bit in singles]
+            ),
         ]
     )
-    vec = jnp.stack(
-        [norm1_gain, norm1_bias, norm2_gain, norm2_bias, scale_attn, scale_mlp, proj_bias, fc2_bias]
-    ).astype(F32)
-    bias_q = jnp.stack([qv_bias[0], jnp.zeros_like(qv_bias[0]), qv_bias[1]]).astype(F32)
-    bias_1 = fc1_bias.astype(F32)[None, :]
-    mark_column = marked.astype(F32)
-
-    def qkv(x):
+    table = [
+        norm1_gain,
+        norm1_bias,
+        norm2_gain,
+        norm2_bias,
+        scale_attn,
+        scale_mlp,
+        proj_bias,
+        fc2_bias,
+        mask_token,
+        qv_bias.reshape(width),
+    ] + [fc1_bias[k * width : (k + 1) * width] for k in range(units // width)]
+    lines = lax.broadcasted_iota(jnp.int32, (len(table), width), 0)
+    vec = jnp.zeros((len(table), width), BF16)
+    for k, line in enumerate(table):
+        vec = jnp.where(lines == k, line[None, :], vec)
+
+    def qkv(rows, marks):
         return call(
             qkv_kernel,
-            [shape((half, width)), shape((3, pairs, half, 128))],
-            (x, vec, bias_q, w_qkv),
+            [shape((half, width)), shape((3, pairs, half, 128)), shape((half, width))],
+            (rows, marks, vec, w_qkv),
             2,
             "norm_qkv",
         )
 
-    n_own, qkv_own = qkv(x_own)
+    mark_column = (token_marks == 1).astype(F32)[:, None]
+    n_own, qkv_own, x_own = qkv(tokens, mark_column)
     n_own, gb_start, wp_start = lax.optimization_barrier((n_own, gb_own, w_proj))
     gb_other = swap(gb_start)
     wp_mine = column_half(wp_start)
-    n_other, qkv_other = qkv(x_other)
-    heads, qkv_all = call(
+    n_other, qkv_other, x_other = qkv(tokens_other, (marks_other == 1).astype(F32)[:, None])
+    heads_own, heads_other, qkv_all = call(
         partial(attention_kernel, slots),
-        [shape((2, half, local)), shape((3, pairs, 2 * half + WINDOW, 128))],
+        [shape((half, local)), shape((half, local)), shape((3, pairs, 2 * half + WINDOW, 128))],
         (meta, qkv_own, qkv_other),
         8,
         "attention",
         scratch=[pltpu.VMEM((pairs, 2 * half + WINDOW, 128), BF16)],
         scalars=1,
     )
-    heads, gb_other, wp_mine = lax.optimization_barrier((heads, gb_other, wp_mine))
-    got = swap(heads)
-    wp_next = hop(wp_mine, (0, 0))
-
-    def feed(x, gb, keep):
+    heads_own, heads_other, gb_other, wp_mine = lax.optimization_barrier(
+        (heads_own, heads_other, gb_other, wp_mine)
+    )
+    got_other = swap(heads_own)
+    got_own = swap(heads_other)
+    wp_next = hop(wp_mine, 1)
+
+    def feed(mine, theirs, x, gb, keep):
         outs = [shape((half, width)), shape((half, units)), shape((half, units)), shape((half, width))]
         if keep:
             outs.append(shape((half, width), F32))
         return call(
             partial(feed_kernel, keep),
             outs,
-            (meta, heads, got, x, gb, vec, bias_1, w_proj, wp_mine, wp_next, w_fc1, w_fc2),
+            (meta, mine, theirs, x, gb, vec, w_proj, wp_mine, wp_next, w_fc1, w_fc2),
             7,
             "feed",
+            scratch=[pltpu.VMEM((WINDOW, width), F32)],
             scalars=1,
         )
 
-    n2_other, act_other, gpre_other, gn2_other = feed(x_other, gb_other, False)
-    gn2_got = swap(gn2_other)
-    n2_own, act_own, gpre_own, gn2_own, attn_own = feed(x_own, gb_own, True)
+    n2_other, act_other, gpre_other, gn2_other = feed(
+        heads_other, got_other, x_other, gb_other, False
+    )
+    gn2_got = [swap(gn2_other[:WINDOW]), swap(gn2_other[WINDOW:])]
+    n2_own, act_own, gpre_own, gn2_own, attn_own = feed(
+        heads_own, got_own, x_own, gb_own, True
+    )
+    def middle(k, *arrays):
+        return call(
+            partial(middle_kernel, k * WINDOW),
+            [shape((WINDOW, width), F32), shape((WINDOW, width)), shape((4, width), F32)],
+            (*arrays, vec),
+            2,
+            "middle",
+        )
+
+    hidden_0, ga_own_0, sums_0 = middle(0, gn2_own, gn2_got[0], attn_own, x_own, gout_own)
+    ga_other_0 = swap(ga_own_0)
+    act_own, ga_own_0 = lax.optimization_barrier((act_own, ga_own_0))
     g_fc1, g_fc2, g_fc1b = feed_grads(
         n2_own, n2_other, act_own, act_other, gpre_own, gpre_other, gb_own, gb_other
     )
 
-    gn2_got, g_fc1, g_fc2 = lax.optimization_barrier((gn2_got, g_fc1, g_fc2))
+    gn2_got_1, g_fc1, g_fc2, ga_other_0 = lax.optimization_barrier(
+        (gn2_got[1], g_fc1, g_fc2, ga_other_0)
+    )
     sum_fc1, sum_fc2 = lax.psum((g_fc1, g_fc2), "wide")
 
     operands = (
-        gn2_own, gn2_got, attn_own, x_own, gout_own, gb_own, act_own, act_other, qkv_all, n_own, n_other, heads, g_fc1b
+        gn2_own, gn2_got_1, attn_own, x_own, gout_own, gb_own, act_own, act_other, qkv_all, n_own, n_other,
+        heads_own, heads_other, g_fc1b, hidden_0, ga_own_0, ga_other_0, sums_0
     )
 
     def rest(operands):
-        gn2_own, gn2_got, attn_own, x_own, gout_own, gb_own, act_own, act_other, qkv_all, n_own, n_other, heads, g_fc1b = operands
-        grad_hidden, ga_own, sums2 = call(
-            middle_kernel,
-            [shape((half, width), F32), shape((half, width)), shape((4, width), F32)],
-            (gn2_own, gn2_got, attn_own, x_own, gout_own, vec),
-            3,
-            "middle",
-        )
-        ga_other = swap(ga_own)
+        (
+            gn2_own, gn2_got_1, attn_own, x_own, gout_own, gb_own, act_own, act_other, qkv_all, n_own, n_other, heads_own, heads_other, g_fc1b, hidden_0, ga_own_0, ga_other_0, sums_0
+        ) = operands
+        hidden_1, ga_own_1, sums_1 = middle(1, gn2_own, gn2_got_1, attn_own, x_own, gout_own)
+        ga_other_1 = swap(ga_own_1)
+        sums2 = sums_0 + sums_1
         def branch_of(act, kind):
             return call(
                 branch_kernel, shape((half, width), kind), (act, w_fc2), 2, "branch"
@@ -677,11 +751,12 @@
 
         branch_got = swap(branch_of(act_other, BF16))
         branch_own = branch_of(act_own, F32)
-        ga_other, branch_own = lax.optimization_barrier((ga_other, branch_own))
+        ga_other_1, branch_own = lax.optimization_barrier((ga_other_1, branch_own))
+        ga = (ga_own_0, ga_own_1, ga_other_0, ga_other_1)
         d_qkv = call(
             partial(attention_back_kernel, slots),
             shape((3, pairs, 2 * half + WINDOW, 128)),
-            (meta, qkv_all, ga_own, ga_other, w_proj),
+            (meta, qkv_all, *ga, w_proj),
             9,
             "attention_back",
             scratch=[
@@ -691,6 +766,16 @@
             scalars=1,
         )
         d_qkv, branch_got = lax.optimization_barrier((d_qkv, branch_got))
+        keep, give, d_bias = call(
+            weight_kernel,
+            [shape((2 * width, local)), shape((2 * width, local)), shape((3, local), F32)],
+            (meta, d_qkv, n_own, n_other, heads_own, heads_other, *ga),
+            4,
+            "weights",
+            scalars=1,
+        )
+        d_qkv, keep, give = lax.optimization_barrier((d_qkv, keep, give))
+        got = hop(give, 1)
         gn1_own, gn1_other = call(
             share_kernel,
             [shape((half, width)), shape((half, width))],
@@ -700,58 +785,63 @@
             scalars=1,
         )
         gn1_got = swap(gn1_other)
-        d_qkv, gn1_own = lax.optimization_barrier((d_qkv, gn1_own))
-        g_attn, d_bias = call(
-            weight_kernel,
-            [shape((4 * width, local)), shape((3, local), F32)],
-            (meta, d_qkv, n_own, n_other, heads, ga_own, ga_other),
-            5,
-            "weights",
-            scalars=1,
-        )
-        steps = steps_of_wide()
-        part = halve(halve(g_attn, steps[0]), steps[1])
-        part, gn1_got = lax.optimization_barrier((part, gn1_got))
+        got, gn1_own = lax.optimization_barrier((got, gn1_own))
         branch = branch_own + branch_got.astype(F32) + fc2_bias.astype(F32)
         hidden = x_own.astype(F32) + scale_attn.astype(F32) * attn_own
         output = jnp.where(valid, hidden + scale2 * branch, 0.0).astype(BF16)
         g_smlp = jnp.sum(gout_own.astype(F32) * branch, axis=0)
         g_fc2b = jnp.sum(gb_own.astype(F32), axis=0)
+        for k, bit in enumerate(singles):
+            keep, give = fold(meta, keep, got, 2, 66 + k, bits_at(bit))
+            got = hop(give, 1 << bit)
+            if k == 0:
+                got, output, g_smlp, g_fc2b = lax.optimization_barrier((got, output, g_smlp, g_fc2b))
+        keep, gn1_got = lax.optimization_barrier((keep, gn1_got))
         grad_tokens, sums1 = call(
             final_kernel,
             [shape((half, width), F32), shape((3, width), F32)],
-            (gn1_own, gn1_got, x_own, grad_hidden, mark_column, vec),
+            (gn1_own, gn1_got, x_own, hidden_0, hidden_1, mark_column, vec),
             3,
             "final",
         )
+        got, grad_tokens = lax.optimization_barrier((got, grad_tokens))
+        part = (keep.astype(F32) + got.astype(F32)).astype(BF16)
         wide_only = jnp.concatenate([d_bias[0], d_bias[2], g_fc1b[0]]).reshape(-1, width)
         small = jnp.concatenate([sums1, sums2, g_fc2b[None], g_smlp[None], wide_only], axis=0)
-        for step in steps[2:]:
-            part = halve(part, step)
-        for step in reversed(steps[1:]):
+        for k in range(len(singles) - 1, 0, -1):
             part, small = lax.optimization_barrier((part, small))
-            part, small = double(part, step), small + hop(small, step)
-        small = small + hop(small, steps[0])
-        count = 9
-        rows = small[:count] + swap(small[:count])
-        flat = small[count:].reshape(-1)
-        g_qvb = flat[: 2 * local].reshape(2, local)
-        g_fc1b = flat[2 * local :]
-        g_qkv, g_proj = call(
-            unpack_kernel,
-            [shape((3, width, local), F32), shape((local, width), F32)],
-            (meta, part, hop(part, steps[0])),
-            3,
-            "unpack",
-            scalars=1,
-        )
-        return output, grad_tokens, rows, g_qkv, g_qvb, g_proj, g_fc1b
+            pieces = [part, hop(part, 1 << singles[k])]
+            small = small + hop(small, 1 << singles[k])
+            part = gather(meta, pieces, 66 + k, bits_at(singles[k]))
+        return output, grad_tokens, part, small
 
     def none(operands):
         return jax.tree.map(lambda v: jnp.zeros(v.shape, v.dtype), jax.eval_shape(rest, operands))
 
-    output, grad_tokens, rows, g_qkv, g_qvb, g_proj, g_fc1b = lax.cond(
+    output, grad_tokens, part, small = lax.cond(
         jnp.max(crop_lengths) < 65536, rest, none, operands
+    )
+    beside = hop(part, 1 << singles[0])
+    small = small + hop(small, 1 << singles[0])
+    across = hop(part, 1)
+    beside, across, small = lax.optimization_barrier((beside, across, small))
+    corner = hop(beside, 1)
+    small = small + hop(small, 1)
+    corner, small, sum_fc1, sum_fc2 = lax.optimization_barrier(
+        (corner, small, sum_fc1.astype(F32), sum_fc2.astype(F32))
+    )
+    count = 9
+    rows = small[:count] + swap(small[:count])
+    flat = small[count:].reshape(-1)
+    g_qvb = flat[: 2 * local].reshape(2, local)
+    g_fc1b = flat[2 * local :]
+    g_qkv, g_proj = call(
+        unpack_kernel,
+        [shape((3, width, local), F32), shape((local, width), F32)],
+        (meta, part, across, beside, corner),
+        3,
+        "unpack",
+        scalars=1,
     )
     return (
         output,
@@ -766,9 +856,9 @@
         rows[5],
         rows[3],
         rows[4],
-        sum_fc1.astype(F32),
+        sum_fc1,
         g_fc1b,
-        sum_fc2.astype(F32),
+        sum_fc2,
         rows[7],
         rows[8],
     )

time: 269 us -> 256 us (0.952)
  Pallas kernels: 66.6 us -> 84.7 us
  waiting for transfers between devices: 125 us -> 110 us
  other arithmetic: 24.5 us -> 15 us
  starting transfers between devices: 25.9 us -> 20.5 us
    ppermute x8 -> x12, waiting for transfers between devices: 69 us -> 33.1 us  [shards(): swap = lambda v: lax.ppermute(v, 'narrow', SWAP)]
    ppermute x13 -> x14, waiting for transfers between devices: 56.2 us -> 77.2 us  [hop(): lax.ppermute(value, 'wide', tuple(((i, i ^ flip) for i in range(size))))]
    pallas_call x14 -> x20, Pallas kernels: 66.6 us -> 84.7 us  [call(): pl.pallas_call(kernel, out_shape=out_shape, grid_spec=spec, compiler_para...]
    ppermute x13 -> x14, starting transfers between devices: 14.2 us -> 7.89 us  [hop(): lax.ppermute(value, 'wide', tuple(((i, i ^ flip) for i in range(size))))]
    convert_element_type x7 -> x1, other arithmetic: 5.05 us -> 0.04 us  [rest(): part = (keep.astype(F32) + got.astype(F32)).astype(BF16)]
    dynamic_slice x4 -> x0, local copies, waits for them, and re-layouts: 2.88 us -> none  [halve(): give = lax.dynamic_slice_in_dim(part, (1 - high) * rows, rows)]
    ppermute x8 -> x12, starting transfers between devices: 11.6 us -> 10.6 us  [shards(): swap = lambda v: lax.ppermute(v, 'narrow', SWAP)]
  transfers between devices with their start and end apart: 23 -> 28, of which waited for: 17 -> 13; matrix products, arithmetic and copies ran while one was open for 7% -> 7% of each run, Pallas kernels for 22% -> 33%
where the time goes in v3:
time: 256 us; the launch traced here: 257 us
  waiting for transfers between devices  110 us (43%)
  Pallas kernels  84.7 us (33%)
  starting transfers between devices  20.5 us (8%)
  other arithmetic  15 us (6%)
  between operations  15 us (6%)
  local copies, waits for them, and re-layouts  10.6 us (4%)
    pallas_call x20, Pallas kernels, call(): pl.pallas_call(kernel, out_shape=out_shape, grid_spec=spec, compiler_para...  84.7 us
    ppermute x14, waiting for transfers between devices, hop(): lax.ppermute(value, 'wide', tuple(((i, i ^ flip) for i in range(size))))  77.2 us
    ppermute x12, waiting for transfers between devices, shards(): swap = lambda v: lax.ppermute(v, 'narrow', SWAP)  33.1 us
    ppermute x12, starting transfers between devices, shards(): swap = lambda v: lax.ppermute(v, 'narrow', SWAP)  10.6 us
    ppermute x14, starting transfers between devices, hop(): lax.ppermute(value, 'wide', tuple(((i, i ^ flip) for i in range(size))))  7.89 us
  transfers between devices with their start and end apart: 28, of which 13 were waited for; matrix products, arithmetic and copies ran while one was open for 7% of the time, Pallas kernels for 33%

profile of v3, /device:TPU:0, one launch (start us, length us, event | category | flops | bytes accessed | tf_op | source)
XLA Modules:
  0.0 256.6 jit_solution(2007147496496124816)
XLA Ops:
  7.2 3.0 %collective-permute-start.12 = (s32[512]{0:T(512)}, s32[512]{0:T(512)S(1)}, u32[]{:S(2)}, u32[]{:S(2)}) collective-permute-start(s32[512]{0:T(512)} %param.23), channel_id=1, source_target_pairs={{0,1},{1,0},{2,3},{3,2},{4,5},{5,4},{6,7},{7,6},{8,9},{9,8},{10,11... | collective-permute-start | bytes 6152 | tf_op jit(solution)/shard_map/ppermute | solution.py:624
  17.7 3.5 %norm_qkv.2 = (bf16[512,768]{1,0:T(8,128)(2,1)}, bf16[3,3,512,128]{3,2,1,0:T(8,128)(2,1)S(1)}, bf16[512,768]{1,0:T(8,128)(2,1)}) custom-call(bf16[512,768]{1,0:T(8,128)(2,1)S(1)} %copy-done.1, f32[512,1]{1,0:T(8,128)S(1)} %copy.40.mark_ref, bf16[12,768]{1,0:T(8,128)(2,1)S(1)} %select_select_fusion.vec_ref, bf16[3,768,384]{2,1,0:T(8,128)(2,1)} %w_ref.3), custom_call_target="tpu_custom_call" | custom-call | flops 2000000000 | bytes 1000 | tf_op jit(solution)/shard_map/norm_qkv/pallas_call | solution.py:66
  23.4 1.9 collective-permute-start.14
  25.7 5.3 %collective-permute-done.11.tokens_ref = bf16[512,768]{1,0:T(8,128)(2,1)S(1)} collective-permute-done((bf16[512,768]{1,0:T(8,128)(2,1)}, bf16[512,768]{1,0:T(8,128)(2,1)S(1)}, u32[]{:S(2)}, u32[]{:S(2)}) %collective-permute-start.11) | collective-permute-done | bytes 786464 | tf_op jit(solution)/shard_map/ppermute | solution.py:624
  30.9 3.4 %norm_qkv.3 = (bf16[512,768]{1,0:T(8,128)(2,1)}, bf16[3,3,512,128]{3,2,1,0:T(8,128)(2,1)S(1)}, bf16[512,768]{1,0:T(8,128)(2,1)S(1)}) custom-call(bf16[512,768]{1,0:T(8,128)(2,1)S(1)} %collective-permute-done.11.tokens_ref, f32[512,1]{1,0:T(8,128)S(1)} %copy.41.mark_ref, bf16[12,768]{1,0:T(8,128)(2,1)S(1)} %select_select_fusion.vec_ref, ...), custom_call_target="tpu_custom_call" | custom-call | flops 2000000000 | bytes 1000 | tf_op jit(solution)/shard_map/norm_qkv/pallas_call | solution.py:66
  34.4 11.1 %attention.1 = (bf16[512,384]{1,0:T(8,128)(2,1)S(1)}, bf16[512,384]{1,0:T(8,128)(2,1)S(1)}, bf16[3,3,1280,128]{3,2,1,0:T(8,128)(2,1)}) custom-call(s32[69]{0:T(128)S(1)} %concatenate.9.meta, bf16[3,3,512,128]{3,2,1,0:T(8,128)(2,1)S(1)} %get-tuple-element.189.own_ref, bf16[3,3,512,128]{3,2,1,0:T(8,128)(2,1)S(1)} %get-tuple-element.190.other_ref), custom_call_target="tpu_custom_call" | custom-call | flops 8000000000 | bytes 1000 | tf_op jit(solution)/shard_map/attention/pallas_call | solution.py:66
  45.5 7.1 %collective-permute-done.13.gb_ref.g_other = bf16[512,768]{1,0:T(8,128)(2,1)S(1)} collective-permute-done((bf16[512,768]{1,0:T(8,128)(2,1)}, bf16[512,768]{1,0:T(8,128)(2,1)S(1)}, u32[]{:S(2)}, u32[]{:S(2)}) %collective-permute-start.13) | collective-permute-done | bytes 786464 | tf_op jit(solution)/shard_map/ppermute | solution.py:624
  53.0 1.6 collective-permute-start.15
  54.7 10.0 %collective-permute-done.17.theirs_ref = bf16[512,384]{1,0:T(8,128)(2,1)S(1)} collective-permute-done((bf16[512,384]{1,0:T(8,128)(2,1)S(1)}, bf16[512,384]{1,0:T(8,128)(2,1)S(1)}, u32[]{:S(2)}, u32[]{:S(2)}) %collective-permute-start.17) | collective-permute-done | bytes 393248 | tf_op jit(solution)/shard_map/ppermute | solution.py:624
  64.7 7.4 %feed.3 = (bf16[512,768]{1,0:T(8,128)(2,1)S(1)}, bf16[512,1536]{1,0:T(8,128)(2,1)S(1)}, bf16[512,1536]{1,0:T(8,128)(2,1)S(1)}, bf16[512,768]{1,0:T(8,128)(2,1)S(1)}) custom-call(s32[69]{0:T(128)S(1)} %concatenate.9.meta, bf16[512,384]{1,0:T(8,128)(2,1)S(1)} %get-tuple-element.197.mine_ref, bf16[512,384]{1,0:T(8,128)(2,1)S(1)} %collective-permute-done.17.theirs_ref, ...), custom_call_target="tpu_custom_call" | custom-call | flops 7000000000 | bytes 1000 | tf_op jit(solution)/shard_map/feed/pallas_call | solution.py:66
  74.3 7.4 %feed.2 = (bf16[512,768]{1,0:T(8,128)(2,1)S(1)}, bf16[512,1536]{1,0:T(8,128)(2,1)S(1)}, bf16[512,1536]{1,0:T(8,128)(2,1)S(1)}, bf16[512,768]{1,0:T(8,128)(2,1)S(1)}, f32[512,768]{1,0:T(8,128)S(1)}) custom-call(s32[69]{0:T(128)S(1)} %concatenate.9.meta, bf16[512,384]{1,0:T(8,128)(2,1)S(1)} %get-tuple-element.196.mine_ref, ...), custom_call_target="tpu_custom_call" | custom-call | flops 7000000000 | bytes 1000 | tf_op jit(solution)/shard_map/feed/pallas_call | solution.py:66
  81.8 2.5 collective-permute-done.19.got_ref
  84.3 1.8 middle.3
  86.5 7.4 %feed_grads.1 = (bf16[768,1536]{1,0:T(8,128)(2,1)}, bf16[1536,768]{1,0:T(8,128)(2,1)}, f32[1,1536]{1,0:T(1,128)S(1)}) custom-call(bf16[512,768]{1,0:T(8,128)(2,1)S(1)} %get-tuple-element.204.n_own, bf16[512,768]{1,0:T(8,128)(2,1)S(1)} %get-tuple-element.205.n_other, bf16[512,1536]{1,0:T(8,128)(2,1)S(1)} %get-tuple-element.209.a_own, ...), custom_call_target="tpu_custom_call" | custom-call | flops 8000000000 | bytes 1000 | tf_op jit(solution)/shard_map/feed_grads/pallas_call | solution.py:66
  97.9 119.4 %conditional.1 = (bf16[512,768]{1,0:T(8,128)(2,1)}, f32[512,768]{1,0:T(8,128)}, bf16[768,384]{1,0:T(8,128)(2,1)}, f32[12,768]{1,0:T(8,128)S(1)}) conditional(s32[]{:T(128)} %convert_element_type.52, () %tuple.31, (bf16[512,768]{1,0:T(8,128)(2,1)}, bf16[256,768]{1,0:T(8,128)(2,1)}, f32[512,768]{1,0:T(8,128)}, bf16[512,768]{1,0:T(8,128)(2,1)S(1)}, ...), branch_computations={%region_3.4_spmd, %region_4.7_spmd} | conditional | flops 30006214656 | bytes 113245488 | solution.py:821
  98.0 3.3 %middle.2 = (f32[256,768]{1,0:T(8,128)S(1)}, bf16[256,768]{1,0:T(8,128)(2,1)S(1)}, f32[4,768]{1,0:T(4,128)S(1)}) custom-call(bf16[512,768]{1,0:T(8,128)(2,1)} %get-tuple-element.60.mine_ref, bf16[256,768]{1,0:T(8,128)(2,1)} %get-tuple-element.61.got_ref, f32[512,768]{1,0:T(8,128)} %get-tuple-element.62.attn_ref, ...), custom_call_target="tpu_custom_call" | custom-call | flops 2000000000 | bytes 1000 | tf_op jit(solution)/shard_map/cond/branch_1_fun/middle/pallas_call | solution.py:66
  106.5 6.8 %collective-permute-done.other_1.g_3 = bf16[256,768]{1,0:T(8,128)(2,1)S(1)} collective-permute-done((bf16[256,768]{1,0:T(8,128)(2,1)S(1)}, bf16[256,768]{1,0:T(8,128)(2,1)S(1)}, u32[]{:S(2)}, u32[]{:S(2)}) %collective-permute-start) | collective-permute-done | bytes 393248 | tf_op jit(solution)/shard_map/cond/branch_1_fun/ppermute | solution.py:624
  113.4 17.7 %attention_back.1.grad_ref = bf16[3,3,1280,128]{3,2,1,0:T(8,128)(2,1)S(1)} custom-call(s32[69]{0:T(128)S(1)} %get-tuple-element.57.meta, bf16[3,3,1280,128]{3,2,1,0:T(8,128)(2,1)S(1)} %copy-done.45, bf16[256,768]{1,0:T(8,128)(2,1)S(1)} %copy-done.34, bf16[256,768]{1,0:T(8,128)(2,1)S(1)} %get-tuple-element.66.own_1.g_1, bf16[256,768]{1,0:T(8,128)(2,1)S(1)} %copy-done.36, ...), custom_call_target="tpu_custom_call" | custom-call | flops 8999999488 | bytes 1000 | tf_op jit(solution)/shard_map/cond/branch_1_fun/attention_back/pallas_call | solution.py:66
  131.2 4.0 %weights.1 = (bf16[1536,384]{1,0:T(8,128)(2,1)S(1)}, bf16[1536,384]{1,0:T(8,128)(2,1)S(1)}, f32[3,384]{1,0:T(4,128)S(1)}) custom-call(s32[69]{0:T(128)S(1)} %get-tuple-element.57.meta, bf16[3,3,1280,128]{3,2,1,0:T(8,128)(2,1)S(1)} %attention_back.1.grad_ref, bf16[512,768]{1,0:T(8,128)(2,1)S(1)} %copy-done.43, bf16[512,768]{1,0:T(8,128)(2,1)S(1)} %copy-done.44, ...), custom_call_target="tpu_custom_call" | custom-call | flops 4000000000 | bytes 1000 | tf_op jit(solution)/shard_map/cond/branch_1_fun/weights/pallas_call | solution.py:66
  135.3 3.7 %share.1 = (bf16[512,768]{1,0:T(8,128)(2,1)S(1)}, bf16[512,768]{1,0:T(8,128)(2,1)S(1)}) custom-call(s32[69]{0:T(128)S(1)} %get-tuple-element.57.meta, bf16[3,3,1280,128]{3,2,1,0:T(8,128)(2,1)S(1)} %attention_back.1.grad_ref, bf16[3,768,384]{2,1,0:T(8,128)(2,1)S(1)} %copy-done.27), custom_call_target="tpu_custom_call" | custom-call | flops 3000000000 | bytes 1000 | tf_op jit(solution)/shard_map/cond/branch_1_fun/share/pallas_call | solution.py:66
  142.6 17.1 %collective-permute-done.3.got_ref = bf16[768,384]{1,0:T(8,128)(2,1)S(1)} collective-permute-done((bf16[768,384]{1,0:T(8,128)(2,1)S(1)}, bf16[768,384]{1,0:T(8,128)(2,1)S(1)}, u32[]{:S(2)}, u32[]{:S(2)}) %collective-permute-start.3) | collective-permute-done | bytes 589856 | tf_op jit(solution)/shard_map/cond/branch_1_fun/ppermute | solution.py:531
  161.4 11.1 %collective-permute-done.4.got_ref = bf16[384,384]{1,0:T(8,128)(2,1)S(1)} collective-permute-done((bf16[384,384]{1,0:T(8,128)(2,1)S(1)}, bf16[384,384]{1,0:T(8,128)(2,1)S(1)}, u32[]{:S(2)}, u32[]{:S(2)}) %collective-permute-start.4) | collective-permute-done | bytes 294944 | tf_op jit(solution)/shard_map/cond/branch_1_fun/ppermute | solution.py:531
  175.0 2.6 %final.1 = (f32[512,768]{1,0:T(8,128)}, f32[3,768]{1,0:T(4,128)S(1)}) custom-call(bf16[512,768]{1,0:T(8,128)(2,1)S(1)} %copy-done.5, bf16[512,768]{1,0:T(8,128)(2,1)S(1)} %collective-permute-done.6.got_ref, bf16[512,768]{1,0:T(8,128)(2,1)S(1)} %copy-done.16, f32[256,768]{1,0:T(8,128)S(1)} %copy-done.42, f32[256,768]{1,0:T(8,128)S(1)} %get-tuple-element.105.hidden_1, ...), custom_call_target="tpu_custom_call" | custom-call | flops 3000000000 | bytes 1000 | tf_op jit(solution)/shard_map/cond/branch_1_fun/final/pallas_call | solution.py:66
  177.7 6.8 %collective-permute-done.5 = bf16[192,384]{1,0:T(8,128)(2,1)S(1)} collective-permute-done((bf16[192,384]{1,0:T(8,128)(2,1)S(1)}, bf16[192,384]{1,0:T(8,128)(2,1)S(1)}, u32[]{:S(2)}, u32[]{:S(2)}) %collective-permute-start.5) | collective-permute-done | bytes 147488 | tf_op jit(solution)/shard_map/cond/branch_1_fun/ppermute | solution.py:531
  184.7 2.9 %collective-permute-start.8 = (f32[12,768]{1,0:T(8,128)S(1)}, f32[12,768]{1,0:T(8,128)S(1)}, u32[]{:S(2)}, u32[]{:S(2)}) collective-permute-start(f32[12,768]{1,0:T(8,128)S(1)} %concatenate.7), channel_id=1, source_target_pairs={{0,16},{2,18},{4,20},{6,22},{8,24},{10,26},{12,28},{14,30},{16,0},... | collective-permute-start | bytes 110600 | tf_op jit(solution)/shard_map/cond/branch_1_fun/ppermute | solution.py:531
  187.6 9.7 %collective-permute-done.8 = f32[12,768]{1,0:T(8,128)S(1)} collective-permute-done((f32[12,768]{1,0:T(8,128)S(1)}, f32[12,768]{1,0:T(8,128)S(1)}, u32[]{:S(2)}, u32[]{:S(2)}) %collective-permute-start.8) | collective-permute-done | bytes 36896 | tf_op jit(solution)/shard_map/cond/branch_1_fun/ppermute | solution.py:531
  200.0 15.9 %collective-permute-done.10 = f32[12,768]{1,0:T(8,128)S(1)} collective-permute-done((f32[12,768]{1,0:T(8,128)S(1)}, f32[12,768]{1,0:T(8,128)S(1)}, u32[]{:S(2)}, u32[]{:S(2)}) %collective-permute-start.10) | collective-permute-done | bytes 36896 | tf_op jit(solution)/shard_map/cond/branch_1_fun/ppermute | solution.py:531
  217.3 2.0 collective-permute-start.23
  219.3 15.0 %collective-permute-done.23 = f32[12,768]{1,0:T(8,128)S(1)} collective-permute-done((f32[12,768]{1,0:T(8,128)S(1)}, f32[12,768]{1,0:T(8,128)S(1)}, u32[]{:S(2)}, u32[]{:S(2)}) %collective-permute-start.23) | collective-permute-done | bytes 36896 | tf_op jit(solution)/shard_map/ppermute | solution.py:531
  236.5 4.6 %convert_element_type.56 = f32[768,1536]{1,0:T(8,128)} convert(bf16[768,1536]{1,0:T(8,128)(2,1)} %get-tuple-element.306) | non-fusion elementwise | flops 1179648 | bytes 7077888 | tf_op jit(solution)/shard_map/convert_element_type | solution.py:831
  241.2 2.5 convert_element_type.57
  243.7 4.1 %unpack.1 = (f32[3,768,384]{2,1,0:T(8,128)}, f32[384,768]{1,0:T(8,128)}) custom-call(s32[69]{0:T(128)S(1)} %concatenate.9.meta, bf16[768,384]{1,0:T(8,128)(2,1)} %get-tuple-element.226.mine_ref, bf16[768,384]{1,0:T(8,128)(2,1)S(1)} %collective-permute-done.22.across_ref, bf16[768,384]{1,0:T(8,128)(2,1)S(1)} %collective-permute-done.21.beside_ref, ...), custom_call_target="tpu_custom_call" | custom-call | flops 3000000000 | bytes 1000 | tf_op jit(solution)/shard_map/unpack/pallas_call | solution.py:66
  (188 shorter events, 37.6 us)
Async XLA Ops:
  7.2 229.3 %all-reduce.3.cloned.1.call-start = ((), (), s32[]{:S(2)}) async-start(), calls=%async_computation | async-start | bytes 9437184 | tf_op jit(solution)/shard_map/psum | solution.py:733
  7.2 18.3 %collective-permute-start.12 = (s32[512]{0:T(512)}, s32[512]{0:T(512)S(1)}, u32[]{:S(2)}, u32[]{:S(2)}) collective-permute-start(s32[512]{0:T(512)} %param.23), channel_id=1, source_target_pairs={{0,1},{1,0},{2,3},{3,2},{4,5},{5,4},{6,7},{7,6},{8,9},{9,8},{10,11... | collective-permute-start | bytes 6152 | tf_op jit(solution)/shard_map/ppermute | solution.py:624
  10.3 20.7 %collective-permute-start.11 = (bf16[512,768]{1,0:T(8,128)(2,1)}, bf16[512,768]{1,0:T(8,128)(2,1)S(1)}, u32[]{:S(2)}, u32[]{:S(2)}) collective-permute-start(bf16[512,768]{1,0:T(8,128)(2,1)} %tokens_ref.1), channel_id=1, source_target_pairs={{0,1},{1,0},{2,3},{3,2},{4,5},{5,4},{6,7},{7,6},{8,9},{9,8},{10,11... | collective-permute-start | bytes 2359304 | tf_op jit(solution)/shard_map/ppermute | solution.py:624
  23.4 22.1 %collective-permute-start.14 = (bf16[384,384]{1,0:T(8,128)(2,1)}, bf16[384,384]{1,0:T(8,128)(2,1)S(1)}, u32[]{:S(2)}, u32[]{:S(2)}) collective-permute-start(bf16[384,384]{1,0:T(8,128)(2,1)} %constant_dynamic-slice_fusion), channel_id=1, source_target_pairs={{0,1},{1,0},{2,3},{3,2},{4,5},{5,4},{6,7},{7,6},{8,9},{9,8},{10,11... | collective-permute-start | bytes 884744 | tf_op jit(solution)/shard_map/ppermute | solution.py:591
  25.3 27.3 %collective-permute-start.13 = (bf16[512,768]{1,0:T(8,128)(2,1)}, bf16[512,768]{1,0:T(8,128)(2,1)S(1)}, u32[]{:S(2)}, u32[]{:S(2)}) collective-permute-start(bf16[512,768]{1,0:T(8,128)(2,1)} %get-tuple-element.194.gb_ref.g_own), channel_id=1, source_target_pairs={{0,1},{1,0},{2,3},{3,2},{4,5},{5,4},{6,7},{7,6},{8,9},{9,8},{10,11... | collective-permute-start | bytes 2359304 | tf_op jit(solution)/shard_map/ppermute | solution.py:624
  34.4 30.3 %copy-start = (bf16[768,1536]{1,0:T(8,128)(2,1)S(1)}, bf16[768,1536]{1,0:T(8,128)(2,1)}, u32[]{:S(2)}) copy-start(bf16[768,1536]{1,0:T(8,128)(2,1)} %w1_ref.3) | copy-start | bytes 7077892
  34.4 30.3 %copy-start.19 = (bf16[384,768]{1,0:T(8,128)(2,1)S(1)}, bf16[384,768]{1,0:T(8,128)(2,1)}, u32[]{:S(2)}) copy-start(bf16[384,768]{1,0:T(8,128)(2,1)} %wp_ref.3) | copy-start | bytes 1769476
  34.4 30.3 %copy-start.25 = (bf16[1536,768]{1,0:T(8,128)(2,1)S(1)}, bf16[1536,768]{1,0:T(8,128)(2,1)}, u32[]{:S(2)}) copy-start(bf16[1536,768]{1,0:T(8,128)(2,1)} %w2_ref.3) | copy-start | bytes 7077892
  52.7 12.1 %collective-permute-start.17 = (bf16[512,384]{1,0:T(8,128)(2,1)S(1)}, bf16[512,384]{1,0:T(8,128)(2,1)S(1)}, u32[]{:S(2)}, u32[]{:S(2)}) collective-permute-start(bf16[512,384]{1,0:T(8,128)(2,1)S(1)} %get-tuple-element.196.mine_ref), channel_id=1, source_target_pairs={{0,1},{1,0},{2,3},{3,2},{4,5},{5,4},{6,7},{7,6},{8,9},{9,8},{10,11... | collective-permute-start | bytes 1179656 | tf_op jit(solution)/shard_map/ppermute | solution.py:624
  53.0 1.6 collective-permute-start.16
  53.0 21.3 %collective-permute-start.15 = (bf16[512,384]{1,0:T(8,128)(2,1)S(1)}, bf16[512,384]{1,0:T(8,128)(2,1)S(1)}, u32[]{:S(2)}, u32[]{:S(2)}) collective-permute-start(bf16[512,384]{1,0:T(8,128)(2,1)S(1)} %get-tuple-element.197.mine_ref), channel_id=1, source_target_pairs={{0,1},{1,0},{2,3},{3,2},{4,5},{5,4},{6,7},{7,6},{8,9},{9,8},{10,11... | collective-permute-start | bytes 1179656 | tf_op jit(solution)/shard_map/ppermute | solution.py:624
  72.2 12.1 %collective-permute-start.19 = (bf16[256,768]{1,0:T(8,128)(2,1)S(1)}, bf16[256,768]{1,0:T(8,128)(2,1)S(1)}, u32[]{:S(2)}, u32[]{:S(2)}) collective-permute-start(bf16[256,768]{1,0:T(8,128)(2,1)S(1)} %get-tuple-element.312), channel_id=1, source_target_pairs={{0,1},{1,0},{2,3},{3,2},{4,5},{5,4},{6,7},{7,6},{8,9},{9,8},{10,11... | collective-permute-start | bytes 1179656 | tf_op jit(solution)/shard_map/ppermute | solution.py:624
  72.7 21.2 %collective-permute-start.18 = (bf16[256,768]{1,0:T(8,128)(2,1)S(1)}, bf16[256,768]{1,0:T(8,128)(2,1)S(1)}, u32[]{:S(2)}, u32[]{:S(2)}) collective-permute-start(bf16[256,768]{1,0:T(8,128)(2,1)S(1)} %get-tuple-element.313), channel_id=1, source_target_pairs={{0,1},{1,0},{2,3},{3,2},{4,5},{5,4},{6,7},{7,6},{8,9},{9,8},{10,11... | collective-permute-start | bytes 1179656 | tf_op jit(solution)/shard_map/ppermute | solution.py:624
  86.1 9.9 %collective-permute-start.20 = (bf16[256,768]{1,0:T(8,128)(2,1)S(1)}, bf16[256,768]{1,0:T(8,128)(2,1)S(1)}, u32[]{:S(2)}, u32[]{:S(2)}) collective-permute-start(bf16[256,768]{1,0:T(8,128)(2,1)S(1)} %get-tuple-element.217), channel_id=1, source_target_pairs={{0,1},{1,0},{2,3},{3,2},{4,5},{5,4},{6,7},{7,6},{8,9},{9,8},{10,11... | collective-permute-start | bytes 1179656 | tf_op jit(solution)/shard_map/ppermute | solution.py:624
  97.9 43.0 %copy-start.15 = (bf16[512,768]{1,0:T(8,128)(2,1)}, bf16[512,768]{1,0:T(8,128)(2,1)S(1)}, u32[]{:S(2)}) copy-start(bf16[512,768]{1,0:T(8,128)(2,1)S(1)} %get-tuple-element.63.x_ref) | copy-start | bytes 2359300 | tf_op jit(solution)/shard_map/cond
  101.2 12.1 %collective-permute-start = (bf16[256,768]{1,0:T(8,128)(2,1)S(1)}, bf16[256,768]{1,0:T(8,128)(2,1)S(1)}, u32[]{:S(2)}, u32[]{:S(2)}) collective-permute-start(bf16[256,768]{1,0:T(8,128)(2,1)S(1)} %get-tuple-element.66.own_1.g_1), channel_id=1, source_target_pairs={{0,1},{1,0},{2,3},{3,2},{4,5},{5,4},{6,7},{7,6},{8,9},{9,8},{10,11... | collective-permute-start | bytes 1179656 | tf_op jit(solution)/shard_map/cond/branch_1_fun/ppermute | solution.py:624
  103.6 27.6 %collective-permute-start.1 = (bf16[512,768]{1,0:T(8,128)(2,1)S(1)}, bf16[512,768]{1,0:T(8,128)(2,1)S(1)}, u32[]{:S(2)}, u32[]{:S(2)}) collective-permute-start(bf16[512,768]{1,0:T(8,128)(2,1)S(1)} %branch.3), channel_id=1, source_target_pairs={{0,1},{1,0},{2,3},{3,2},{4,5},{5,4},{6,7},{7,6},{8,9},{9,8},{10,11... | collective-permute-start | bytes 2359304 | tf_op jit(solution)/shard_map/cond/branch_1_fun/ppermute | solution.py:624
  135.2 3.8 %collective-permute-start.2 = (bf16[1536,384]{1,0:T(8,128)(2,1)S(1)}, bf16[1536,384]{1,0:T(8,128)(2,1)S(1)}, u32[]{:S(2)}, u32[]{:S(2)}) collective-permute-start(bf16[1536,384]{1,0:T(8,128)(2,1)S(1)} %get-tuple-element.81), channel_id=1, source_target_pairs={{0,2},{2,0},{4,6},{6,4},{8,10},{10,8},{12,14},{14,12},{16,18},{18,... | collective-permute-start | bytes 3538952 | tf_op jit(solution)/shard_map/cond/branch_1_fun/ppermute | solution.py:531
  139.9 19.8 %collective-permute-start.3 = (bf16[768,384]{1,0:T(8,128)(2,1)S(1)}, bf16[768,384]{1,0:T(8,128)(2,1)S(1)}, u32[]{:S(2)}, u32[]{:S(2)}) collective-permute-start(bf16[768,384]{1,0:T(8,128)(2,1)S(1)} %get-tuple-element.86), channel_id=1, source_target_pairs={{0,4},{2,6},{4,0},{6,2},{8,12},{10,14},{12,8},{14,10},{16,20},{18,... | collective-permute-start | bytes 1769480 | tf_op jit(solution)/shard_map/cond/branch_1_fun/ppermute | solution.py:531
  140.2 34.0 %collective-permute-start.6 = (bf16[512,768]{1,0:T(8,128)(2,1)S(1)}, bf16[512,768]{1,0:T(8,128)(2,1)S(1)}, u32[]{:S(2)}, u32[]{:S(2)}) collective-permute-start(bf16[512,768]{1,0:T(8,128)(2,1)S(1)} %get-tuple-element.102), channel_id=1, source_target_pairs={{0,1},{1,0},{2,3},{3,2},{4,5},{5,4},{6,7},{7,6},{8,9},{9,8},{10,11... | collective-permute-start | bytes 2359304 | tf_op jit(solution)/shard_map/cond/branch_1_fun/ppermute | solution.py:624
  161.1 11.4 %collective-permute-start.4 = (bf16[384,384]{1,0:T(8,128)(2,1)S(1)}, bf16[384,384]{1,0:T(8,128)(2,1)S(1)}, u32[]{:S(2)}, u32[]{:S(2)}) collective-permute-start(bf16[384,384]{1,0:T(8,128)(2,1)S(1)} %get-tuple-element.98), channel_id=1, source_target_pairs={{0,8},{2,10},{4,12},{6,14},{8,0},{10,2},{12,4},{14,6},{16,24},{18,... | collective-permute-start | bytes 884744 | tf_op jit(solution)/shard_map/cond/branch_1_fun/ppermute | solution.py:531
  174.1 10.5 %collective-permute-start.5 = (bf16[192,384]{1,0:T(8,128)(2,1)S(1)}, bf16[192,384]{1,0:T(8,128)(2,1)S(1)}, u32[]{:S(2)}, u32[]{:S(2)}) collective-permute-start(bf16[192,384]{1,0:T(8,128)(2,1)S(1)} %get-tuple-element.99), channel_id=1, source_target_pairs={{0,16},{2,18},{4,20},{6,22},{8,24},{10,26},{12,28},{14,30},{16,0},... | collective-permute-start | bytes 442376 | tf_op jit(solution)/shard_map/cond/branch_1_fun/ppermute | solution.py:531
  184.6 12.7 %collective-permute-start.7 = (bf16[192,384]{1,0:T(8,128)(2,1)S(1)}, bf16[192,384]{1,0:T(8,128)(2,1)S(1)}, u32[]{:S(2)}, u32[]{:S(2)}) collective-permute-start(bf16[192,384]{1,0:T(8,128)(2,1)S(1)} %add_convert_fusion.refs_0_), channel_id=1, source_target_pairs={{0,16},{2,18},{4,20},{6,22},{8,24},{10,26},{12,28},{14,30},{16,0},... | collective-permute-start | bytes 442376 | tf_op jit(solution)/shard_map/cond/branch_1_fun/ppermute | solution.py:531
  184.7 12.6 %collective-permute-start.8 = (f32[12,768]{1,0:T(8,128)S(1)}, f32[12,768]{1,0:T(8,128)S(1)}, u32[]{:S(2)}, u32[]{:S(2)}) collective-permute-start(f32[12,768]{1,0:T(8,128)S(1)} %concatenate.7), channel_id=1, source_target_pairs={{0,16},{2,18},{4,20},{6,22},{8,24},{10,26},{12,28},{14,30},{16,0},... | collective-permute-start | bytes 110600 | tf_op jit(solution)/shard_map/cond/branch_1_fun/ppermute | solution.py:531
  197.9 18.0 %collective-permute-start.9 = (bf16[384,384]{1,0:T(8,128)(2,1)S(1)}, bf16[384,384]{1,0:T(8,128)(2,1)S(1)}, u32[]{:S(2)}, u32[]{:S(2)}) collective-permute-start(bf16[384,384]{1,0:T(8,128)(2,1)S(1)} %gather.2.refs_0_), channel_id=1, source_target_pairs={{0,8},{2,10},{4,12},{6,14},{8,0},{10,2},{12,4},{14,6},{16,24},{18,... | collective-permute-start | bytes 884744 | tf_op jit(solution)/shard_map/cond/branch_1_fun/ppermute | solution.py:531
  199.1 16.7 %collective-permute-start.10 = (f32[12,768]{1,0:T(8,128)S(1)}, f32[12,768]{1,0:T(8,128)S(1)}, u32[]{:S(2)}, u32[]{:S(2)}) collective-permute-start(f32[12,768]{1,0:T(8,128)S(1)} %add.64), channel_id=1, source_target_pairs={{0,8},{2,10},{4,12},{6,14},{8,0},{10,2},{12,4},{14,6},{16,24},{18,... | collective-permute-start | bytes 110600 | tf_op jit(solution)/shard_map/cond/branch_1_fun/ppermute | solution.py:531
  217.3 17.0 %collective-permute-start.22 = (bf16[768,384]{1,0:T(8,128)(2,1)}, bf16[768,384]{1,0:T(8,128)(2,1)S(1)}, u32[]{:S(2)}, u32[]{:S(2)}) collective-permute-start(bf16[768,384]{1,0:T(8,128)(2,1)} %get-tuple-element.226.mine_ref), channel_id=1, source_target_pairs={{0,2},{2,0},{4,6},{6,4},{8,10},{10,8},{12,14},{14,12},{16,18},{18,... | collective-permute-start | bytes 1769480 | tf_op jit(solution)/shard_map/ppermute | solution.py:531
  217.3 17.0 %collective-permute-start.21 = (bf16[768,384]{1,0:T(8,128)(2,1)}, bf16[768,384]{1,0:T(8,128)(2,1)S(1)}, u32[]{:S(2)}, u32[]{:S(2)}) collective-permute-start(bf16[768,384]{1,0:T(8,128)(2,1)} %get-tuple-element.226.mine_ref), channel_id=1, source_target_pairs={{0,4},{2,6},{4,0},{6,2},{8,12},{10,14},{12,8},{14,10},{16,20},{18,... | collective-permute-start | bytes 1769480 | tf_op jit(solution)/shard_map/ppermute | solution.py:531
  217.3 17.0 %collective-permute-start.23 = (f32[12,768]{1,0:T(8,128)S(1)}, f32[12,768]{1,0:T(8,128)S(1)}, u32[]{:S(2)}, u32[]{:S(2)}) collective-permute-start(f32[12,768]{1,0:T(8,128)S(1)} %get-tuple-element.227), channel_id=1, source_target_pairs={{0,4},{2,6},{4,0},{6,2},{8,12},{10,14},{12,8},{14,10},{16,20},{18,... | collective-permute-start | bytes 110600 | tf_op jit(solution)/shard_map/ppermute | solution.py:531
  234.3 9.4 %collective-permute-start.24 = (bf16[768,384]{1,0:T(8,128)(2,1)S(1)}, bf16[768,384]{1,0:T(8,128)(2,1)S(1)}, u32[]{:S(2)}, u32[]{:S(2)}) collective-permute-start(bf16[768,384]{1,0:T(8,128)(2,1)S(1)} %collective-permute-done.21.beside_ref), channel_id=1, source_target_pairs={{0,2},{2,0},{4,6},{6,4},{8,10},{10,8},{12,14},{14,12},{16,18},{18,... | collective-permute-start | bytes 1769480 | tf_op jit(solution)/shard_map/ppermute | solution.py:531
  234.4 2.1 collective-permute-start.25
  243.7 5.4 %collective-permute-start.26 = (f32[9,768]{1,0:T(8,128)S(1)}, f32[9,768]{1,0:T(8,128)S(1)}, u32[]{:S(2)}, u32[]{:S(2)}) collective-permute-start(f32[9,768]{1,0:T(8,128)S(1)} %bitcast.8), channel_id=1, source_target_pairs={{0,1},{1,0},{2,3},{3,2},{4,5},{5,4},{6,7},{7,6},{8,9},{9,8},{10,11... | collective-permute-start | bytes 82952 | tf_op jit(solution)/shard_map/ppermute | solution.py:624
  (42 other events, 263.2 us)
Sparse Core Ops, SparseCore 0:
  96.9 135.4 all-reduce.2

commit v4 on v3

--- a/solution.py
+++ b/solution.py
@@ -89,11 +89,11 @@
     return lax.fori_loop(0, total // WINDOW, step, carry)
 
 
-def qkv_kernel(tokens_ref, mark_ref, vec_ref, w_ref, normed_ref, qkv_ref, x_ref):
-    pairs = qkv_ref.shape[1]
-    local = pairs * 128
-
-    def block(rows, carry):
+def project_rows(tokens_ref, mark_ref, vec_ref, w_ref, normed_ref, x_ref, store):
+    local = w_ref.shape[2]
+    count = x_ref.shape[0]
+    for first in range(0, count, count):
+        rows = pl.ds(first, count)
         x = jnp.where(mark_ref[rows, :] > 0.5, vec_ref[8:9, :], tokens_ref[rows, :])
         x_ref[rows, :] = x
         normal, inverse = normed_of(x.astype(F32))
@@ -107,11 +107,15 @@
             part = part.astype(BF16)
             if c == 0:
                 part = part * 0.125
-            for p in range(pairs):
-                qkv_ref[c, p, rows, :] = part[:, p * 128 : (p + 1) * 128]
-
-    for first in range(0, x_ref.shape[0], WINDOW):
-        block(pl.ds(first, WINDOW), 0)
+            for p in range(local // 128):
+                store(c, p, first, part[:, p * 128 : (p + 1) * 128])
+
+
+def qkv_kernel(tokens_ref, mark_ref, vec_ref, w_ref, normed_ref, qkv_ref, x_ref):
+    def store(c, p, first, value):
+        qkv_ref[c, p, pl.ds(first, value.shape[0]), :] = value
+
+    project_rows(tokens_ref, mark_ref, vec_ref, w_ref, normed_ref, x_ref, store)
 
 
 def slot_rows(meta, slot):
@@ -161,17 +165,34 @@
 
 
 def attention_kernel(
-    slots, meta, own_ref, other_ref, heads_own_ref, heads_other_ref, qkv_ref, mixed_ref
+    slots,
+    meta,
+    own_ref,
+    tokens_ref,
+    mark_ref,
+    vec_ref,
+    w_ref,
+    heads_own_ref,
+    heads_other_ref,
+    qkv_ref,
+    normed_ref,
+    x_ref,
+    mixed_ref,
 ):
     pairs = own_ref.shape[1]
     half = own_ref.shape[2]
     total = 2 * half
     first_own = pl.multiple_of(meta[64], half)
     first_other = pl.multiple_of(half - meta[64], half)
+
+    def store(c, p, first, value):
+        begin = pl.multiple_of(first_other + first, WINDOW)
+        qkv_ref[c, p, pl.ds(begin, value.shape[0]), :] = value
+
+    project_rows(tokens_ref, mark_ref, vec_ref, w_ref, normed_ref, x_ref, store)
     for c in range(3):
         for p in range(pairs):
             qkv_ref[c, p, pl.ds(first_own, half), :] = own_ref[c, p]
-            qkv_ref[c, p, pl.ds(first_other, half), :] = other_ref[c, p]
             qkv_ref[c, p, pl.ds(total, WINDOW), :] = jnp.zeros((WINDOW, 128), BF16)
     mixed_ref[...] = jnp.zeros(mixed_ref.shape, BF16)
     low = lax.broadcasted_iota(jnp.int32, (1, 128), 1) < HEAD_DIM
@@ -365,7 +386,7 @@
         lax.fori_loop(0, units // step, chunk, 0)
         grad_ref[rows, :] = sum_ref[...].astype(BF16)
 
-    over_rows(x_ref.shape[0], block)
+    block(pl.ds(0, x_ref.shape[0]), 0)
 
 
 def feed_grad_kernel(
@@ -493,22 +514,20 @@
         sum_ref[k : k + 1, :] = sums[k]
 
 
-def unpack_kernel(meta, mine_ref, across_ref, beside_ref, corner_ref, qkv_ref, proj_ref):
+def unpack_kernel(meta, *refs):
+    qkv_ref, proj_ref = refs[-2:]
     local = qkv_ref.shape[2]
-    pieces = ((mine_ref, 0, 0), (across_ref, 1, 0), (beside_ref, 0, 1), (corner_ref, 1, 1))
-    for ref, core_flip, side_flip in pieces:
-        begin = pl.ds(pl.multiple_of((meta[65] ^ core_flip) * local, local), local)
-        upper = (meta[66] ^ side_flip) == 1
-
-        @pl.when(jnp.logical_not(upper))
-        def first(ref=ref, begin=begin):
-            qkv_ref[0, begin, :] = ref[:local, :].astype(F32)
-            qkv_ref[1, begin, :] = ref[local:, :].astype(F32)
-
-        @pl.when(upper)
+    for k, ref in enumerate(refs[:-2]):
+        begin = pl.ds(pl.multiple_of((meta[65] ^ (k % 2)) * local, local), local)
+        block = (meta[66] ^ (k // 2 % 2)) * 2 + (meta[67] ^ (k // 4))
+
+        @pl.when(block < 3)
+        def first(ref=ref, begin=begin, block=block):
+            qkv_ref[block, begin, :] = ref[...].astype(F32)
+
+        @pl.when(block == 3)
         def second(ref=ref, begin=begin):
-            qkv_ref[2, begin, :] = ref[:local, :].astype(F32)
-            proj_ref[:, begin] = ref[local:, :].astype(F32)
+            proj_ref[:, begin] = ref[...].astype(F32)
 
 
 def own_validity(lengths, buckets, first_own, own_rows):
@@ -585,12 +604,10 @@
     )
 
 
-def column_half(w_proj):
-    columns = w_proj.shape[1] // 2
-    core = lax.axis_index("wide") % 2
-    return lax.ppermute(
-        lax.dynamic_slice_in_dim(w_proj, core * columns, columns, 1), "narrow", SWAP
-    )
+def quarter(w_proj, bit):
+    rows, columns = w_proj.shape[0] // 2, w_proj.shape[1] // 2
+    part = lax.dynamic_slice(w_proj, (bits_at(bit) * rows, bits_at(0) * columns), (rows, columns))
+    return lax.ppermute(part, "narrow", SWAP)
 
 
 def shards(
@@ -670,24 +687,33 @@
 
     mark_column = (token_marks == 1).astype(F32)[:, None]
     n_own, qkv_own, x_own = qkv(tokens, mark_column)
-    n_own, gb_start, wp_start = lax.optimization_barrier((n_own, gb_own, w_proj))
+    n_own, wp_start = lax.optimization_barrier((n_own, w_proj))
+    wp_mine = quarter(wp_start, singles[0])
+    tokens_other, gb_start = lax.optimization_barrier((tokens_other, gb_own))
     gb_other = swap(gb_start)
-    wp_mine = column_half(wp_start)
-    n_other, qkv_other, x_other = qkv(tokens_other, (marks_other == 1).astype(F32)[:, None])
-    heads_own, heads_other, qkv_all = call(
+    heads_own, heads_other, qkv_all, n_other, x_other = call(
         partial(attention_kernel, slots),
-        [shape((half, local)), shape((half, local)), shape((3, pairs, 2 * half + WINDOW, 128))],
-        (meta, qkv_own, qkv_other),
-        8,
+        [
+            shape((half, local)),
+            shape((half, local)),
+            shape((3, pairs, 2 * half + WINDOW, 128)),
+            shape((half, width)),
+            shape((half, width)),
+        ],
+        (meta, qkv_own, tokens_other, (marks_other == 1).astype(F32)[:, None], vec, w_qkv),
+        12,
         "attention",
         scratch=[pltpu.VMEM((pairs, 2 * half + WINDOW, 128), BF16)],
         scalars=1,
     )
-    heads_own, heads_other, gb_other, wp_mine = lax.optimization_barrier(
-        (heads_own, heads_other, gb_other, wp_mine)
+    heads_own, heads_other, wp_mine = lax.optimization_barrier((heads_own, heads_other, wp_mine))
+    wp_side = hop(wp_mine, 1 << singles[0])
+    heads_own, heads_other, gb_other, wp_side = lax.optimization_barrier(
+        (heads_own, heads_other, gb_other, wp_side)
     )
     got_other = swap(heads_own)
     got_own = swap(heads_other)
+    wp_mine = gather(meta, [wp_mine, wp_side], 66, bits_at(singles[0]))
     wp_next = hop(wp_mine, 1)
 
     def feed(mine, theirs, x, gb, keep):
@@ -700,7 +726,7 @@
             (meta, mine, theirs, x, gb, vec, w_proj, wp_mine, wp_next, w_fc1, w_fc2),
             7,
             "feed",
-            scratch=[pltpu.VMEM((WINDOW, width), F32)],
+            scratch=[pltpu.VMEM((half, width), F32)],
             scalars=1,
         )
 
@@ -808,41 +834,44 @@
         part = (keep.astype(F32) + got.astype(F32)).astype(BF16)
         wide_only = jnp.concatenate([d_bias[0], d_bias[2], g_fc1b[0]]).reshape(-1, width)
         small = jnp.concatenate([sums1, sums2, g_fc2b[None], g_smlp[None], wide_only], axis=0)
-        for k in range(len(singles) - 1, 0, -1):
+        for k in range(len(singles) - 1, 1, -1):
             part, small = lax.optimization_barrier((part, small))
             pieces = [part, hop(part, 1 << singles[k])]
             small = small + hop(small, 1 << singles[k])
             part = gather(meta, pieces, 66 + k, bits_at(singles[k]))
-        return output, grad_tokens, part, small
+        part, small = lax.optimization_barrier((part, small))
+        side, near = 1 << singles[0], 1 << singles[1]
+        next_part, beside, across = hop(part, near), hop(part, side), hop(part, 1)
+        small = small + hop(small, near)
+        next_part, beside, across, small = lax.optimization_barrier((next_part, beside, across, small))
+        next_beside, next_across, corner = hop(next_part, side), hop(next_part, 1), hop(beside, 1)
+        small = small + hop(small, side)
+        next_beside, next_across, corner, small = lax.optimization_barrier(
+            (next_beside, next_across, corner, small)
+        )
+        next_corner = hop(next_beside, 1)
+        small = small + hop(small, 1)
+        count = 9
+        rows = small[:count] + swap(small[:count])
+        g_qkv, g_proj = call(
+            unpack_kernel,
+            [shape((3, width, local), F32), shape((local, width), F32)],
+            (meta, part, across, beside, corner, next_part, next_across, next_beside, next_corner),
+            3,
+            "unpack",
+            scalars=1,
+        )
+        return output, grad_tokens, rows, small[count:], g_qkv, g_proj
 
     def none(operands):
         return jax.tree.map(lambda v: jnp.zeros(v.shape, v.dtype), jax.eval_shape(rest, operands))
 
-    output, grad_tokens, part, small = lax.cond(
+    output, grad_tokens, rows, flat, g_qkv, g_proj = lax.cond(
         jnp.max(crop_lengths) < 65536, rest, none, operands
     )
-    beside = hop(part, 1 << singles[0])
-    small = small + hop(small, 1 << singles[0])
-    across = hop(part, 1)
-    beside, across, small = lax.optimization_barrier((beside, across, small))
-    corner = hop(beside, 1)
-    small = small + hop(small, 1)
-    corner, small, sum_fc1, sum_fc2 = lax.optimization_barrier(
-        (corner, small, sum_fc1.astype(F32), sum_fc2.astype(F32))
-    )
-    count = 9
-    rows = small[:count] + swap(small[:count])
-    flat = small[count:].reshape(-1)
+    flat = flat.reshape(-1)
     g_qvb = flat[: 2 * local].reshape(2, local)
     g_fc1b = flat[2 * local :]
-    g_qkv, g_proj = call(
-        unpack_kernel,
-        [shape((3, width, local), F32), shape((local, width), F32)],
-        (meta, part, across, beside, corner),
-        3,
-        "unpack",
-        scalars=1,
-    )
     return (
         output,
         grad_tokens,
@@ -856,9 +885,9 @@
         rows[5],
         rows[3],
         rows[4],
-        sum_fc1,
+        sum_fc1.astype(F32),
         g_fc1b,
-        sum_fc2,
+        sum_fc2.astype(F32),
         rows[7],
         rows[8],
     )

time: 256 us -> 249 us (0.973)
  Pallas kernels: 84.7 us -> 59.9 us
  starting transfers between devices: 20.5 us -> 36 us
    pallas_call x20 -> x19, Pallas kernels: 84.7 us -> 59.9 us  [call(): pl.pallas_call(kernel, out_shape=out_shape, grid_spec=spec, compiler_para...]
    ppermute x14 -> x18, starting transfers between devices: 7.89 us -> 21.8 us  [hop(): lax.ppermute(value, 'wide', tuple(((i, i ^ flip) for i in range(size))))]
    ppermute x12, waiting for transfers between devices: 33.1 us -> 40.7 us  [shards(): swap = lambda v: lax.ppermute(v, 'narrow', SWAP)]
    ppermute x14 -> x18, waiting for transfers between devices: 77.2 us -> 70.7 us  [hop(): lax.ppermute(value, 'wide', tuple(((i, i ^ flip) for i in range(size))))]
    slice x0 -> x2, other arithmetic: none -> 2.87 us  [the longest x1 2.27 us: shards(): rows[8]]
  transfers between devices with their start and end apart: 28 -> 32, of which waited for: 13 -> 16; matrix products, arithmetic and copies ran while one was open for 7% -> 6% of each run, Pallas kernels for 33% -> 24%
where the time goes in v4:
time: 249 us; the launch traced here: 250 us
  waiting for transfers between devices  112 us (45%)
  Pallas kernels  59.9 us (24%)
  starting transfers between devices  36 us (14%)
  other arithmetic  17.4 us (7%)
  between operations  15 us (6%)
  local copies, waits for them, and re-layouts  9.52 us (4%)
    ppermute x18, waiting for transfers between devices, hop(): lax.ppermute(value, 'wide', tuple(((i, i ^ flip) for i in range(size))))  70.7 us
    pallas_call x19, Pallas kernels, call(): pl.pallas_call(kernel, out_shape=out_shape, grid_spec=spec, compiler_para...  59.9 us
    ppermute x12, waiting for transfers between devices, shards(): swap = lambda v: lax.ppermute(v, 'narrow', SWAP)  40.7 us
    ppermute x18, starting transfers between devices, hop(): lax.ppermute(value, 'wide', tuple(((i, i ^ flip) for i in range(size))))  21.8 us
    ppermute x12, starting transfers between devices, shards(): swap = lambda v: lax.ppermute(v, 'narrow', SWAP)  12.1 us
  transfers between devices with their start and end apart: 32, of which 16 were waited for; matrix products, arithmetic and copies ran while one was open for 6% of the time, Pallas kernels for 24%

profile of v4, /device:TPU:0, one launch (start us, length us, event | category | flops | bytes accessed | tf_op | source)
XLA Modules:
  0.0 250.0 jit_solution(14710315789148413923)
XLA Ops:
  7.2 3.0 %collective-permute-start.21 = (s32[512]{0:T(512)}, s32[512]{0:T(512)S(1)}, u32[]{:S(2)}, u32[]{:S(2)}) collective-permute-start(s32[512]{0:T(512)} %param.23), channel_id=1, source_target_pairs={{0,1},{1,0},{2,3},{3,2},{4,5},{5,4},{6,7},{7,6},{8,9},{9,8},{10,11... | collective-permute-start | bytes 6152 | tf_op jit(solution)/shard_map/ppermute | solution.py:641
  14.8 3.6 %norm_qkv.1 = (bf16[512,768]{1,0:T(8,128)(2,1)}, bf16[3,3,512,128]{3,2,1,0:T(8,128)(2,1)S(1)}, bf16[512,768]{1,0:T(8,128)(2,1)}) custom-call(bf16[512,768]{1,0:T(8,128)(2,1)S(1)} %copy-done.1, f32[512,1]{1,0:T(8,128)S(1)} %copy.40.mark_ref, bf16[12,768]{1,0:T(8,128)(2,1)S(1)} %select_select_fusion.vec_ref, bf16[3,768,384]{2,1,0:T(8,128)(2,1)} %w_ref.3), custom_call_target="tpu_custom_call" | custom-call | flops 2000000000 | bytes 1000 | tf_op jit(solution)/shard_map/norm_qkv/pallas_call | solution.py:66
  22.3 2.3 multiply_convert_fusion
  24.9 6.1 %collective-permute-done.20.tokens_ref = bf16[512,768]{1,0:T(8,128)(2,1)S(1)} collective-permute-done((bf16[512,768]{1,0:T(8,128)(2,1)}, bf16[512,768]{1,0:T(8,128)(2,1)S(1)}, u32[]{:S(2)}, u32[]{:S(2)}) %collective-permute-start.20) | collective-permute-done | bytes 786464 | tf_op jit(solution)/shard_map/ppermute | solution.py:641
  31.0 7.6 %attention.1 = (bf16[512,384]{1,0:T(8,128)(2,1)S(1)}, bf16[512,384]{1,0:T(8,128)(2,1)S(1)}, bf16[3,3,1280,128]{3,2,1,0:T(8,128)(2,1)}, bf16[512,768]{1,0:T(8,128)(2,1)}, bf16[512,768]{1,0:T(8,128)(2,1)S(1)}) custom-call(s32[69]{0:T(128)S(1)} %concatenate.9.meta, bf16[3,3,512,128]{3,2,1,0:T(8,128)(2,1)S(1)} %get-tuple-element.226.own_ref, ...), custom_call_target="tpu_custom_call" | custom-call | flops 12000000000 | bytes 1000 | tf_op jit(solution)/shard_map/attention/pallas_call | solution.py:66
  40.6 3.2 %collective-permute-done.24.refs_1_ = bf16[192,384]{1,0:T(8,128)(2,1)S(1)} collective-permute-done((bf16[192,384]{1,0:T(8,128)(2,1)S(1)}, bf16[192,384]{1,0:T(8,128)(2,1)S(1)}, u32[]{:S(2)}, u32[]{:S(2)}) %collective-permute-start.24) | collective-permute-done | bytes 147488 | tf_op jit(solution)/shard_map/ppermute | solution.py:550
  43.8 5.7 %collective-permute-done.23.gb_ref.g_other = bf16[512,768]{1,0:T(8,128)(2,1)S(1)} collective-permute-done((bf16[512,768]{1,0:T(8,128)(2,1)}, bf16[512,768]{1,0:T(8,128)(2,1)S(1)}, u32[]{:S(2)}, u32[]{:S(2)}) %collective-permute-start.23) | collective-permute-done | bytes 786464 | tf_op jit(solution)/shard_map/ppermute | solution.py:641
  52.2 9.3 %collective-permute-done.27.theirs_ref = bf16[512,384]{1,0:T(8,128)(2,1)S(1)} collective-permute-done((bf16[512,384]{1,0:T(8,128)(2,1)S(1)}, bf16[512,384]{1,0:T(8,128)(2,1)S(1)}, u32[]{:S(2)}, u32[]{:S(2)}) %collective-permute-start.27) | collective-permute-done | bytes 393248 | tf_op jit(solution)/shard_map/ppermute | solution.py:641
  61.6 6.5 %feed.3 = (bf16[512,768]{1,0:T(8,128)(2,1)S(1)}, bf16[512,1536]{1,0:T(8,128)(2,1)S(1)}, bf16[512,1536]{1,0:T(8,128)(2,1)S(1)}, bf16[512,768]{1,0:T(8,128)(2,1)S(1)}) custom-call(s32[69]{0:T(128)S(1)} %concatenate.9.meta, bf16[512,384]{1,0:T(8,128)(2,1)S(1)} %get-tuple-element.237.mine_ref, bf16[512,384]{1,0:T(8,128)(2,1)S(1)} %collective-permute-done.27.theirs_ref, ...), custom_call_target="tpu_custom_call" | custom-call | flops 7000000000 | bytes 1000 | tf_op jit(solution)/shard_map/feed/pallas_call | solution.py:66
  70.3 6.5 %feed.2 = (bf16[512,768]{1,0:T(8,128)(2,1)S(1)}, bf16[512,1536]{1,0:T(8,128)(2,1)S(1)}, bf16[512,1536]{1,0:T(8,128)(2,1)S(1)}, bf16[512,768]{1,0:T(8,128)(2,1)S(1)}, f32[512,768]{1,0:T(8,128)S(1)}) custom-call(s32[69]{0:T(128)S(1)} %concatenate.9.meta, bf16[512,384]{1,0:T(8,128)(2,1)S(1)} %get-tuple-element.236.mine_ref, ...), custom_call_target="tpu_custom_call" | custom-call | flops 7000000000 | bytes 1000 | tf_op jit(solution)/shard_map/feed/pallas_call | solution.py:66
  76.9 3.4 %collective-permute-done.29.got_ref = bf16[256,768]{1,0:T(8,128)(2,1)S(1)} collective-permute-done((bf16[256,768]{1,0:T(8,128)(2,1)S(1)}, bf16[256,768]{1,0:T(8,128)(2,1)S(1)}, u32[]{:S(2)}, u32[]{:S(2)}) %collective-permute-start.29) | collective-permute-done | bytes 393248 | tf_op jit(solution)/shard_map/ppermute | solution.py:641
  82.4 7.4 %feed_grads.1 = (bf16[768,1536]{1,0:T(8,128)(2,1)}, bf16[1536,768]{1,0:T(8,128)(2,1)}, f32[1,1536]{1,0:T(1,128)S(1)}) custom-call(bf16[512,768]{1,0:T(8,128)(2,1)S(1)} %get-tuple-element.244.n_own, bf16[512,768]{1,0:T(8,128)(2,1)S(1)} %get-tuple-element.245.n_other, bf16[512,1536]{1,0:T(8,128)(2,1)S(1)} %get-tuple-element.249.a_own, ...), custom_call_target="tpu_custom_call" | custom-call | flops 8000000000 | bytes 1000 | tf_op jit(solution)/shard_map/feed_grads/pallas_call | solution.py:66
  89.8 2.4 collective-permute-done.30
  93.6 142.2 %conditional.1 = (bf16[512,768]{1,0:T(8,128)(2,1)}, f32[512,768]{1,0:T(8,128)}, f32[9,768]{1,0:T(8,128)}, bf16[3,768]{1,0:T(4,128)(2,1)S(1)}, f32[3,768,384]{2,1...) conditional(s32[]{:T(128)} %convert_element_type.52, () %tuple.37, ...), branch_computations={%region_3.4_spmd, %region_4.7_spmd} | conditional | flops 32006246400 | bytes 121152576 | solution.py:869
  94.8 2.8 %middle.2 = (f32[256,768]{1,0:T(8,128)S(1)}, bf16[256,768]{1,0:T(8,128)(2,1)S(1)}, f32[4,768]{1,0:T(4,128)S(1)}) custom-call(bf16[512,768]{1,0:T(8,128)(2,1)} %get-tuple-element.82.mine_ref, bf16[256,768]{1,0:T(8,128)(2,1)} %copy-done.35, f32[512,768]{1,0:T(8,128)} %get-tuple-element.84.attn_ref, bf16[512,768]{1,0:T(8,128)(2,1)S(1)} %get-tuple-element.85.x_ref, ...), custom_call_target="tpu_custom_call" | custom-call | flops 2000000000 | bytes 1000 | tf_op jit(solution)/shard_map/cond/branch_1_fun/middle/pallas_call | solution.py:66
  102.9 6.8 %collective-permute-done.other_1.g_3 = bf16[256,768]{1,0:T(8,128)(2,1)S(1)} collective-permute-done((bf16[256,768]{1,0:T(8,128)(2,1)S(1)}, bf16[256,768]{1,0:T(8,128)(2,1)S(1)}, u32[]{:S(2)}, u32[]{:S(2)}) %collective-permute-start) | collective-permute-done | bytes 393248 | tf_op jit(solution)/shard_map/cond/branch_1_fun/ppermute | solution.py:641
  109.7 3.9 %attention_back.1.grad_ref = bf16[3,3,1280,128]{3,2,1,0:T(8,128)(2,1)S(1)} custom-call(s32[69]{0:T(128)S(1)} %get-tuple-element.79.meta, bf16[3,3,1280,128]{3,2,1,0:T(8,128)(2,1)S(1)} %copy-done.48, bf16[256,768]{1,0:T(8,128)(2,1)S(1)} %copy-done.37, bf16[256,768]{1,0:T(8,128)(2,1)S(1)} %get-tuple-element.88.own_1.g_1, bf16[256,768]{1,0:T(8,128)(2,1)S(1)} %copy-done.39, ...), custom_call_target="tpu_custom_call" | custom-call | flops 8999999488 | bytes 1000 | tf_op jit(solution)/shard_map/cond/branch_1_fun/attention_back/pallas_call | solution.py:66
  113.6 7.0 %collective-permute-done.1 = bf16[512,768]{1,0:T(8,128)(2,1)S(1)} collective-permute-done((bf16[512,768]{1,0:T(8,128)(2,1)S(1)}, bf16[512,768]{1,0:T(8,128)(2,1)S(1)}, u32[]{:S(2)}, u32[]{:S(2)}) %collective-permute-start.1) | collective-permute-done | bytes 786464 | tf_op jit(solution)/shard_map/cond/branch_1_fun/ppermute | solution.py:641
  120.7 4.0 %weights.1 = (bf16[1536,384]{1,0:T(8,128)(2,1)S(1)}, bf16[1536,384]{1,0:T(8,128)(2,1)S(1)}, f32[3,384]{1,0:T(4,128)S(1)}) custom-call(s32[69]{0:T(128)S(1)} %get-tuple-element.79.meta, bf16[3,3,1280,128]{3,2,1,0:T(8,128)(2,1)S(1)} %attention_back.1.grad_ref, bf16[512,768]{1,0:T(8,128)(2,1)S(1)} %copy-done.46, bf16[512,768]{1,0:T(8,128)(2,1)S(1)} %copy-done.47, ...), custom_call_target="tpu_custom_call" | custom-call | flops 4000000000 | bytes 1000 | tf_op jit(solution)/shard_map/cond/branch_1_fun/weights/pallas_call | solution.py:66
  124.8 3.7 %share.1 = (bf16[512,768]{1,0:T(8,128)(2,1)S(1)}, bf16[512,768]{1,0:T(8,128)(2,1)S(1)}) custom-call(s32[69]{0:T(128)S(1)} %get-tuple-element.79.meta, bf16[3,3,1280,128]{3,2,1,0:T(8,128)(2,1)S(1)} %attention_back.1.grad_ref, bf16[3,768,384]{2,1,0:T(8,128)(2,1)S(1)} %copy-done.30), custom_call_target="tpu_custom_call" | custom-call | flops 3000000000 | bytes 1000 | tf_op jit(solution)/shard_map/cond/branch_1_fun/share/pallas_call | solution.py:66
  133.3 16.1 %collective-permute-done.3.got_ref = bf16[768,384]{1,0:T(8,128)(2,1)S(1)} collective-permute-done((bf16[768,384]{1,0:T(8,128)(2,1)S(1)}, bf16[768,384]{1,0:T(8,128)(2,1)S(1)}, u32[]{:S(2)}, u32[]{:S(2)}) %collective-permute-start.3) | collective-permute-done | bytes 589856 | tf_op jit(solution)/shard_map/cond/branch_1_fun/ppermute | solution.py:550
  152.6 8.2 %collective-permute-done.4.got_ref = bf16[384,384]{1,0:T(8,128)(2,1)S(1)} collective-permute-done((bf16[384,384]{1,0:T(8,128)(2,1)S(1)}, bf16[384,384]{1,0:T(8,128)(2,1)S(1)}, u32[]{:S(2)}, u32[]{:S(2)}) %collective-permute-start.4) | collective-permute-done | bytes 294944 | tf_op jit(solution)/shard_map/cond/branch_1_fun/ppermute | solution.py:550
  162.4 6.8 %collective-permute-start.5 = (bf16[192,384]{1,0:T(8,128)(2,1)S(1)}, bf16[192,384]{1,0:T(8,128)(2,1)S(1)}, u32[]{:S(2)}, u32[]{:S(2)}) collective-permute-start(bf16[192,384]{1,0:T(8,128)(2,1)S(1)} %get-tuple-element.121), channel_id=1, source_target_pairs={{0,16},{2,18},{4,20},{6,22},{8,24},{10,26},{12,28},{14,30},{16,0},... | collective-permute-start | bytes 442376 | tf_op jit(solution)/shard_map/cond/branch_1_fun/ppermute | solution.py:550
  169.2 2.6 %final.1 = (f32[512,768]{1,0:T(8,128)}, f32[3,768]{1,0:T(4,128)S(1)}) custom-call(bf16[512,768]{1,0:T(8,128)(2,1)S(1)} %copy-done.5, bf16[512,768]{1,0:T(8,128)(2,1)S(1)} %collective-permute-done.6.got_ref, bf16[512,768]{1,0:T(8,128)(2,1)S(1)} %copy-done.13, f32[256,768]{1,0:T(8,128)S(1)} %copy-done.45, f32[256,768]{1,0:T(8,128)S(1)} %get-tuple-element.127.hidden_1, ...), custom_call_target="tpu_custom_call" | custom-call | flops 3000000000 | bytes 1000 | tf_op jit(solution)/shard_map/cond/branch_1_fun/final/pallas_call | solution.py:66
  171.9 8.2 %collective-permute-done.5 = bf16[192,384]{1,0:T(8,128)(2,1)S(1)} collective-permute-done((bf16[192,384]{1,0:T(8,128)(2,1)S(1)}, bf16[192,384]{1,0:T(8,128)(2,1)S(1)}, u32[]{:S(2)}, u32[]{:S(2)}) %collective-permute-start.5) | collective-permute-done | bytes 147488 | tf_op jit(solution)/shard_map/cond/branch_1_fun/ppermute | solution.py:550
  180.2 2.9 %collective-permute-start.8 = (f32[12,768]{1,0:T(8,128)S(1)}, f32[12,768]{1,0:T(8,128)S(1)}, u32[]{:S(2)}, u32[]{:S(2)}) collective-permute-start(f32[12,768]{1,0:T(8,128)S(1)} %concatenate.7), channel_id=1, source_target_pairs={{0,16},{2,18},{4,20},{6,22},{8,24},{10,26},{12,28},{14,30},{16,0},... | collective-permute-start | bytes 110600 | tf_op jit(solution)/shard_map/cond/branch_1_fun/ppermute | solution.py:550
  183.1 10.4 %collective-permute-done.8 = f32[12,768]{1,0:T(8,128)S(1)} collective-permute-done((f32[12,768]{1,0:T(8,128)S(1)}, f32[12,768]{1,0:T(8,128)S(1)}, u32[]{:S(2)}, u32[]{:S(2)}) %collective-permute-start.8) | collective-permute-done | bytes 36896 | tf_op jit(solution)/shard_map/cond/branch_1_fun/ppermute | solution.py:550
  197.7 16.0 %collective-permute-done.12 = f32[12,768]{1,0:T(8,128)S(1)} collective-permute-done((f32[12,768]{1,0:T(8,128)S(1)}, f32[12,768]{1,0:T(8,128)S(1)}, u32[]{:S(2)}, u32[]{:S(2)}) %collective-permute-start.12) | collective-permute-done | bytes 36896 | tf_op jit(solution)/shard_map/cond/branch_1_fun/ppermute | solution.py:550
  216.3 8.0 %collective-permute-done.16 = f32[12,768]{1,0:T(8,128)S(1)} collective-permute-done((f32[12,768]{1,0:T(8,128)S(1)}, f32[12,768]{1,0:T(8,128)S(1)}, u32[]{:S(2)}, u32[]{:S(2)}) %collective-permute-start.16) | collective-permute-done | bytes 36896 | tf_op jit(solution)/shard_map/cond/branch_1_fun/ppermute | solution.py:550
  232.7 3.1 %unpack.1 = (f32[3,768,384]{2,1,0:T(8,128)}, f32[384,768]{1,0:T(8,128)}) custom-call(s32[69]{0:T(128)S(1)} %copy-done.27, bf16[384,384]{1,0:T(8,128)(2,1)S(1)} %gather.2.refs_0_, bf16[384,384]{1,0:T(8,128)(2,1)S(1)} %collective-permute-done.11.refs_1_, bf16[384,384]{1,0:T(8,128)(2,1)S(1)} %collective-permute-done.10.refs_2_, ...), custom_call_target="tpu_custom_call" | custom-call | flops 3000000000 | bytes 1000 | tf_op jit(solution)/shard_map/cond/branch_1_fun/unpack/pallas_call | solution.py:66
  235.9 4.6 %convert_element_type.56 = f32[768,1536]{1,0:T(8,128)} convert(bf16[768,1536]{1,0:T(8,128)(2,1)} %get-tuple-element.339) | non-fusion elementwise | flops 1179648 | bytes 7077888 | tf_op jit(solution)/shard_map/convert_element_type | solution.py:888
  240.6 2.5 %convert_element_type.57 = f32[1536,768]{1,0:T(8,128)} convert(bf16[1536,768]{1,0:T(8,128)(2,1)S(1)} %copy-done.7) | non-fusion elementwise | flops 1179648 | bytes 7077888 | tf_op jit(solution)/shard_map/convert_element_type | solution.py:890
  (202 shorter events, 49.7 us)
Async XLA Ops:
  7.2 228.7 %all-reduce.3.cloned.1.call-start = ((), (), s32[]{:S(2)}) async-start(), calls=%async_computation | async-start | bytes 9437184 | tf_op jit(solution)/shard_map/psum | solution.py:759
  7.2 17.5 %collective-permute-start.21 = (s32[512]{0:T(512)}, s32[512]{0:T(512)S(1)}, u32[]{:S(2)}, u32[]{:S(2)}) collective-permute-start(s32[512]{0:T(512)} %param.23), channel_id=1, source_target_pairs={{0,1},{1,0},{2,3},{3,2},{4,5},{5,4},{6,7},{7,6},{8,9},{9,8},{10,11... | collective-permute-start | bytes 6152 | tf_op jit(solution)/shard_map/ppermute | solution.py:641
  10.3 20.7 %collective-permute-start.20 = (bf16[512,768]{1,0:T(8,128)(2,1)}, bf16[512,768]{1,0:T(8,128)(2,1)S(1)}, u32[]{:S(2)}, u32[]{:S(2)}) collective-permute-start(bf16[512,768]{1,0:T(8,128)(2,1)} %tokens_ref.1), channel_id=1, source_target_pairs={{0,1},{1,0},{2,3},{3,2},{4,5},{5,4},{6,7},{7,6},{8,9},{9,8},{10,11... | collective-permute-start | bytes 2359304 | tf_op jit(solution)/shard_map/ppermute | solution.py:641
  19.4 19.2 %collective-permute-start.22 = (bf16[192,384]{1,0:T(8,128)(2,1)S(1)}, bf16[192,384]{1,0:T(8,128)(2,1)S(1)}, u32[]{:S(2)}, u32[]{:S(2)}) collective-permute-start(bf16[192,384]{1,0:T(8,128)(2,1)S(1)} %dynamic_slice.3), channel_id=1, source_target_pairs={{0,1},{1,0},{2,3},{3,2},{4,5},{5,4},{6,7},{7,6},{8,9},{9,8},{10,11... | collective-permute-start | bytes 442376 | tf_op jit(solution)/shard_map/ppermute | solution.py:610
  30.9 18.5 %collective-permute-start.23 = (bf16[512,768]{1,0:T(8,128)(2,1)}, bf16[512,768]{1,0:T(8,128)(2,1)S(1)}, u32[]{:S(2)}, u32[]{:S(2)}) collective-permute-start(bf16[512,768]{1,0:T(8,128)(2,1)} %get-tuple-element.234.gb_ref.g_own), channel_id=1, source_target_pairs={{0,1},{1,0},{2,3},{3,2},{4,5},{5,4},{6,7},{7,6},{8,9},{9,8},{10,11... | collective-permute-start | bytes 2359304 | tf_op jit(solution)/shard_map/ppermute | solution.py:641
  38.6 5.2 %collective-permute-start.24 = (bf16[192,384]{1,0:T(8,128)(2,1)S(1)}, bf16[192,384]{1,0:T(8,128)(2,1)S(1)}, u32[]{:S(2)}, u32[]{:S(2)}) collective-permute-start(bf16[192,384]{1,0:T(8,128)(2,1)S(1)} %collective-permute-done.22.refs_0_), channel_id=1, source_target_pairs={{0,4},{2,6},{4,0},{6,2},{8,12},{10,14},{12,8},{14,10},{16,20},{18,... | collective-permute-start | bytes 442376 | tf_op jit(solution)/shard_map/ppermute | solution.py:550
  49.5 12.1 %collective-permute-start.27 = (bf16[512,384]{1,0:T(8,128)(2,1)S(1)}, bf16[512,384]{1,0:T(8,128)(2,1)S(1)}, u32[]{:S(2)}, u32[]{:S(2)}) collective-permute-start(bf16[512,384]{1,0:T(8,128)(2,1)S(1)} %get-tuple-element.236.mine_ref), channel_id=1, source_target_pairs={{0,1},{1,0},{2,3},{3,2},{4,5},{5,4},{6,7},{7,6},{8,9},{9,8},{10,11... | collective-permute-start | bytes 1179656 | tf_op jit(solution)/shard_map/ppermute | solution.py:641
  50.5 1.8 collective-permute-start.26
  50.5 19.8 %collective-permute-start.25 = (bf16[512,384]{1,0:T(8,128)(2,1)S(1)}, bf16[512,384]{1,0:T(8,128)(2,1)S(1)}, u32[]{:S(2)}, u32[]{:S(2)}) collective-permute-start(bf16[512,384]{1,0:T(8,128)(2,1)S(1)} %get-tuple-element.237.mine_ref), channel_id=1, source_target_pairs={{0,1},{1,0},{2,3},{3,2},{4,5},{5,4},{6,7},{7,6},{8,9},{9,8},{10,11... | collective-permute-start | bytes 1179656 | tf_op jit(solution)/shard_map/ppermute | solution.py:641
  68.2 12.1 %collective-permute-start.29 = (bf16[256,768]{1,0:T(8,128)(2,1)S(1)}, bf16[256,768]{1,0:T(8,128)(2,1)S(1)}, u32[]{:S(2)}, u32[]{:S(2)}) collective-permute-start(bf16[256,768]{1,0:T(8,128)(2,1)S(1)} %get-tuple-element.381), channel_id=1, source_target_pairs={{0,1},{1,0},{2,3},{3,2},{4,5},{5,4},{6,7},{7,6},{8,9},{9,8},{10,11... | collective-permute-start | bytes 1179656 | tf_op jit(solution)/shard_map/ppermute | solution.py:641
  68.6 21.2 %collective-permute-start.28 = (bf16[256,768]{1,0:T(8,128)(2,1)S(1)}, bf16[256,768]{1,0:T(8,128)(2,1)S(1)}, u32[]{:S(2)}, u32[]{:S(2)}) collective-permute-start(bf16[256,768]{1,0:T(8,128)(2,1)S(1)} %get-tuple-element.382), channel_id=1, source_target_pairs={{0,1},{1,0},{2,3},{3,2},{4,5},{5,4},{6,7},{7,6},{8,9},{9,8},{10,11... | collective-permute-start | bytes 1179656 | tf_op jit(solution)/shard_map/ppermute | solution.py:641
  82.0 10.1 %collective-permute-start.30 = (bf16[256,768]{1,0:T(8,128)(2,1)S(1)}, bf16[256,768]{1,0:T(8,128)(2,1)S(1)}, u32[]{:S(2)}, u32[]{:S(2)}) collective-permute-start(bf16[256,768]{1,0:T(8,128)(2,1)S(1)} %get-tuple-element.257), channel_id=1, source_target_pairs={{0,1},{1,0},{2,3},{3,2},{4,5},{5,4},{6,7},{7,6},{8,9},{9,8},{10,11... | collective-permute-start | bytes 1179656 | tf_op jit(solution)/shard_map/ppermute | solution.py:641
  97.6 12.1 %collective-permute-start = (bf16[256,768]{1,0:T(8,128)(2,1)S(1)}, bf16[256,768]{1,0:T(8,128)(2,1)S(1)}, u32[]{:S(2)}, u32[]{:S(2)}) collective-permute-start(bf16[256,768]{1,0:T(8,128)(2,1)S(1)} %get-tuple-element.88.own_1.g_1), channel_id=1, source_target_pairs={{0,1},{1,0},{2,3},{3,2},{4,5},{5,4},{6,7},{7,6},{8,9},{9,8},{10,11... | collective-permute-start | bytes 1179656 | tf_op jit(solution)/shard_map/cond/branch_1_fun/ppermute | solution.py:641
  99.9 20.7 %collective-permute-start.1 = (bf16[512,768]{1,0:T(8,128)(2,1)S(1)}, bf16[512,768]{1,0:T(8,128)(2,1)S(1)}, u32[]{:S(2)}, u32[]{:S(2)}) collective-permute-start(bf16[512,768]{1,0:T(8,128)(2,1)S(1)} %branch.3), channel_id=1, source_target_pairs={{0,1},{1,0},{2,3},{3,2},{4,5},{5,4},{6,7},{7,6},{8,9},{9,8},{10,11... | collective-permute-start | bytes 2359304 | tf_op jit(solution)/shard_map/cond/branch_1_fun/ppermute | solution.py:641
  124.7 3.8 %collective-permute-start.2 = (bf16[1536,384]{1,0:T(8,128)(2,1)S(1)}, bf16[1536,384]{1,0:T(8,128)(2,1)S(1)}, u32[]{:S(2)}, u32[]{:S(2)}) collective-permute-start(bf16[1536,384]{1,0:T(8,128)(2,1)S(1)} %get-tuple-element.103), channel_id=1, source_target_pairs={{0,2},{2,0},{4,6},{6,4},{8,10},{10,8},{12,14},{14,12},{16,18},{18,... | collective-permute-start | bytes 3538952 | tf_op jit(solution)/shard_map/cond/branch_1_fun/ppermute | solution.py:550
  129.4 20.0 %collective-permute-start.3 = (bf16[768,384]{1,0:T(8,128)(2,1)S(1)}, bf16[768,384]{1,0:T(8,128)(2,1)S(1)}, u32[]{:S(2)}, u32[]{:S(2)}) collective-permute-start(bf16[768,384]{1,0:T(8,128)(2,1)S(1)} %get-tuple-element.108), channel_id=1, source_target_pairs={{0,4},{2,6},{4,0},{6,2},{8,12},{10,14},{12,8},{14,10},{16,20},{18,... | collective-permute-start | bytes 1769480 | tf_op jit(solution)/shard_map/cond/branch_1_fun/ppermute | solution.py:550
  131.1 38.1 %collective-permute-start.6 = (bf16[512,768]{1,0:T(8,128)(2,1)S(1)}, bf16[512,768]{1,0:T(8,128)(2,1)S(1)}, u32[]{:S(2)}, u32[]{:S(2)}) collective-permute-start(bf16[512,768]{1,0:T(8,128)(2,1)S(1)} %get-tuple-element.124), channel_id=1, source_target_pairs={{0,1},{1,0},{2,3},{3,2},{4,5},{5,4},{6,7},{7,6},{8,9},{9,8},{10,11... | collective-permute-start | bytes 2359304 | tf_op jit(solution)/shard_map/cond/branch_1_fun/ppermute | solution.py:641
  150.8 10.0 %collective-permute-start.4 = (bf16[384,384]{1,0:T(8,128)(2,1)S(1)}, bf16[384,384]{1,0:T(8,128)(2,1)S(1)}, u32[]{:S(2)}, u32[]{:S(2)}) collective-permute-start(bf16[384,384]{1,0:T(8,128)(2,1)S(1)} %get-tuple-element.120), channel_id=1, source_target_pairs={{0,8},{2,10},{4,12},{6,14},{8,0},{10,2},{12,4},{14,6},{16,24},{18,... | collective-permute-start | bytes 884744 | tf_op jit(solution)/shard_map/cond/branch_1_fun/ppermute | solution.py:550
  162.4 17.7 %collective-permute-start.5 = (bf16[192,384]{1,0:T(8,128)(2,1)S(1)}, bf16[192,384]{1,0:T(8,128)(2,1)S(1)}, u32[]{:S(2)}, u32[]{:S(2)}) collective-permute-start(bf16[192,384]{1,0:T(8,128)(2,1)S(1)} %get-tuple-element.121), channel_id=1, source_target_pairs={{0,16},{2,18},{4,20},{6,22},{8,24},{10,26},{12,28},{14,30},{16,0},... | collective-permute-start | bytes 442376 | tf_op jit(solution)/shard_map/cond/branch_1_fun/ppermute | solution.py:550
  180.2 13.4 %collective-permute-start.7 = (bf16[192,384]{1,0:T(8,128)(2,1)S(1)}, bf16[192,384]{1,0:T(8,128)(2,1)S(1)}, u32[]{:S(2)}, u32[]{:S(2)}) collective-permute-start(bf16[192,384]{1,0:T(8,128)(2,1)S(1)} %add_convert_fusion.refs_0_), channel_id=1, source_target_pairs={{0,16},{2,18},{4,20},{6,22},{8,24},{10,26},{12,28},{14,30},{16,0},... | collective-permute-start | bytes 442376 | tf_op jit(solution)/shard_map/cond/branch_1_fun/ppermute | solution.py:550
  180.2 13.3 %collective-permute-start.8 = (f32[12,768]{1,0:T(8,128)S(1)}, f32[12,768]{1,0:T(8,128)S(1)}, u32[]{:S(2)}, u32[]{:S(2)}) collective-permute-start(f32[12,768]{1,0:T(8,128)S(1)} %concatenate.7), channel_id=1, source_target_pairs={{0,16},{2,18},{4,20},{6,22},{8,24},{10,26},{12,28},{14,30},{16,0},... | collective-permute-start | bytes 110600 | tf_op jit(solution)/shard_map/cond/branch_1_fun/ppermute | solution.py:550
  194.1 19.6 %collective-permute-start.11 = (bf16[384,384]{1,0:T(8,128)(2,1)S(1)}, bf16[384,384]{1,0:T(8,128)(2,1)S(1)}, u32[]{:S(2)}, u32[]{:S(2)}) collective-permute-start(bf16[384,384]{1,0:T(8,128)(2,1)S(1)} %gather.2.refs_0_), channel_id=1, source_target_pairs={{0,2},{2,0},{4,6},{6,4},{8,10},{10,8},{12,14},{14,12},{16,18},{18,... | collective-permute-start | bytes 884744 | tf_op jit(solution)/shard_map/cond/branch_1_fun/ppermute | solution.py:550
  194.2 19.5 %collective-permute-start.10 = (bf16[384,384]{1,0:T(8,128)(2,1)S(1)}, bf16[384,384]{1,0:T(8,128)(2,1)S(1)}, u32[]{:S(2)}, u32[]{:S(2)}) collective-permute-start(bf16[384,384]{1,0:T(8,128)(2,1)S(1)} %gather.2.refs_0_), channel_id=1, source_target_pairs={{0,4},{2,6},{4,0},{6,2},{8,12},{10,14},{12,8},{14,10},{16,20},{18,... | collective-permute-start | bytes 884744 | tf_op jit(solution)/shard_map/cond/branch_1_fun/ppermute | solution.py:550
  195.7 18.0 %collective-permute-start.9 = (bf16[384,384]{1,0:T(8,128)(2,1)S(1)}, bf16[384,384]{1,0:T(8,128)(2,1)S(1)}, u32[]{:S(2)}, u32[]{:S(2)}) collective-permute-start(bf16[384,384]{1,0:T(8,128)(2,1)S(1)} %gather.2.refs_0_), channel_id=1, source_target_pairs={{0,8},{2,10},{4,12},{6,14},{8,0},{10,2},{12,4},{14,6},{16,24},{18,... | collective-permute-start | bytes 884744 | tf_op jit(solution)/shard_map/cond/branch_1_fun/ppermute | solution.py:550
  195.7 18.0 %collective-permute-start.12 = (f32[12,768]{1,0:T(8,128)S(1)}, f32[12,768]{1,0:T(8,128)S(1)}, u32[]{:S(2)}, u32[]{:S(2)}) collective-permute-start(f32[12,768]{1,0:T(8,128)S(1)} %add.66), channel_id=1, source_target_pairs={{0,8},{2,10},{4,12},{6,14},{8,0},{10,2},{12,4},{14,6},{16,24},{18,... | collective-permute-start | bytes 110600 | tf_op jit(solution)/shard_map/cond/branch_1_fun/ppermute | solution.py:550
  213.7 10.6 %collective-permute-start.15 = (bf16[384,384]{1,0:T(8,128)(2,1)S(1)}, bf16[384,384]{1,0:T(8,128)(2,1)S(1)}, u32[]{:S(2)}, u32[]{:S(2)}) collective-permute-start(bf16[384,384]{1,0:T(8,128)(2,1)S(1)} %collective-permute-done.10.refs_2_), channel_id=1, source_target_pairs={{0,2},{2,0},{4,6},{6,4},{8,10},{10,8},{12,14},{14,12},{16,18},{18,... | collective-permute-start | bytes 884744 | tf_op jit(solution)/shard_map/cond/branch_1_fun/ppermute | solution.py:550
  213.8 10.6 %collective-permute-start.14 = (bf16[384,384]{1,0:T(8,128)(2,1)S(1)}, bf16[384,384]{1,0:T(8,128)(2,1)S(1)}, u32[]{:S(2)}, u32[]{:S(2)}) collective-permute-start(bf16[384,384]{1,0:T(8,128)(2,1)S(1)} %collective-permute-done.9.refs_4_), channel_id=1, source_target_pairs={{0,2},{2,0},{4,6},{6,4},{8,10},{10,8},{12,14},{14,12},{16,18},{18,... | collective-permute-start | bytes 884744 | tf_op jit(solution)/shard_map/cond/branch_1_fun/ppermute | solution.py:550
  214.3 10.1 %collective-permute-start.13 = (bf16[384,384]{1,0:T(8,128)(2,1)S(1)}, bf16[384,384]{1,0:T(8,128)(2,1)S(1)}, u32[]{:S(2)}, u32[]{:S(2)}) collective-permute-start(bf16[384,384]{1,0:T(8,128)(2,1)S(1)} %collective-permute-done.9.refs_4_), channel_id=1, source_target_pairs={{0,4},{2,6},{4,0},{6,2},{8,12},{10,14},{12,8},{14,10},{16,20},{18,... | collective-permute-start | bytes 884744 | tf_op jit(solution)/shard_map/cond/branch_1_fun/ppermute | solution.py:550
  214.9 9.5 %collective-permute-start.16 = (f32[12,768]{1,0:T(8,128)S(1)}, f32[12,768]{1,0:T(8,128)S(1)}, u32[]{:S(2)}, u32[]{:S(2)}) collective-permute-start(f32[12,768]{1,0:T(8,128)S(1)} %add.67), channel_id=1, source_target_pairs={{0,4},{2,6},{4,0},{6,2},{8,12},{10,14},{12,8},{14,10},{16,20},{18,... | collective-permute-start | bytes 110600 | tf_op jit(solution)/shard_map/cond/branch_1_fun/ppermute | solution.py:550
  224.4 1.3 collective-permute-start.17
  224.4 8.3 %collective-permute-start.19 = (bf16[384,384]{1,0:T(8,128)(2,1)S(1)}, bf16[384,384]{1,0:T(8,128)(2,1)S(1)}, u32[]{:S(2)}, u32[]{:S(2)}) collective-permute-start(bf16[384,384]{1,0:T(8,128)(2,1)S(1)} %collective-permute-done.13.refs_6_), channel_id=1, source_target_pairs={{0,2},{2,0},{4,6},{6,4},{8,10},{10,8},{12,14},{14,12},{16,18},{18,... | collective-permute-start | bytes 884744 | tf_op jit(solution)/shard_map/cond/branch_1_fun/ppermute | solution.py:550
  225.7 4.2 %collective-permute-start.18 = (f32[9,768]{1,0:T(8,128)S(1)}, f32[9,768]{1,0:T(8,128)S(1)}, u32[]{:S(2)}, u32[]{:S(2)}) collective-permute-start(f32[9,768]{1,0:T(8,128)S(1)} %bitcast.8), channel_id=1, source_target_pairs={{0,1},{1,0},{2,3},{3,2},{4,5},{5,4},{6,7},{7,6},{8,9},{9,8},{10,11... | collective-permute-start | bytes 82952 | tf_op jit(solution)/shard_map/cond/branch_1_fun/ppermute | solution.py:641
  (49 other events, 398.3 us)
Sparse Core Ops, SparseCore 0:
  93.1 136.2 all-reduce.2
